TPU v7x, 32 devices: a whole 2x2x4 slice. The times are simulated.
32 devices in a mesh: dp: 8 (over z, x), expert: 4 (over y, core).
Axes of the slice: x: 2, y: 2, z: 4, core: 2. Of those that a mesh axis runs over, the one named last changes fastest.
Arguments:
- tokens: bfloat16 [4, 1024, 2048], P('expert', 'dp'), may hold values from -6 to 6
- cotangent: bfloat16 [4, 1024, 2048], P('expert', 'dp'), may hold values from -6 to 6
- lengths: int32 [4], replicated, may hold values from 256 to 1024, as said below
- routes: int32 [4, 1024, 4], P('expert', 'dp'), may hold values from 0 to 7, all different within a row; in each aligned block of 128 rows (0 to 127, 128 to 255, ..., all dimensions but the last counted through in order) at most 80 rows name the same one
- query_weight: bfloat16 [2048, 2048], P(('dp', 'expert')), may hold values from -0.1875 to 0.1875
- key_weight: bfloat16 [2048, 2048], P(('dp', 'expert')), may hold values from -0.1875 to 0.1875
- value_weight: bfloat16 [2048, 2048], P(('dp', 'expert')), may hold values from -0.125 to 0.125
- output_weight: bfloat16 [2048, 2048], P(('dp', 'expert')), may hold values from -0.75 to 0.75
- query_bias: bfloat16 [2048], P(('dp', 'expert')), may hold values from -1.1953125 to 1.1953125
- key_bias: bfloat16 [2048], P(('dp', 'expert')), may hold values from -1.1953125 to 1.1953125
- value_bias: bfloat16 [2048], P(('dp', 'expert')), may hold values from -1.1953125 to 1.1953125
- attention_gain: bfloat16 [2048], P(('dp', 'expert')), may hold values from 0.5 to 1.5
- router_weight: bfloat16 [2048, 8], P(('dp', 'expert')), may hold values from -0.0625 to 0.0625
- shared_switch: bfloat16 [2048], P(('dp', 'expert')), may hold values from -0.125 to 0.125
- mixer_gain: bfloat16 [2048], P(('dp', 'expert')), may hold values from 0.5 to 1.5
- shared_gate_weight: bfloat16 [2048, 5632], P(('dp', 'expert')), may hold values from -0.125 to 0.125
- shared_up_weight: bfloat16 [2048, 5632], P(('dp', 'expert')), may hold values from -0.125 to 0.125
- shared_down_weight: bfloat16 [2048, 5632], P(('dp', 'expert')), may hold values from -0.15625 to 0.15625
- expert_gate: bfloat16 [8, 2048, 1408], P('expert', 'dp'), may hold values from -0.125 to 0.125
- expert_up: bfloat16 [8, 2048, 1408], P('expert', 'dp'), may hold values from -0.125 to 0.125
- expert_down: bfloat16 [8, 2048, 1408], P('expert', 'dp'), may hold values from -0.625 to 0.625
Outputs:
- layer_out: bfloat16 [4, 1024, 2048], P('expert', 'dp')
- balance_loss: float32 [1], replicated
- grad_tokens: bfloat16 [4, 1024, 2048], P('expert', 'dp')
- grad_query_weight: float32 [2048, 2048], P(('dp', 'expert'))
- grad_key_weight: float32 [2048, 2048], P(('dp', 'expert'))
- grad_value_weight: float32 [2048, 2048], P(('dp', 'expert'))
- grad_output_weight: float32 [2048, 2048], P(('dp', 'expert'))
- grad_query_bias: float32 [2048], P(('dp', 'expert'))
- grad_key_bias: float32 [2048], P(('dp', 'expert'))
- grad_value_bias: float32 [2048], P(('dp', 'expert'))
- grad_attention_gain: float32 [2048], P(('dp', 'expert'))
- grad_router_weight: float32 [2048, 8], P(('dp', 'expert'))
- grad_shared_switch: float32 [2048], P(('dp', 'expert'))
- grad_mixer_gain: float32 [2048], P(('dp', 'expert'))
- grad_shared_gate_weight: float32 [2048, 5632], P(('dp', 'expert'))
- grad_shared_up_weight: float32 [2048, 5632], P(('dp', 'expert'))
- grad_shared_down_weight: float32 [2048, 5632], P(('dp', 'expert'))
- grad_expert_gate: float32 [8, 2048, 1408], P('expert', 'dp')
- grad_expert_up: float32 [8, 2048, 1408], P('expert', 'dp')
- grad_expert_down: float32 [8, 2048, 1408], P('expert', 'dp')
Inputs may be any that keep to these rules, and one draw needn't show every extreme that they name: Sequence s has lengths[s] valid slots at its start, the rest is padding; one sequence is full at 1024. The 4 experts of a slot differ. In the rows of one device (aligned blocks of 128 slots) no expert is named more than 80 times, and in some block one is named exactly 80 times. Padding slots carry routes too; they are not used.
All inputs are finite; a program needn't handle non-finite values.
Results may differ from a plain program's by a relative error of at most 0.023.
Values may be sent and summed in bfloat16 or wider, within the bound.
No kernel may reach another device: no remote copies, remote signals or barrier semaphores. Data moves between devices by JAX's collectives and lax.ppermute only.
A program may use at most 640 MiB of HBM per device.

v0:
```python
import math

import jax
import jax.numpy as jnp
from jax import lax
from jax.sharding import PartitionSpec as P

HEADS = 16
HD = 128


epsilon = 1e-06
rope_base = 1000000.0
highest = lax.Precision.HIGHEST
neg_large = -1e30


def transpose_times(left, right):
    return lax.dot_general(
        left, right, (((0,), (0,)), ((), ())), preferred_element_type=jnp.float32
    )


def times_transpose(left, right):
    return lax.dot_general(
        left, right, (((1,), (1,)), ((), ())), preferred_element_type=jnp.float32
    )


def rope_tables(positions, head_width):
    halfway = head_width // 2
    freqs = rope_base ** (-jnp.arange(halfway, dtype=jnp.float32) * 2.0 / head_width)
    angles = positions.astype(jnp.float32)[:, None] * freqs[None, :]
    angles = jnp.concatenate([angles, angles], axis=1)
    return (jnp.cos(angles), jnp.sin(angles))


def rotate(values, cosine, sine):
    halfway = values.shape[-1] // 2
    turned = jnp.concatenate([-values[..., halfway:], values[..., :halfway]], axis=-1)
    return values * cosine[:, None, :] + turned * sine[:, None, :]


def rotate_back(grads_in, cosine, sine):
    halfway = grads_in.shape[-1] // 2
    scaled = grads_in * sine[:, None, :]
    turned = jnp.concatenate([scaled[..., halfway:], -scaled[..., :halfway]], axis=-1)
    return grads_in * cosine[:, None, :] + turned


def swiglu_back(grad_hidden, gate_pre, up_pre):
    sigma = jax.nn.sigmoid(gate_pre)
    grad_gate = grad_hidden * up_pre * sigma * (1.0 + gate_pre * (1.0 - sigma))
    grad_up = grad_hidden * (gate_pre * sigma)
    return (grad_gate, grad_up)


def norm_back(grad_normed, rows_in, inverse, gain):
    weighted = grad_normed * gain
    inner = jnp.sum(weighted * rows_in, axis=-1, keepdims=True)
    grad_rows = inverse * weighted - rows_in * inverse**3 * inner / rows_in.shape[-1]
    grad_gain = jnp.sum(grad_normed * rows_in * inverse, axis=0)
    return (grad_rows, grad_gain)


def masked_scores(queries, keys_all, query_pos, length, first_key, block_rows, scale):
    keys_blk = lax.dynamic_slice_in_dim(keys_all, first_key, block_rows, 0)
    scores = (
        jnp.einsum("qhd,khd->hqk", queries, keys_blk, preferred_element_type=jnp.float32) * scale
    )
    key_pos = first_key + jnp.arange(block_rows)
    allowed = (key_pos[None, :] <= query_pos[:, None]) & (key_pos[None, :] < length)
    return (jnp.where(allowed[None], scores, neg_large), keys_blk)


def softmax_totals(queries, keys_all, query_pos, length, block_rows, scale):
    block_count = keys_all.shape[0] // block_rows
    shape_rows = (queries.shape[1], queries.shape[0])

    def softmax_step(block_index, running):
        top_now, total_now = running
        scores, keys_blk = masked_scores(
            queries, keys_all, query_pos, length, block_index * block_rows, block_rows, scale
        )
        top_new = jnp.maximum(top_now, jnp.max(scores, axis=-1))
        total_new = total_now * jnp.exp(top_now - top_new) + jnp.sum(
            jnp.exp(scores - top_new[..., None]), axis=-1
        )
        return (top_new, total_new)

    initial = (jnp.full(shape_rows, neg_large, jnp.float32), jnp.zeros(shape_rows, jnp.float32))
    top_end, total_end = lax.fori_loop(0, block_count, softmax_step, initial)
    return top_end + jnp.log(total_end)


def attend(queries, keys_all, values_all, query_pos, length, block_rows, scale, log_totals):
    block_count = keys_all.shape[0] // block_rows

    def attend_step(block_index, accum):
        main_acc, rest_acc = accum
        first_key = block_index * block_rows
        scores, keys_blk = masked_scores(
            queries, keys_all, query_pos, length, first_key, block_rows, scale
        )
        attn_weights = jnp.exp(scores - log_totals[..., None])
        weights_low = attn_weights.astype(jnp.bfloat16)
        weights_rest = (attn_weights - weights_low.astype(jnp.float32)).astype(jnp.bfloat16)
        values_blk = lax.dynamic_slice_in_dim(values_all, first_key, block_rows, 0)
        main_acc = main_acc + jnp.einsum(
            "hqk,khd->qhd", weights_low, values_blk, preferred_element_type=jnp.float32
        )
        rest_acc = rest_acc + jnp.einsum(
            "hqk,khd->qhd", weights_rest, values_blk, preferred_element_type=jnp.float32
        )
        return (main_acc, rest_acc)

    initial = (jnp.zeros(queries.shape, jnp.float32), jnp.zeros(queries.shape, jnp.float32))
    return lax.fori_loop(0, block_count, attend_step, initial)


def weights_and_grads(
    queries,
    keys_all,
    values_all,
    grad_mixed,
    query_pos,
    length,
    block_rows,
    scale,
    log_totals,
    block_index,
):
    first_key = block_index * block_rows
    scores, keys_blk = masked_scores(
        queries, keys_all, query_pos, length, first_key, block_rows, scale
    )
    attn_weights = jnp.exp(scores - log_totals[..., None])
    values_blk = lax.dynamic_slice_in_dim(values_all, first_key, block_rows, 0)
    grad_attn = jnp.einsum(
        "qhd,khd->hqk", grad_mixed, values_blk, preferred_element_type=jnp.float32
    )
    return (attn_weights, grad_attn, keys_blk, first_key)


def attention_back(
    queries,
    keys_all,
    values_all,
    grad_mixed,
    query_pos,
    length,
    block_rows,
    scale,
    log_totals,
    delta,
):
    block_count = keys_all.shape[0] // block_rows

    def second_pass(running, block_index):
        attn_weights, grad_attn, keys_blk, first_key = weights_and_grads(
            queries,
            keys_all,
            values_all,
            grad_mixed,
            query_pos,
            length,
            block_rows,
            scale,
            log_totals,
            block_index,
        )
        grad_scores = (attn_weights * (grad_attn - delta[..., None])).astype(jnp.bfloat16)
        query_part = (
            jnp.einsum("hqk,khd->qhd", grad_scores, keys_blk, preferred_element_type=jnp.float32)
            * scale
        )
        keys_part = (
            jnp.einsum("hqk,qhd->khd", grad_scores, queries, preferred_element_type=jnp.float32)
            * scale
        )
        values_part = jnp.einsum(
            "hqk,qhd->khd",
            attn_weights.astype(jnp.bfloat16),
            grad_mixed,
            preferred_element_type=jnp.float32,
        )
        return (running + query_part, (keys_part, values_part))

    grad_queries, parts = lax.scan(
        second_pass, jnp.zeros(queries.shape, jnp.float32), jnp.arange(block_count)
    )
    return (grad_queries, parts[0].reshape(keys_all.shape), parts[1].reshape(values_all.shape))


def per_device(
    tokens,
    cotangent,
    lengths,
    routes,
    query_weight,
    key_weight,
    value_weight,
    output_weight,
    query_bias,
    key_bias,
    value_bias,
    attention_gain,
    router_weight,
    shared_switch,
    mixer_gain,
    shared_gate_weight,
    shared_up_weight,
    shared_down_weight,
    expert_gate,
    expert_up,
    expert_down,
):
    tok_rows = tokens.shape[1]
    width = tokens.shape[2]
    top_count = routes.shape[2]
    groups = lax.axis_size("expert")
    local_experts = expert_gate.shape[0]
    num_experts = local_experts * groups
    capacity = tok_rows * top_count * 5 // (num_experts * 4)
    scale = HD ** (-0.5)
    all_slots = float(groups * tok_rows * lax.axis_size("dp"))
    token_rows = tokens.reshape(tok_rows, width).astype(jnp.float32)
    length = jnp.take(lengths, lax.axis_index("expert"))
    positions = lax.axis_index("dp") * tok_rows + jnp.arange(tok_rows)
    valid = positions < length
    live = valid.astype(jnp.float32)[:, None]
    grad_final = cotangent.reshape(tok_rows, width).astype(jnp.float32) * live
    (
        query_full,
        key_full,
        value_full,
        output_full,
        query_bias_full,
        key_bias_full,
        value_bias_full,
        attn_gain_full,
        router_full,
        switch_full,
        mixer_gain_full,
        shared_gate_full,
        shared_up_full,
        shared_down_full,
    ) = (
        lax.all_gather(query_weight, ("dp", "expert"), axis=0, tiled=True),
        lax.all_gather(key_weight, ("dp", "expert"), axis=0, tiled=True),
        lax.all_gather(value_weight, ("dp", "expert"), axis=0, tiled=True),
        lax.all_gather(output_weight, ("dp", "expert"), axis=0, tiled=True),
        lax.all_gather(query_bias, ("dp", "expert"), axis=0, tiled=True),
        lax.all_gather(key_bias, ("dp", "expert"), axis=0, tiled=True),
        lax.all_gather(value_bias, ("dp", "expert"), axis=0, tiled=True),
        lax.all_gather(attention_gain, ("dp", "expert"), axis=0, tiled=True),
        lax.all_gather(router_weight, ("dp", "expert"), axis=0, tiled=True),
        lax.all_gather(shared_switch, ("dp", "expert"), axis=0, tiled=True),
        lax.all_gather(mixer_gain, ("dp", "expert"), axis=0, tiled=True),
        lax.all_gather(shared_gate_weight, ("dp", "expert"), axis=0, tiled=True),
        lax.all_gather(shared_up_weight, ("dp", "expert"), axis=0, tiled=True),
        lax.all_gather(shared_down_weight, ("dp", "expert"), axis=0, tiled=True),
    )
    attn_gain_f = attn_gain_full.astype(jnp.float32)
    mixer_gain_f = mixer_gain_full.astype(jnp.float32)
    attn_inv = lax.rsqrt(jnp.mean(token_rows * token_rows, axis=-1, keepdims=True) + epsilon)
    normed_attn = (token_rows * attn_inv * attn_gain_f).astype(jnp.bfloat16)
    query_pre = jnp.dot(
        normed_attn, query_full, preferred_element_type=jnp.float32
    ) + query_bias_full.astype(jnp.float32)
    key_pre = jnp.dot(
        normed_attn, key_full, preferred_element_type=jnp.float32
    ) + key_bias_full.astype(jnp.float32)
    value_pre = jnp.dot(
        normed_attn, value_full, preferred_element_type=jnp.float32
    ) + value_bias_full.astype(jnp.float32)
    cosine, sine = rope_tables(positions, HD)
    queries = rotate(query_pre.reshape(tok_rows, HEADS, HD), cosine, sine).astype(jnp.bfloat16)
    keys_own = rotate(key_pre.reshape(tok_rows, HEADS, HD), cosine, sine).astype(jnp.bfloat16)
    values_own = value_pre.reshape(tok_rows, HEADS, HD).astype(jnp.bfloat16)
    keys_all, values_all = (
        lax.all_gather(keys_own, "dp", axis=0, tiled=True),
        lax.all_gather(values_own, "dp", axis=0, tiled=True),
    )
    block_rows = math.gcd(keys_all.shape[0], 1024)
    log_totals = softmax_totals(queries, keys_all, positions, length, block_rows, scale)
    mixed, mixed_rest = attend(
        queries, keys_all, values_all, positions, length, block_rows, scale, log_totals
    )
    mixed_low = mixed.reshape(tok_rows, width).astype(jnp.bfloat16)
    resid = token_rows + jnp.dot(mixed_low, output_full, preferred_element_type=jnp.float32)
    mix_inv = lax.rsqrt(jnp.mean(resid * resid, axis=-1, keepdims=True) + epsilon)
    normed_mix = (resid * mix_inv * mixer_gain_f).astype(jnp.bfloat16)
    logits = jnp.dot(normed_mix, router_full, preferred_element_type=jnp.float32)
    probs = jax.nn.softmax(logits, axis=-1)
    route_ids = routes.reshape(tok_rows, top_count)
    chosen = (route_ids[:, :, None] == jnp.arange(num_experts)[None, None, :]) & valid[
        :, None, None
    ]
    gates = jnp.sum(jnp.where(chosen, probs[:, None, :], 0.0), axis=2)
    chosen_flat = chosen.reshape(tok_rows * top_count, num_experts).astype(jnp.int32)
    earlier = jnp.cumsum(chosen_flat, axis=0) - chosen_flat
    places = jnp.sum(earlier * chosen_flat, axis=1).reshape(tok_rows, top_count)
    slot_ids = jnp.where(valid[:, None], route_ids * capacity + places, -1)
    picked = slot_ids[None, :, :] == jnp.arange(num_experts * capacity)[:, None, None]
    route_map = jnp.any(picked, axis=2).astype(jnp.bfloat16)
    gate_map = jnp.sum(jnp.where(picked, gates[None, :, :], 0.0), axis=2)
    counts = jnp.sum(chosen_flat, axis=0).astype(jnp.float32)
    mass = jnp.sum(probs * live, axis=0)
    counts_all, mass_all = lax.psum((counts, mass), ("dp", "expert"))
    fraction = counts_all / (top_count * all_slots)
    balance_loss = (num_experts * jnp.sum(fraction * mass_all / all_slots)).reshape(1)
    outgoing = jnp.dot(route_map, normed_mix, preferred_element_type=jnp.float32).astype(
        jnp.bfloat16
    )
    outgoing = outgoing.reshape(groups, local_experts, capacity, width)
    gate_full, up_full, down_full = (
        lax.all_gather(expert_gate, "dp", axis=1, tiled=True),
        lax.all_gather(expert_up, "dp", axis=1, tiled=True),
        lax.all_gather(expert_down, "dp", axis=1, tiled=True),
    )
    arrived = lax.all_to_all(outgoing, "expert", split_axis=0, concat_axis=2, tiled=True)[0]
    gate_pre = jnp.einsum("jrd,jdf->jrf", arrived, gate_full, preferred_element_type=jnp.float32)
    up_pre = jnp.einsum("jrd,jdf->jrf", arrived, up_full, preferred_element_type=jnp.float32)
    hidden = (jax.nn.silu(gate_pre) * up_pre).astype(jnp.bfloat16)
    expert_out = jnp.einsum(
        "jrf,jdf->jrd", hidden, down_full, preferred_element_type=jnp.float32
    ).astype(jnp.bfloat16)
    returned = lax.all_to_all(
        expert_out[None], "expert", split_axis=2, concat_axis=0, tiled=True
    ).reshape(num_experts * capacity, width)
    gathered_out = jnp.take(returned, jnp.maximum(slot_ids, 0), axis=0).astype(jnp.float32)
    routed = jnp.sum(gates[:, :, None] * gathered_out, axis=1)
    switch = jax.nn.sigmoid(jnp.dot(normed_mix, switch_full, preferred_element_type=jnp.float32))[
        :, None
    ]
    shared_gate_pre = jnp.dot(normed_mix, shared_gate_full, preferred_element_type=jnp.float32)
    shared_up_pre = jnp.dot(normed_mix, shared_up_full, preferred_element_type=jnp.float32)
    shared_hidden = (jax.nn.silu(shared_gate_pre) * shared_up_pre).astype(jnp.bfloat16)
    shared_out = times_transpose(shared_hidden, shared_down_full)
    layer_out = ((resid + routed + switch * shared_out) * live).astype(jnp.bfloat16)
    grad_shared_out = (switch * grad_final).astype(jnp.bfloat16)
    grad_switch_logit = (
        jnp.sum(grad_final * shared_out, axis=1) * switch[:, 0] * (1.0 - switch[:, 0])
    )
    grad_shared_hidden = jnp.dot(
        grad_shared_out, shared_down_full, preferred_element_type=jnp.float32
    )
    grad_sg, grad_su = swiglu_back(grad_shared_hidden, shared_gate_pre, shared_up_pre)
    grad_sg = grad_sg.astype(jnp.bfloat16)
    grad_su = grad_su.astype(jnp.bfloat16)
    hidden_width = shared_gate_weight.shape[1]
    zero_pair = jnp.zeros((tok_rows, 2 * hidden_width), jnp.bfloat16)
    zero_single = jnp.zeros((tok_rows, hidden_width), jnp.bfloat16)
    right_block = jnp.concatenate(
        [
            jnp.concatenate([grad_sg, grad_su, zero_single], axis=1),
            jnp.concatenate([zero_pair, shared_hidden], axis=1),
        ],
        axis=0,
    )
    left_block = jnp.concatenate([normed_mix, grad_shared_out], axis=0)
    shared_grads = lax.psum_scatter(
        transpose_times(left_block, right_block), ("dp", "expert"), scatter_dimension=0, tiled=True
    )
    grad_shared_switch = jnp.dot(
        grad_switch_logit, normed_mix.astype(jnp.float32), precision=highest
    )
    grad_gates = jnp.sum(grad_final[:, None, :] * gathered_out, axis=2)
    grad_slots = jnp.dot(gate_map, grad_final, precision=highest).astype(jnp.bfloat16)
    grad_slots = grad_slots.reshape(groups, local_experts, capacity, width)
    grad_arrived = lax.all_to_all(grad_slots, "expert", split_axis=0, concat_axis=2, tiled=True)[0]
    grad_hidden = jnp.einsum(
        "jrd,jdf->jrf", grad_arrived, down_full, preferred_element_type=jnp.float32
    )
    grad_eg, grad_eu = swiglu_back(grad_hidden, gate_pre, up_pre)
    grad_eg = grad_eg.astype(jnp.bfloat16)
    grad_eu = grad_eu.astype(jnp.bfloat16)
    grad_in = (
        jnp.einsum("jrf,jdf->jrd", grad_eg, gate_full, preferred_element_type=jnp.float32)
        + jnp.einsum("jrf,jdf->jrd", grad_eu, up_full, preferred_element_type=jnp.float32)
    ).astype(jnp.bfloat16)
    expert_terms = (
        jnp.einsum("jrd,jrf->jdf", arrived, grad_eg, preferred_element_type=jnp.float32),
        jnp.einsum("jrd,jrf->jdf", arrived, grad_eu, preferred_element_type=jnp.float32),
        jnp.einsum("jrd,jrf->jdf", grad_arrived, hidden, preferred_element_type=jnp.float32),
    )
    grad_expert_gate, grad_expert_up, grad_expert_down = (
        lax.psum_scatter(
            expert_terms[0].astype(jnp.bfloat16), "dp", scatter_dimension=1, tiled=True
        ).astype(jnp.float32),
        lax.psum_scatter(
            expert_terms[1].astype(jnp.bfloat16), "dp", scatter_dimension=1, tiled=True
        ).astype(jnp.float32),
        lax.psum_scatter(
            expert_terms[2].astype(jnp.bfloat16), "dp", scatter_dimension=1, tiled=True
        ).astype(jnp.float32),
    )
    grad_returned = lax.all_to_all(
        grad_in[None], "expert", split_axis=2, concat_axis=0, tiled=True
    ).reshape(num_experts * capacity, width)
    grad_normed_mix = transpose_times(route_map, grad_returned)
    grad_probs = (
        jnp.sum(jnp.where(chosen, grad_gates[:, :, None], 0.0), axis=1)
        + live * (num_experts * fraction / all_slots)[None, :]
    )
    grad_logits = (
        probs * (grad_probs - jnp.sum(probs * grad_probs, axis=1, keepdims=True))
    ).astype(jnp.bfloat16)
    grad_router = transpose_times(normed_mix, grad_logits)
    grad_normed_mix = (
        grad_normed_mix
        + times_transpose(grad_sg, shared_gate_full)
        + times_transpose(grad_su, shared_up_full)
        + grad_switch_logit[:, None] * switch_full.astype(jnp.float32)[None, :]
        + times_transpose(grad_logits, router_full)
    )
    grad_mix_rows, grad_mixer_gain = norm_back(grad_normed_mix, resid, mix_inv, mixer_gain_f)
    grad_resid = grad_final + grad_mix_rows
    grad_branch = grad_resid.astype(jnp.bfloat16)
    grad_output_weight = transpose_times(mixed_low, grad_branch)
    grad_mixed = (
        times_transpose(grad_branch, output_full).astype(jnp.bfloat16).reshape(tok_rows, HEADS, HD)
    )
    delta = jnp.sum(grad_mixed.astype(jnp.float32) * (mixed + mixed_rest), axis=-1).T
    grad_queries, grad_keys_all, grad_values_all = attention_back(
        queries,
        keys_all,
        values_all,
        grad_mixed,
        positions,
        length,
        block_rows,
        scale,
        log_totals,
        delta,
    )
    grad_keys, grad_values = (
        lax.psum_scatter(grad_keys_all, "dp", scatter_dimension=0, tiled=True),
        lax.psum_scatter(grad_values_all, "dp", scatter_dimension=0, tiled=True),
    )
    grad_query_pre = (
        rotate_back(grad_queries, cosine, sine).reshape(tok_rows, width).astype(jnp.bfloat16)
    )
    grad_key_pre = (
        rotate_back(grad_keys, cosine, sine).reshape(tok_rows, width).astype(jnp.bfloat16)
    )
    grad_value_pre = grad_values.reshape(tok_rows, width).astype(jnp.bfloat16)
    grad_normed_attn = (
        times_transpose(grad_query_pre, query_full)
        + times_transpose(grad_key_pre, key_full)
        + times_transpose(grad_value_pre, value_full)
    )
    grad_attn_rows, grad_attention_gain = norm_back(
        grad_normed_attn, token_rows, attn_inv, attn_gain_f
    )
    grad_tokens = (grad_resid + grad_attn_rows).astype(jnp.bfloat16).reshape(1, tok_rows, width)
    (
        grad_query_weight,
        grad_key_weight,
        grad_value_weight,
        grad_output_shard,
        grad_query_bias,
        grad_key_bias,
        grad_value_bias,
        grad_attention_shard,
        grad_router_shard,
        grad_switch_shard,
        grad_mixer_shard,
    ) = (
        lax.psum_scatter(
            transpose_times(normed_attn, grad_query_pre),
            ("dp", "expert"),
            scatter_dimension=0,
            tiled=True,
        ),
        lax.psum_scatter(
            transpose_times(normed_attn, grad_key_pre),
            ("dp", "expert"),
            scatter_dimension=0,
            tiled=True,
        ),
        lax.psum_scatter(
            transpose_times(normed_attn, grad_value_pre),
            ("dp", "expert"),
            scatter_dimension=0,
            tiled=True,
        ),
        lax.psum_scatter(grad_output_weight, ("dp", "expert"), scatter_dimension=0, tiled=True),
        lax.psum_scatter(
            jnp.sum(grad_query_pre.astype(jnp.float32), axis=0),
            ("dp", "expert"),
            scatter_dimension=0,
            tiled=True,
        ),
        lax.psum_scatter(
            jnp.sum(grad_key_pre.astype(jnp.float32), axis=0),
            ("dp", "expert"),
            scatter_dimension=0,
            tiled=True,
        ),
        lax.psum_scatter(
            jnp.sum(grad_value_pre.astype(jnp.float32), axis=0),
            ("dp", "expert"),
            scatter_dimension=0,
            tiled=True,
        ),
        lax.psum_scatter(grad_attention_gain, ("dp", "expert"), scatter_dimension=0, tiled=True),
        lax.psum_scatter(grad_router, ("dp", "expert"), scatter_dimension=0, tiled=True),
        lax.psum_scatter(grad_shared_switch, ("dp", "expert"), scatter_dimension=0, tiled=True),
        lax.psum_scatter(grad_mixer_gain, ("dp", "expert"), scatter_dimension=0, tiled=True),
    )
    return (
        layer_out.reshape(1, tok_rows, width),
        balance_loss,
        grad_tokens,
        grad_query_weight,
        grad_key_weight,
        grad_value_weight,
        grad_output_shard,
        grad_query_bias,
        grad_key_bias,
        grad_value_bias,
        grad_attention_shard,
        grad_router_shard,
        grad_switch_shard,
        grad_mixer_shard,
        shared_grads[:, :hidden_width],
        shared_grads[:, hidden_width : 2 * hidden_width],
        shared_grads[:, 2 * hidden_width :],
        grad_expert_gate,
        grad_expert_up,
        grad_expert_down,
    )


def solution(mesh):
    placed = (
        P("expert", "dp", None),
        P("expert", "dp", None),
        P(),
        P("expert", "dp", None),
        P(("dp", "expert"), None),
        P(("dp", "expert"), None),
        P(("dp", "expert"), None),
        P(("dp", "expert"), None),
        P(("dp", "expert")),
        P(("dp", "expert")),
        P(("dp", "expert")),
        P(("dp", "expert")),
        P(("dp", "expert"), None),
        P(("dp", "expert")),
        P(("dp", "expert")),
        P(("dp", "expert"), None),
        P(("dp", "expert"), None),
        P(("dp", "expert"), None),
        P("expert", "dp", None),
        P("expert", "dp", None),
        P("expert", "dp", None),
    )
    return jax.shard_map(
        per_device,
        mesh=mesh,
        in_specs=placed,
        out_specs=(
            P("expert", "dp", None),
            P(),
            P("expert", "dp", None),
            P(("dp", "expert"), None),
            P(("dp", "expert"), None),
            P(("dp", "expert"), None),
            P(("dp", "expert"), None),
            P(("dp", "expert")),
            P(("dp", "expert")),
            P(("dp", "expert")),
            P(("dp", "expert")),
            P(("dp", "expert"), None),
            P(("dp", "expert")),
            P(("dp", "expert")),
            P(("dp", "expert"), None),
            P(("dp", "expert"), None),
            P(("dp", "expert"), None),
            P("expert", "dp", None),
            P("expert", "dp", None),
            P("expert", "dp", None),
        ),
        check_vma=False,
    )
```

profile of v0, /device:TPU:0, one launch (start us, length us, event | category | flops | bytes accessed | tf_op | source)
XLA Modules:
  0.0 5234.4 jit_solution(2402582556990608438)
XLA Ops:
  14.6 42.7 all-reduce.15
  96.1 74.0 %all-gather.20.cloned.1.call-done = bf16[2048,2048]{1,0:T(8,128)(2,1)} async-done(((bf16[64,2048]{1,0:T(8,128)(2,1)}), bf16[2048,2048]{1,0:T(8,128)(2,1)}) %all-gather.20.cloned.1.call-update) | async-done | bytes 8388624 | tf_op jit(solution)/shard_map/all_gather | solution.py:250
  177.2 72.0 %all-gather.14.cloned.1.call-done = bf16[2048,2048]{1,0:T(8,128)(2,1)} async-done(((bf16[64,2048]{1,0:T(8,128)(2,1)}), bf16[2048,2048]{1,0:T(8,128)(2,1)}) %all-gather.14.cloned.1.call-update) | async-done | bytes 8388624 | tf_op jit(solution)/shard_map/all_gather | solution.py:251
  263.6 40.6 all-gather
  330.8 69.0 %all-gather.16.cloned.1.call-done = bf16[1024,16,128]{0,2,1:T(8,128)(2,1)} async-done(((bf16[128,16,128]{0,2,1:T(8,128)(2,1)}), bf16[1024,16,128]{0,2,1:T(8,128)(2,1)}) %all-gather.16.cloned.1.call-update) | async-done | bytes 4194320 | tf_op jit(solution)/shard_map/all_gather | solution.py:283
  408.0 70.3 %all-gather.24.cloned.1.call-done = bf16[2048,2048]{1,0:T(8,128)(2,1)} async-done(((bf16[64,2048]{1,0:T(8,128)(2,1)}), bf16[2048,2048]{1,0:T(8,128)(2,1)}) %all-gather.24.cloned.1.call-update) | async-done | bytes 8388624 | tf_op jit(solution)/shard_map/all_gather | solution.py:252
  565.1 77.7 %all-gather.28.cloned.1.call-done = bf16[2,2048,1408]{2,1,0:T(8,128)(2,1)} async-done(((bf16[2,256,1408]{2,1,0:T(8,128)(2,1)}), bf16[2,2048,1408]{2,1,0:T(8,128)(2,1)}) %all-gather.28.cloned.1.call-update) | async-done | bytes 11534352 | tf_op jit(solution)/shard_map/all_gather | solution.py:319
  651.7 155.2 %all-gather.26.cloned.1.call-done = bf16[2,2048,1408]{2,1,0:T(8,128)(2,1)} async-done(((bf16[2,256,1408]{2,1,0:T(8,128)(2,1)}), bf16[2,2048,1408]{2,1,0:T(8,128)(2,1)}) %all-gather.26.cloned.1.call-update) | async-done | bytes 11534352 | tf_op jit(solution)/shard_map/all_gather | solution.py:318
  815.7 155.2 %all-gather.30.cloned.1.call-done = bf16[2,2048,1408]{2,1,0:T(8,128)(2,1)} async-done(((bf16[2,256,1408]{2,1,0:T(8,128)(2,1)}), bf16[2,2048,1408]{2,1,0:T(8,128)(2,1)}) %all-gather.30.cloned.1.call-update) | async-done | bytes 11534352 | tf_op jit(solution)/shard_map/all_gather | solution.py:320
  1050.2 95.8 %psum.14 = f32[8]{0:T(128)S(1)} all-reduce(f32[8]{0:T(128)S(1)} %convert_element_type.252), channel_id=1, replica_groups=mesh['dp'=8,'expert'=4] {'dp','expert'}, use_global_device_ids=true, to_apply=%region_13.14 | all-reduce | flops 8 | bytes 64 | tf_op jit(solution)/shard_map/psum | solution.py:310
  1174.9 119.3 %all-gather.36.cloned.1.call-done = bf16[2048,5632]{1,0:T(8,128)(2,1)} async-done(((bf16[64,5632]{1,0:T(8,128)(2,1)}), bf16[2048,5632]{1,0:T(8,128)(2,1)}) %all-gather.36.cloned.1.call-update) | async-done | bytes 23068688 | tf_op jit(solution)/shard_map/all_gather | solution.py:262
  1306.7 133.1 %all-gather.32.cloned.1.call-done = bf16[2048,5632]{1,0:T(8,128)(2,1)} async-done(((bf16[64,5632]{1,0:T(8,128)(2,1)}), bf16[2048,5632]{1,0:T(8,128)(2,1)}) %all-gather.32.cloned.1.call-update) | async-done | bytes 23068688 | tf_op jit(solution)/shard_map/all_gather | solution.py:260
  1576.8 49.4 fusion.2
  1675.3 142.1 %reduce-scatter.13.cloned.1.call-done = f32[128,16,128]{2,0,1:T(8,128)} async-done(((f32[1024,16,128]{2,0,1:T(8,128)}), f32[128,16,128]{2,0,1:T(8,128)}) %reduce-scatter.13.cloned.1.call-update) | async-done | bytes 1048592 | tf_op jit(solution)/shard_map/reduce_scatter | solution.py:439
  1836.6 116.7 %reduce-scatter.31.cloned.1.call-done = f32[64,8]{1,0:T(8,128)} async-done(((f32[2048,8]{1,0:T(8,128)}), f32[64,8]{1,0:T(8,128)}) %reduce-scatter.31.cloned.1.call-update) | async-done | bytes 2064
  1954.7 191.1 %reduce-scatter.29.cloned.1.call-done = bf16[2,256,1408]{2,1,0:T(8,128)(2,1)} async-done(((bf16[2,2048,1408]{2,1,0:T(8,128)(2,1)}), bf16[2,256,1408]{2,1,0:T(8,128)(2,1)}) %reduce-scatter.29.cloned.1.call-update) | async-done | bytes 1441808 | tf_op jit(solution)/shard_map/reduce_scatter | solution.py:395
  2148.9 192.4 %reduce-scatter.27.cloned.1.call-done = bf16[2,256,1408]{2,1,0:T(8,128)(2,1)} async-done(((bf16[2,2048,1408]{2,1,0:T(8,128)(2,1)}), bf16[2,256,1408]{2,1,0:T(8,128)(2,1)}) %reduce-scatter.27.cloned.1.call-update) | async-done | bytes 1441808 | tf_op jit(solution)/shard_map/reduce_scatter | solution.py:392
  2344.5 192.6 %reduce-scatter.25.cloned.1.call-done = bf16[2,256,1408]{2,1,0:T(8,128)(2,1)} async-done(((bf16[2,2048,1408]{2,1,0:T(8,128)(2,1)}), bf16[2,256,1408]{2,1,0:T(8,128)(2,1)}) %reduce-scatter.25.cloned.1.call-update) | async-done | bytes 1441808 | tf_op jit(solution)/shard_map/reduce_scatter | solution.py:389
  2554.3 41.2 all-reduce.14
  2601.6 1875.3 %all-reduce.18.cloned.1.call-done = f32[2048,16896]{1,0:T(8,128)} async-done(((f32[2048,16896]{1,0:T(8,128)}), f32[2048,16896]{1,0:T(8,128)}) %all-reduce.18.cloned.1.call-update) | async-done | bytes 138412048
  4482.0 181.8 %reduce-scatter.23.cloned.1.call-done = f32[64,2048]{1,0:T(8,128)} async-done(((f32[2048,2048]{1,0:T(8,128)}), f32[64,2048]{1,0:T(8,128)}) %reduce-scatter.23.cloned.1.call-update) | async-done | bytes 524304 | tf_op jit(solution)/shard_map/reduce_scatter | solution.py:489
  4663.8 187.5 %reduce-scatter.17.cloned.1.call-done = f32[64,2048]{1,0:T(8,128)} async-done(((f32[2048,2048]{1,0:T(8,128)}), f32[64,2048]{1,0:T(8,128)}) %reduce-scatter.17.cloned.1.call-update) | async-done | bytes 524304 | tf_op jit(solution)/shard_map/reduce_scatter | solution.py:471
  4851.4 187.6 %reduce-scatter.21.cloned.1.call-done = f32[64,2048]{1,0:T(8,128)} async-done(((f32[2048,2048]{1,0:T(8,128)}), f32[64,2048]{1,0:T(8,128)}) %reduce-scatter.21.cloned.1.call-update) | async-done | bytes 524304 | tf_op jit(solution)/shard_map/reduce_scatter | solution.py:483
  5038.9 187.6 %reduce-scatter.19.cloned.1.call-done = f32[64,2048]{1,0:T(8,128)} async-done(((f32[2048,2048]{1,0:T(8,128)}), f32[64,2048]{1,0:T(8,128)}) %reduce-scatter.19.cloned.1.call-update) | async-done | bytes 524304 | tf_op jit(solution)/shard_map/reduce_scatter | solution.py:477
  (351 shorter events, 566.5 us)
Async XLA Ops:
  7.2 83.9 %all-gather.18.cloned.1.call-start = ((), (), s32[]{:S(2)}) async-start(), calls=%async_computation.16 | async-start | bytes 8650752 | tf_op jit(solution)/shard_map/all_gather | solution.py:249
  7.9 162.2 %all-gather.20.cloned.1.call-start = ((), (), s32[]{:S(2)}) async-start(), calls=%async_computation.17 | async-start | bytes 8650752 | tf_op jit(solution)/shard_map/all_gather | solution.py:250
  8.7 240.5 %all-gather.14.cloned.1.call-start = ((), (), s32[]{:S(2)}) async-start(), calls=%async_computation.14 | async-start | bytes 8650752 | tf_op jit(solution)/shard_map/all_gather | solution.py:251
  9.4 314.5 %all-gather.22.cloned.1.call-start = ((), (), s32[]{:S(2)}) async-start(), calls=%async_computation.18 | async-start | bytes 4718592 | tf_op jit(solution)/shard_map/all_gather | solution.py:282
  177.1 222.7 %all-gather.16.cloned.1.call-start = ((), (), s32[]{:S(2)}) async-start(), calls=%async_computation.15 | async-start | bytes 4718592 | tf_op jit(solution)/shard_map/all_gather | solution.py:283
  254.9 223.4 %all-gather.24.cloned.1.call-start = ((), (), s32[]{:S(2)}) async-start(), calls=%async_computation.19 | async-start | bytes 8650752 | tf_op jit(solution)/shard_map/all_gather | solution.py:252
  255.5 387.3 %all-gather.28.cloned.1.call-start = ((), (), s32[]{:S(2)}) async-start(), calls=%async_computation.21 | async-start | bytes 12976128 | tf_op jit(solution)/shard_map/all_gather | solution.py:319
  256.3 550.6 %all-gather.26.cloned.1.call-start = ((), (), s32[]{:S(2)}) async-start(), calls=%async_computation.20 | async-start | bytes 12976128 | tf_op jit(solution)/shard_map/all_gather | solution.py:318
  257.0 713.9 %all-gather.30.cloned.1.call-start = ((), (), s32[]{:S(2)}) async-start(), calls=%async_computation.22 | async-start | bytes 12976128 | tf_op jit(solution)/shard_map/all_gather | solution.py:320
  257.8 904.7 %all-gather.34.cloned.1.call-start = ((), (), s32[]{:S(2)}) async-start(), calls=%async_computation.24 | async-start | bytes 23789568 | tf_op jit(solution)/shard_map/all_gather | solution.py:261
  258.3 1035.8 %all-gather.36.cloned.1.call-start = ((), (), s32[]{:S(2)}) async-start(), calls=%async_computation.25 | async-start | bytes 23789568 | tf_op jit(solution)/shard_map/all_gather | solution.py:262
  259.1 1180.6 %all-gather.32.cloned.1.call-start = ((), (), s32[]{:S(2)}) async-start(), calls=%async_computation.23 | async-start | bytes 23789568 | tf_op jit(solution)/shard_map/all_gather | solution.py:260
  1045.5 113.9 %all-to-all-start.3 = ((bf16[1,2,320,2048]{3,1,0,2:T(2,128)(2,1)}), bf16[1,2,320,2048]{3,1,0,2:T(2,128)(2,1)}, u32[]{:S(2)}, u32[]{:S(2)}) async-start(bf16[1,2,320,2048]{3,1,0,2:T(2,128)(2,1)} %copy.232), calls=%async_computation.3 | async-start | bytes 5242880 | tf_op jit(solution)/shard_map/all_to_all | solution.py:399
  1050.1 614.9 %reduce-scatter.15.cloned.1.call-start = ((), (), s32[]{:S(2)}) async-start(), calls=%async_computation.27 | async-start | bytes 9437184 | tf_op jit(solution)/shard_map/reduce_scatter | solution.py:440
  1517.3 300.1 %reduce-scatter.13.cloned.1.call-start = ((), (), s32[]{:S(2)}) async-start(), calls=%async_computation.26 | async-start | bytes 9437184 | tf_op jit(solution)/shard_map/reduce_scatter | solution.py:439
  1539.1 414.2 %reduce-scatter.31.cloned.1.call-start = ((), (), s32[]{:S(2)}) async-start(), calls=%async_computation.35 | async-start | bytes 1081344
  1540.7 605.2 %reduce-scatter.29.cloned.1.call-start = ((), (), s32[]{:S(2)}) async-start(), calls=%async_computation.34 | async-start | bytes 12976128 | tf_op jit(solution)/shard_map/reduce_scatter | solution.py:395
  1551.8 789.5 %reduce-scatter.27.cloned.1.call-start = ((), (), s32[]{:S(2)}) async-start(), calls=%async_computation.33 | async-start | bytes 12976128 | tf_op jit(solution)/shard_map/reduce_scatter | solution.py:392
  1564.4 972.6 %reduce-scatter.25.cloned.1.call-start = ((), (), s32[]{:S(2)}) async-start(), calls=%async_computation.32 | async-start | bytes 12976128 | tf_op jit(solution)/shard_map/reduce_scatter | solution.py:389
  1575.1 2901.8 %all-reduce.18.cloned.1.call-start = ((), (), s32[]{:S(2)}) async-start(), calls=%async_computation.36 | async-start | bytes 276824064
  1626.2 3037.6 %reduce-scatter.23.cloned.1.call-start = ((), (), s32[]{:S(2)}) async-start(), calls=%async_computation.31 | async-start | bytes 17301504 | tf_op jit(solution)/shard_map/reduce_scatter | solution.py:489
  1636.1 3215.2 %reduce-scatter.17.cloned.1.call-start = ((), (), s32[]{:S(2)}) async-start(), calls=%async_computation.28 | async-start | bytes 17301504 | tf_op jit(solution)/shard_map/reduce_scatter | solution.py:471
  1651.3 3387.6 %reduce-scatter.21.cloned.1.call-start = ((), (), s32[]{:S(2)}) async-start(), calls=%async_computation.30 | async-start | bytes 17301504 | tf_op jit(solution)/shard_map/reduce_scatter | solution.py:483
  1675.1 3551.4 %reduce-scatter.19.cloned.1.call-start = ((), (), s32[]{:S(2)}) async-start(), calls=%async_computation.29 | async-start | bytes 17301504 | tf_op jit(solution)/shard_map/reduce_scatter | solution.py:477
  (70 other events, 2584.9 us)
Sparse Core Ops, SparseCore 0:
  10.9 80.1 all-gather.17
  93.9 76.1 all-gather.19
  173.0 76.1 all-gather.13
  251.8 72.0 all-gather.21
  326.4 73.4 all-gather.15
  402.6 75.7 all-gather.23
  480.5 162.2 all-gather.27
  645.0 161.8 all-gather.25
  809.1 161.8 all-gather.29
  973.7 174.7 all-gather.33
  1151.3 142.8 all-gather.35
  1296.9 142.7 all-gather.31
  1517.4 147.6 reduce-scatter.14
  1669.0 148.4 reduce-scatter.12
  1819.5 133.7 reduce-scatter.30
  1957.2 188.5 reduce-scatter.28
  2149.7 191.6 reduce-scatter.26
  2345.2 191.7 reduce-scatter.24
  2544.6 1932.2 all-reduce.17
  4479.7 184.0 reduce-scatter.22
  4666.8 184.5 reduce-scatter.16
  4854.3 184.5 reduce-scatter.20
  5041.9 184.5 reduce-scatter.18
where the time goes:
time: 5240 us; the launch traced here: 5230 us
  waiting for transfers between devices  4520 us (86%)
  matrix products  360 us (7%)
  blocking collectives  220 us (4%)
  local copies, waits for them, and re-layouts  63.5 us (1%)
    unnamed x25, waiting for transfers between devices  2000 us
    reduce_scatter x1, waiting for transfers between devices, per_device(): lax.psum_scatter(expert_terms[0].astype(jnp.bfloat16), 'dp', scatter_dime...  193 us
    reduce_scatter x1, waiting for transfers between devices, per_device(): lax.psum_scatter(expert_terms[1].astype(jnp.bfloat16), 'dp', scatter_dime...  192 us
    reduce_scatter x1, waiting for transfers between devices, per_device(): lax.psum_scatter(expert_terms[2].astype(jnp.bfloat16), 'dp', scatter_dime...  191 us
    reduce_scatter x1, waiting for transfers between devices, per_device(): lax.psum_scatter(transpose_times(normed_attn, grad_key_pre), ('dp', 'expe...  188 us
    reduce_scatter x1, waiting for transfers between devices, per_device(): lax.psum_scatter(transpose_times(normed_attn, grad_value_pre), ('dp', 'ex...  188 us
    reduce_scatter x1, waiting for transfers between devices, per_device(): lax.psum_scatter(transpose_times(normed_attn, grad_query_pre), ('dp', 'ex...  188 us
    reduce_scatter x1, waiting for transfers between devices, per_device(): lax.psum_scatter(grad_output_weight, ('dp', 'expert'), scatter_dimension=...  182 us
  transfers between devices with their start and end apart: 27, of which 25 were waited for; matrix products, arithmetic and copies ran while one was open for 7% of the time, Pallas kernels for 0%

commit v1 on v0

v1 whole, which is shorter than its diff:
```python
import jax
import jax.numpy as jnp
from jax import lax
from jax.sharding import PartitionSpec as P

HEADS = 16
HD = 128
LANES = 128
PLANES = 4
PAIR = 2

f32 = jnp.float32
bf16 = jnp.bfloat16

epsilon = 1e-06
rope_base = 1000000.0
highest = lax.Precision.HIGHEST
neg_large = -1e30


def mm(left, right, contract=((1,), (0,))):
    return lax.dot_general(left, right, (contract, ((), ())), preferred_element_type=f32)


def mm_t(left, right):
    return mm(left, right, ((1,), (1,)))


def t_mm(left, right):
    return mm(left, right, ((0,), (0,)))


def rope_tables(positions, head_width):
    halfway = head_width // 2
    freqs = rope_base ** (-jnp.arange(halfway, dtype=f32) * 2.0 / head_width)
    angles = positions.astype(f32)[:, None] * freqs[None, :]
    angles = jnp.concatenate([angles, angles], axis=1)
    return (jnp.cos(angles), jnp.sin(angles))


def rotate(values, cosine, sine):
    halfway = values.shape[-1] // 2
    turned = jnp.concatenate([-values[..., halfway:], values[..., :halfway]], axis=-1)
    return values * cosine[:, None, :] + turned * sine[:, None, :]


def rotate_back(grads_in, cosine, sine):
    halfway = grads_in.shape[-1] // 2
    scaled = grads_in * sine[:, None, :]
    turned = jnp.concatenate([scaled[..., halfway:], -scaled[..., :halfway]], axis=-1)
    return grads_in * cosine[:, None, :] + turned


def norm_back(grad_normed, rows_in, inverse, gain):
    weighted = grad_normed * gain
    inner = jnp.sum(weighted * rows_in, axis=-1, keepdims=True)
    grad_rows = inverse * weighted - rows_in * inverse**3 * inner / rows_in.shape[-1]
    grad_gain = jnp.sum(grad_normed * rows_in * inverse, axis=0)
    return (grad_rows, grad_gain)


def add_low(*parts):
    total = parts[0].astype(f32)
    for part in parts[1:]:
        total = total + part.astype(f32)
    return total.astype(bf16)


class Links:
    def __init__(self, dp_size, expert_size):
        self.planes = PLANES
        self.across = dp_size // PLANES
        self.rows = expert_size // PAIR
        self.sizes = dict(z=PLANES, x=self.across, y=self.rows, c=PAIR)
        self.total = dp_size * expert_size
        dp_index = lax.axis_index("dp")
        expert_index = lax.axis_index("expert")
        self.at = dict(
            z=dp_index // self.across,
            x=dp_index % self.across,
            y=expert_index // PAIR,
            c=expert_index % PAIR,
        )

    def place(self, index):
        c = index % PAIR
        y = index // PAIR % self.rows
        x = index // (PAIR * self.rows) % self.across
        z = index // (PAIR * self.rows * self.across)
        return dict(z=z, x=x, y=y, c=c)

    def index(self, where):
        return (
            (where["z"] * self.across + where["x"]) * self.rows + where["y"]
        ) * PAIR + where["c"]

    def send(self, value, target):
        pairs = []
        for source in range(self.total):
            goal = target(self.place(source))
            if goal is not None:
                pairs.append((source, self.index(goal)))
        return lax.ppermute(value, ("dp", "expert"), pairs)

    def turn(self, value, axis, steps):
        size = self.sizes[axis]
        return self.send(value, lambda w: {**w, axis: (w[axis] + steps) % size})

    def swap(self, value, axis, bit):
        return self.send(value, lambda w: {**w, axis: w[axis] ^ bit})

    def step(self, value, steps, lowest, highest_at):
        return self.send(
            value,
            lambda w: {**w, "z": w["z"] + steps} if lowest <= w["z"] <= highest_at else None,
        )

    def behind(self, axis, steps):
        return (self.at[axis] - steps) % self.sizes[axis]

    def ahead(self, axis, steps):
        return (self.at[axis] + steps) % self.sizes[axis]

    def gather_z(self, value):
        return [value] + [self.turn(value, "z", s) for s in range(1, PLANES)]

    def scatter_z(self, blocks):
        got = [self.turn(blocks[s], "z", -s) for s in range(1, PLANES)]
        return [blocks[0]] + got

    def gather_x(self, value):
        return [value] + [self.turn(value, "x", t) for t in range(1, self.across)]

    def place_rows(self, blocks, axis, dim):
        shape = blocks[0].shape[:dim] + (self.sizes[axis],) + blocks[0].shape[dim:]
        buffer = jnp.zeros(shape, blocks[0].dtype)
        for s, block in enumerate(blocks):
            buffer = lax.dynamic_update_slice_in_dim(
                buffer, jnp.expand_dims(block, dim), self.behind(axis, s), dim
            )
        return buffer

    def pick(self, value, index, dim):
        return lax.dynamic_index_in_dim(value, index, dim, keepdims=False)

    def reduce_all(self, value):
        for axis in ("c", "y", "x", "z"):
            bit = 1
            while bit < self.sizes[axis]:
                value = value + self.swap(value, axis, bit)
                bit *= 2
        return value

    def scatter_axis(self, value, axis, dim):
        total = self.pick(value, self.at[axis], dim).astype(f32)
        for s in range(1, self.sizes[axis]):
            total = total + self.turn(
                self.pick(value, self.ahead(axis, s), dim), axis, s
            ).astype(f32)
        return total


def per_device(
    tokens,
    cotangent,
    lengths,
    routes,
    query_weight,
    key_weight,
    value_weight,
    output_weight,
    query_bias,
    key_bias,
    value_bias,
    attention_gain,
    router_weight,
    shared_switch,
    mixer_gain,
    shared_gate_weight,
    shared_up_weight,
    shared_down_weight,
    expert_gate,
    expert_up,
    expert_down,
):
    dp_size = lax.axis_size("dp")
    groups = lax.axis_size("expert")
    net = Links(dp_size, groups)
    across, yrows = net.across, net.rows
    rows = tokens.shape[1]
    width = tokens.shape[2]
    top_count = routes.shape[2]
    local_experts = expert_gate.shape[0]
    num_experts = local_experts * groups
    units = local_experts + 1
    inner = expert_gate.shape[2]
    weight_rows = expert_gate.shape[1]
    shard = query_weight.shape[0]
    head_cols = width // PLANES
    heads = head_cols // HD
    window = -(-inner // (PLANES * LANES)) * LANES
    scale = HD ** (-0.5)
    all_slots = float(groups * rows * dp_size)
    iz, ix, iy, ic = net.at["z"], net.at["x"], net.at["y"], net.at["c"]
    expert_at = lax.axis_index("expert")

    tok = tokens.reshape(rows, width)
    cot = cotangent.reshape(rows, width)
    length = jnp.take(lengths, expert_at)
    own_start = lax.axis_index("dp") * rows
    positions = own_start + jnp.arange(rows)
    valid = positions < length
    live = valid.astype(f32)[:, None]
    token_rows = tok.astype(f32)
    grad_final = cot.astype(f32) * live

    tok_blocks = net.gather_z(tok)
    extras = jnp.concatenate(
        [
            attention_gain[:, None],
            mixer_gain[:, None],
            shared_switch[:, None],
            router_weight,
            jnp.zeros((shard, LANES - 3 - num_experts), bf16),
        ],
        axis=1,
    )

    def head_slice(goal):
        return jnp.concatenate(
            [
                lax.dynamic_slice_in_dim(w, goal * head_cols, head_cols, 1)
                for w in (query_weight, key_weight, value_weight)
            ]
            + [extras],
            axis=1,
        )

    qkv_blocks = [
        head_slice(iz) if s == 0 else net.turn(head_slice(net.ahead("z", s)), "z", s)
        for s in range(PLANES)
    ]
    qkv_w = net.place_rows(qkv_blocks, "z", 0)
    qkv_w = net.place_rows(net.gather_x(qkv_w), "x", 1)
    qkv_w = net.place_rows([qkv_w, net.turn(qkv_w, "y", 1)], "y", 2)
    qkv_w = net.place_rows([qkv_w, net.turn(qkv_w, "c", 1)], "c", 3)
    qkv_w = qkv_w.reshape(width, 3 * head_cols + LANES)
    small = qkv_w[:, 3 * head_cols :]
    qkv_w = qkv_w[:, : 3 * head_cols]
    attn_gain_f = small[:, 0].astype(f32)
    mixer_gain_f = small[:, 1].astype(f32)
    switch_full = small[:, 2]
    router_full = small[:, 3 : 3 + num_experts]

    biases = jnp.concatenate(
        [
            query_bias[:, None],
            key_bias[:, None],
            value_bias[:, None],
            jnp.zeros((shard, LANES - 3), bf16),
        ],
        axis=1,
    )
    out_w = jnp.concatenate([output_weight, biases], axis=1)
    out_w = net.place_rows(net.gather_x(out_w), "x", 0)
    out_w = net.place_rows([out_w, net.turn(out_w, "y", 1)], "y", 1)
    out_w = net.place_rows([out_w, net.turn(out_w, "c", 1)], "c", 2)
    out_w = out_w.reshape(head_cols, width + LANES)
    bias_cols = out_w[:, width : width + 3].astype(f32)
    out_w = out_w[:, :width]
    qkv_bias = jnp.concatenate([bias_cols[:, 0], bias_cols[:, 1], bias_cols[:, 2]])

    def start_of(goal):
        return jnp.minimum(goal * window, inner - window)

    shared_stack = [
        w.reshape(shard, groups, inner)
        for w in (shared_gate_weight, shared_up_weight, shared_down_weight)
    ]

    def shared_for(dy, dc):
        goal = net.ahead("y", dy) * PAIR + net.ahead("c", dc)
        return jnp.stack([net.pick(w, goal, 1) for w in shared_stack])

    shared_rows = jnp.zeros((3, groups, shard, inner), bf16)
    for dy in range(yrows):
        for dc in range(PAIR):
            block = shared_for(dy, dc)
            if dy or dc:
                block = net.send(
                    block,
                    lambda w, dy=dy, dc=dc: {
                        **w,
                        "y": (w["y"] + dy) % yrows,
                        "c": (w["c"] + dc) % PAIR,
                    },
                )
            origin = net.behind("y", dy) * PAIR + net.behind("c", dc)
            shared_rows = lax.dynamic_update_slice_in_dim(
                shared_rows, block[:, None], origin, 1
            )
    shared_rows = shared_rows.reshape(3, groups * shard, inner)
    gate_set = [expert_gate[j] for j in range(local_experts)] + [shared_rows[0]]
    up_set = [expert_up[j] for j in range(local_experts)] + [shared_rows[1]]
    down_set = [expert_down[j] for j in range(local_experts)] + [shared_rows[2]]

    def spread(arrays):
        wide = len(arrays) * window
        full = jnp.zeros((PLANES, across, weight_rows, wide), bf16)
        for s in range(PLANES):
            goal = start_of(net.ahead("z", s))
            block = jnp.concatenate(
                [lax.dynamic_slice_in_dim(w, goal, window, 1) for w in arrays], axis=1
            )
            if s:
                block = net.turn(block, "z", s)
            for t, piece in enumerate(net.gather_x(block)):
                full = lax.dynamic_update_slice(
                    full, piece[None, None], (net.behind("z", s), net.behind("x", t), 0, 0)
                )
        return full.reshape(width, wide)

    def gather_group(value):
        blocks = net.gather_z(value)
        blocks = [[b, net.turn(b, "y", 1)] for b in blocks]
        flat = [b for pair in blocks for b in pair]
        both = jnp.stack(flat)
        other = net.turn(both, "c", 1)
        return jnp.concatenate([both, other], axis=0).reshape(-1, value.shape[1])

    def scatter_group(value, size):
        parts = value.reshape(2, PLANES, yrows, size, -1)
        kept = []
        for s in (1, 2, 3, 0):
            pair = parts[0, s].astype(f32) + net.turn(parts[1, s], "c", 1).astype(f32)
            pair = pair.astype(bf16)
            one = add_low(pair[0], net.turn(pair[1], "y", 1))
            kept.append(net.turn(one, "z", -s) if s else one)
        total = kept[0].astype(f32)
        for part in kept[1:]:
            total = total + part.astype(f32)
        return total

    cot_group = gather_group(cot)
    down_w = spread(down_set)
    gate_w = spread(gate_set)
    up_w = spread(up_set)

    hidden_rows = jnp.concatenate(tok_blocks, axis=0)
    hidden_f = hidden_rows.astype(f32)
    attn_inv_group = lax.rsqrt(jnp.mean(hidden_f * hidden_f, axis=-1, keepdims=True) + epsilon)
    normed_attn = (hidden_f * attn_inv_group * attn_gain_f).astype(bf16)
    qkv_pre = mm(normed_attn, qkv_w) + qkv_bias
    query_pos = jnp.concatenate(
        [
            (net.behind("z", s) * across + ix) * rows + jnp.arange(rows)
            for s in range(PLANES)
        ]
    )
    group_rows = PLANES * rows
    cosine, sine = rope_tables(query_pos, HD)
    queries = rotate(
        qkv_pre[:, :head_cols].reshape(group_rows, heads, HD), cosine, sine
    ).astype(bf16)
    keys_own = (
        rotate(
            qkv_pre[:, head_cols : 2 * head_cols].reshape(group_rows, heads, HD), cosine, sine
        )
        .astype(bf16)
        .reshape(group_rows, head_cols)
    )
    values_own = qkv_pre[:, 2 * head_cols :].astype(bf16)
    keys_values = net.gather_x(jnp.concatenate([keys_own, values_own], axis=1))
    key_pos = jnp.concatenate(
        [query_pos + (net.behind("x", t) - ix) * rows for t in range(across)]
    )
    all_kv = jnp.concatenate(keys_values, axis=0)
    keys_all = all_kv[:, :head_cols].reshape(-1, heads, HD)
    values_all = all_kv[:, head_cols:].reshape(-1, heads, HD)
    scores = jnp.einsum("qhd,khd->hqk", queries, keys_all, preferred_element_type=f32) * scale
    allowed = (key_pos[None, :] <= query_pos[:, None]) & (key_pos[None, :] < length)
    scores = jnp.where(allowed[None], scores, neg_large)
    attn_weights = jax.nn.softmax(scores, axis=-1)
    weights_low = attn_weights.astype(bf16)
    mixed = jnp.einsum("hqk,khd->qhd", weights_low, values_all, preferred_element_type=f32)
    mixed = mixed.astype(bf16).reshape(group_rows, head_cols)
    branch = mm(mixed, out_w).astype(bf16).reshape(PLANES, rows, width)
    resid = token_rows
    for part in net.scatter_z([branch[s] for s in range(PLANES)]):
        resid = resid + part.astype(f32)

    mix_inv = lax.rsqrt(jnp.mean(resid * resid, axis=-1, keepdims=True) + epsilon)
    normed_mix = (resid * mix_inv * mixer_gain_f).astype(bf16)
    logits = mm(normed_mix, router_full)
    probs = jax.nn.softmax(logits, axis=-1)
    route_ids = routes.reshape(rows, top_count)
    chosen = (route_ids[:, :, None] == jnp.arange(num_experts)[None, None, :]) & valid[
        :, None, None
    ]
    chosen_any = jnp.sum(chosen.astype(f32), axis=1)
    gates = probs * chosen_any
    switch = jax.nn.sigmoid(mm(normed_mix, switch_full[:, None]))
    gate_columns = jnp.concatenate([gates, switch * live], axis=1)
    gate_high = lax.reduce_precision(gate_columns, 8, 7)
    gate_rest = gate_columns - gate_high
    gate_count = num_experts + 1
    payload = jnp.concatenate(
        [
            normed_mix,
            gate_high.astype(bf16),
            gate_rest.astype(bf16),
            jnp.zeros((rows, LANES - 2 * gate_count), bf16),
        ],
        axis=1,
    )
    mix_group = gather_group(payload)
    gate_group = mix_group[:, width : width + 2 * gate_count].astype(f32)
    gate_group = gate_group[:, :gate_count] + gate_group[:, gate_count:]
    mix_group = mix_group[:, :width]
    counts = jnp.sum(chosen_any, axis=0)
    mass = jnp.sum(probs * live, axis=0)
    sums = net.reduce_all(jnp.concatenate([counts, mass]).reshape(1, -1))[0]
    fraction = sums[:num_experts] / (top_count * all_slots)
    balance_loss = (
        num_experts * jnp.sum(fraction * sums[num_experts:] / all_slots)
    ).reshape(1)

    unit_gates = jnp.concatenate(
        [
            lax.dynamic_slice_in_dim(gate_group, expert_at * local_experts, local_experts, 1),
            gate_group[:, num_experts:],
        ],
        axis=1,
    )
    column = jnp.arange(window)
    fresh = (column + start_of(iz) >= iz * window).astype(f32)
    wide_gate = (unit_gates[:, :, None] * fresh[None, None, :]).reshape(-1, units * window)
    fresh_wide = jnp.tile(fresh, units)
    grad_hid = mm(cot_group, down_w)
    gate_pre = mm(mix_group, gate_w)
    up_pre = mm(mix_group, up_w)
    sigma = jax.nn.sigmoid(gate_pre)
    act = gate_pre * sigma
    hidden = act * up_pre
    hidden_gated = (hidden * wide_gate).astype(bf16)
    gated_grad = grad_hid * wide_gate
    grad_gate_pre = (gated_grad * up_pre * sigma * (1.0 + gate_pre * (1.0 - sigma))).astype(bf16)
    grad_up_pre = (gated_grad * act).astype(bf16)
    unit_grads = jnp.sum(
        (hidden * grad_hid * fresh_wide).reshape(-1, units, window), axis=2
    )
    out_group = mm_t(hidden_gated, down_w).astype(bf16)
    grad_in = (mm_t(grad_gate_pre, gate_w) + mm_t(grad_up_pre, up_w)).astype(bf16)
    spot = (
        jnp.arange(num_experts)[None, :] == (expert_at * local_experts + jnp.arange(local_experts))[:, None]
    ).astype(f32)
    expert_grads = jnp.sum(unit_grads[:, :local_experts, None] * spot[None], axis=1)
    grad_payload = jnp.concatenate(
        [
            grad_in,
            expert_grads.astype(bf16),
            unit_grads[:, local_experts:].astype(bf16),
            jnp.zeros((grad_in.shape[0], LANES - gate_count), bf16),
        ],
        axis=1,
    )
    grad_sum = scatter_group(grad_payload, rows)
    grad_gates = grad_sum[:, width : width + num_experts]
    grad_switch = grad_sum[:, width + num_experts : width + gate_count]

    grad_switch_logit = grad_switch * live * switch * (1.0 - switch)
    grad_probs = grad_gates * chosen_any * live + live * (num_experts * fraction / all_slots)[None, :]
    grad_logits = (
        probs * (grad_probs - jnp.sum(probs * grad_probs, axis=1, keepdims=True))
    ).astype(bf16)
    grad_normed_mix = (
        grad_sum[:, :width]
        + grad_switch_logit * switch_full.astype(f32)[None, :]
        + mm_t(grad_logits, router_full)
    )
    grad_mix_rows, grad_mixer_gain = norm_back(grad_normed_mix, resid, mix_inv, mixer_gain_f)
    grad_resid = grad_final + grad_mix_rows
    grad_branch = grad_resid.astype(bf16)
    branch_group = jnp.concatenate(net.gather_z(grad_branch), axis=0)

    grad_mixed = mm_t(branch_group, out_w).astype(bf16).reshape(group_rows, heads, HD)
    grad_attn = jnp.einsum("qhd,khd->hqk", grad_mixed, values_all, preferred_element_type=f32)
    delta = jnp.sum(attn_weights * grad_attn, axis=-1, keepdims=True)
    grad_scores = (attn_weights * (grad_attn - delta)).astype(bf16)
    grad_keys = (
        jnp.einsum("hqk,qhd->khd", grad_scores, queries, preferred_element_type=f32) * scale
    )
    grad_values = jnp.einsum("hqk,qhd->khd", weights_low, grad_mixed, preferred_element_type=f32)
    grad_kv = jnp.concatenate(
        [grad_keys.reshape(-1, head_cols), grad_values.reshape(-1, head_cols)], axis=1
    ).reshape(across, group_rows, 2 * head_cols)
    grad_kv_own = grad_kv[0]
    for t in range(1, across):
        grad_kv_own = grad_kv_own + net.turn(grad_kv[t].astype(bf16), "x", -t).astype(f32)
    grad_queries = (
        jnp.einsum("hqk,khd->qhd", grad_scores, keys_all, preferred_element_type=f32) * scale
    )
    grad_query_pre = (
        rotate_back(grad_queries, cosine, sine).reshape(group_rows, head_cols).astype(bf16)
    )
    grad_key_pre = (
        rotate_back(grad_kv_own[:, :head_cols].reshape(group_rows, heads, HD), cosine, sine)
        .reshape(group_rows, head_cols)
        .astype(bf16)
    )
    grad_value_pre = grad_kv_own[:, head_cols:].astype(bf16)
    grad_qkv = jnp.concatenate([grad_query_pre, grad_key_pre, grad_value_pre], axis=1)
    grad_normed_part = mm_t(grad_qkv, qkv_w)
    gain_part = jnp.sum(grad_normed_part * hidden_f * attn_inv_group, axis=0)
    normed_part_low = grad_normed_part.astype(bf16).reshape(PLANES, rows, width)
    grad_normed_attn = jnp.zeros((rows, width), f32)
    for part in net.scatter_z([normed_part_low[s] for s in range(PLANES)]):
        grad_normed_attn = grad_normed_attn + part.astype(f32)
    attn_inv = attn_inv_group[:rows]
    grad_attn_rows, _ = norm_back(grad_normed_attn, token_rows, attn_inv, attn_gain_f)
    grad_tokens = (grad_resid + grad_attn_rows).astype(bf16).reshape(1, rows, width)

    out_sum = scatter_group(out_group, rows)
    layer_out = ((resid + out_sum) * live).astype(bf16)

    def unspread(grad_full):
        wide = grad_full.shape[1]
        blocks = grad_full.astype(bf16).reshape(PLANES, across, weight_rows, wide)
        mine = net.scatter_axis(blocks, "x", 1).astype(bf16)
        got = [
            net.turn(net.pick(mine, net.ahead("z", s), 0), "z", s) if s else net.pick(mine, iz, 0)
            for s in range(PLANES)
        ]
        by_plane = net.place_rows(got, "z", 0)
        result = []
        for j in range(units):
            cols = [by_plane[k, :, j * window : (j + 1) * window] for k in range(PLANES)]
            used = window * (PLANES - 1)
            cols[-1] = cols[-1][:, window - (inner - used) :]
            result.append(jnp.concatenate(cols, axis=1))
        return result

    grads_down = unspread(t_mm(cot_group, hidden_gated))
    grads_gate = unspread(t_mm(mix_group, grad_gate_pre))
    grads_up = unspread(t_mm(mix_group, grad_up_pre))
    grad_expert_gate = jnp.stack(grads_gate[:local_experts]).astype(f32)
    grad_expert_up = jnp.stack(grads_up[:local_experts]).astype(f32)
    grad_expert_down = jnp.stack(grads_down[:local_experts]).astype(f32)
    shared_parts = jnp.stack(
        [g[local_experts].reshape(groups, shard, inner) for g in (grads_gate, grads_up, grads_down)]
    )
    shared_grads = jnp.zeros((3, groups, shard, inner), bf16)
    for dy in range(yrows):
        for dc in range(PAIR):
            goal = net.ahead("y", dy) * PAIR + net.ahead("c", dc)
            block = net.pick(shared_parts, goal, 1)
            if dy or dc:
                block = net.send(
                    block,
                    lambda w, dy=dy, dc=dc: {
                        **w,
                        "y": (w["y"] + dy) % yrows,
                        "c": (w["c"] + dc) % PAIR,
                    },
                )
            origin = net.behind("y", dy) * PAIR + net.behind("c", dc)
            shared_grads = lax.dynamic_update_slice_in_dim(
                shared_grads, block[:, None], origin, 1
            )
    shared_grads = jnp.concatenate(
        [shared_grads[:, g] for g in range(groups)], axis=2
    ).astype(f32)

    def to_rows(part, dims):
        part = net.scatter_axis(part, "c", dims - 1).astype(bf16)
        part = net.scatter_axis(part, "y", dims - 2).astype(bf16)
        return net.scatter_axis(part, "x", dims - 3)

    grad_out_w = t_mm(mixed, branch_group).astype(bf16)
    grad_output_weight = to_rows(
        grad_out_w.reshape(across, yrows, PAIR, shard, width), 3
    )
    grad_qkv_w = t_mm(normed_attn, grad_qkv).astype(bf16)
    qkv_rows = to_rows(
        grad_qkv_w.reshape(PLANES, across, yrows, PAIR, shard, 3 * head_cols), 4
    ).astype(bf16)
    qkv_got = [
        net.turn(net.pick(qkv_rows, net.ahead("z", s), 0), "z", s)
        if s
        else net.pick(qkv_rows, iz, 0)
        for s in range(PLANES)
    ]
    qkv_planes = net.place_rows(qkv_got, "z", 0)
    grad_qkv_weights = [
        jnp.concatenate(
            [qkv_planes[k, :, j * head_cols : (j + 1) * head_cols] for k in range(PLANES)], axis=1
        ).astype(f32)
        for j in range(3)
    ]

    grad_router = t_mm(normed_mix, grad_logits)
    grad_switch_full = jnp.sum(grad_switch_logit * normed_mix.astype(f32), axis=0)

    def spread_sum(part):
        part = net.scatter_axis(part, "c", 3)
        part = net.scatter_axis(part, "y", 2)
        part = net.scatter_axis(part, "x", 1)
        return net.scatter_axis(part, "z", 0)

    early = jnp.concatenate(
        [grad_router.T, grad_switch_full[None], grad_mixer_gain[None]], axis=0
    )
    early = early.reshape(num_experts + 2, PLANES, across, yrows, PAIR, shard)
    early = spread_sum(jnp.transpose(early, (1, 2, 3, 4, 0, 5)))
    grad_router_shard = early[:num_experts].T
    gain_shard = spread_sum(gain_part.reshape(PLANES, across, yrows, PAIR, 1, shard))[0]
    bias_part = jnp.sum(grad_qkv.astype(f32), axis=0).reshape(3, across, yrows, PAIR, shard)
    bias_part = jnp.transpose(bias_part, (1, 2, 3, 0, 4))
    bias_part = net.scatter_axis(bias_part, "c", 2)
    bias_part = net.scatter_axis(bias_part, "y", 1)
    bias_part = net.scatter_axis(bias_part, "x", 0)
    return (
        layer_out.reshape(1, rows, width),
        balance_loss,
        grad_tokens,
        grad_qkv_weights[0],
        grad_qkv_weights[1],
        grad_qkv_weights[2],
        grad_output_weight,
        bias_part[0],
        bias_part[1],
        bias_part[2],
        gain_shard,
        grad_router_shard,
        early[num_experts],
        early[num_experts + 1],
        shared_grads[0],
        shared_grads[1],
        shared_grads[2],
        grad_expert_gate,
        grad_expert_up,
        grad_expert_down,
    )


def solution(mesh):
    rows = P("expert", "dp", None)
    shard2 = P(("dp", "expert"), None)
    shard1 = P(("dp", "expert"))
    owned = P("expert", "dp", None)
    placed = (
        (rows, rows, P(), rows)
        + (shard2,) * 4
        + (shard1,) * 4
        + (shard2, shard1, shard1)
        + (shard2,) * 3
        + (owned,) * 3
    )
    outs = (
        (rows, P(), rows)
        + (shard2,) * 4
        + (shard1,) * 4
        + (shard2, shard1, shard1)
        + (shard2,) * 3
        + (owned,) * 3
    )
    return jax.shard_map(
        per_device, mesh=mesh, in_specs=placed, out_specs=outs, check_vma=False
    )
```

time: 5240 us -> 1410 us (0.27)
  waiting for transfers between devices: 4520 us -> 518 us
  starting transfers between devices: 18.7 us -> 277 us
  local copies, waits for them, and re-layouts: 63.5 us -> 312 us
  blocking collectives: 220 us -> 0 us
  matrix products: 360 us -> 200 us
    unnamed x25 -> x0, waiting for transfers between devices: 2000 us -> none
    reduce_scatter x9 -> x0, waiting for transfers between devices: 1480 us -> none  [the longest x1 193 us: per_device(): lax.psum_scatter(expert_terms[0].astype(jnp.bfloat16), 'dp', scatter_dime...]
    all_gather x12 -> x0, waiting for transfers between devices: 976 us -> none  [the longest x1 155 us: per_device(): lax.all_gather(expert_down, 'dp', axis=1, tiled=True)]
    ppermute x0 -> x129, waiting for transfers between devices: none -> 518 us  [send(): return lax.ppermute(value, ('dp', 'expert'), pairs)]
    ppermute x0 -> x129, starting transfers between devices: none -> 277 us  [send(): return lax.ppermute(value, ('dp', 'expert'), pairs)]
    dot_general x42 -> x24, matrix products: 359 us -> 193 us  [the longest x19 179 us: mm(): lax.dot_general(left, right, (contract, ((), ())), preferred_element_type...]
    psum x2 -> x0, blocking collectives: 137 us -> none  [per_device(): counts_all, mass_all = lax.psum((counts, mass), ('dp', 'expert'))]
    concatenate x0 -> x17, local copies, waits for them, and re-layouts: none -> 93.1 us  [the longest x2 51.2 us: per_device(): jnp.concatenate([grad_in, expert_grads.astype(bf16), unit_grads[:, local_...]
  transfers between devices with their start and end apart: 27 -> 129, of which waited for: 25 -> 48; matrix products, arithmetic and copies ran while one was open for 7% -> 31% of each run, Pallas kernels for 0% -> 0%
where the time goes in v1:
time: 1410 us; the launch traced here: 1400 us
  waiting for transfers between devices  518 us (37%)
  local copies, waits for them, and re-layouts  312 us (22%)
  starting transfers between devices  277 us (20%)
  matrix products  200 us (14%)
  other arithmetic  87.9 us (6%)
    ppermute x129, waiting for transfers between devices, send(): return lax.ppermute(value, ('dp', 'expert'), pairs)  518 us
    ppermute x129, starting transfers between devices, send(): return lax.ppermute(value, ('dp', 'expert'), pairs)  277 us
    dot_general x19, matrix products, mm(): lax.dot_general(left, right, (contract, ((), ())), preferred_element_type...  179 us
    unnamed x411, local copies, waits for them, and re-layouts  71.8 us
    concatenate x2, local copies, waits for them, and re-layouts, per_device(): jnp.concatenate([grad_in, expert_grads.astype(bf16), unit_grads[:, local_...  51.2 us
    concatenate x4, local copies, waits for them, and re-layouts, gather_group(): return jnp.concatenate([both, other], axis=0).reshape(-1, value.shape[1])  31.5 us
  transfers between devices with their start and end apart: 129, of which 48 were waited for; matrix products, arithmetic and copies ran while one was open for 31% of the time, Pallas kernels for 0%

profile of v1, /device:TPU:0, one launch (start us, length us, event | category | flops | bytes accessed | tf_op | source)
XLA Modules:
  0.0 1400.9 jit_solution(13892905050744076888)
XLA Ops:
  112.8 20.2 %collective-permute-done.1 = bf16[128,2048]{0,1:T(8,128)(2,1)S(1)} collective-permute-done((bf16[128,2048]{0,1:T(8,128)(2,1)S(1)}, bf16[128,2048]{0,1:T(8,128)(2,1)S(1)}, u32[]{:S(2)}, u32[]{:S(2)}) %collective-permute-start.1) | collective-permute-done | bytes 524320 | tf_op jit(solution)/shard_map/ppermute | solution.py:103
  173.9 20.8 %collective-permute-start.42 = (bf16[256,1152]{1,0:T(8,128)(2,1)S(1)}, bf16[256,1152]{1,0:T(8,128)(2,1)S(1)}, u32[]{:S(2)}, u32[]{:S(2)}) collective-permute-start(bf16[256,1152]{1,0:T(8,128)(2,1)S(1)} %pad_maximum_fusion.16), channel_id=1, source_target_pairs={{0,8},{1,9},{2,10},{3,11},{4,12},{5,13},{6,14},{7,15},{8,16},{9,17... | collective-permute-start | bytes 1769480 | tf_op jit(solution)/shard_map/ppermute | solution.py:103
  346.4 15.9 %collective-permute-done.12 = bf16[512,1024]{1,0:T(8,128)(2,1)} collective-permute-done((bf16[512,1024]{1,0:T(8,128)(2,1)}, bf16[512,1024]{1,0:T(8,128)(2,1)}, u32[]{:S(2)}, u32[]{:S(2)}) %collective-permute-start.12) | collective-permute-done | bytes 1048608 | tf_op jit(solution)/shard_map/ppermute | solution.py:103
  393.2 27.6 %collective-permute-start.37 = (bf16[256,1152]{1,0:T(8,128)(2,1)S(1)}, bf16[256,1152]{1,0:T(8,128)(2,1)S(1)}, u32[]{:S(2)}, u32[]{:S(2)}) collective-permute-start(bf16[256,1152]{1,0:T(8,128)(2,1)S(1)} %copy-done.103), channel_id=1, source_target_pairs={{0,16},{1,17},{2,18},{3,19},{4,20},{5,21},{6,22},{7,23},{8,24},{9,... | collective-permute-start | bytes 1769480 | tf_op jit(solution)/shard_map/ppermute | solution.py:103
  420.8 24.0 %collective-permute-done.14 = bf16[128,2048]{0,1:T(8,128)(2,1)S(1)} collective-permute-done((bf16[128,2048]{0,1:T(8,128)(2,1)S(1)}, bf16[128,2048]{0,1:T(8,128)(2,1)S(1)}, u32[]{:S(2)}, u32[]{:S(2)}) %collective-permute-start.14) | collective-permute-done | bytes 524320 | tf_op jit(solution)/shard_map/ppermute | solution.py:103
  627.3 16.0 %fusion.15 = f32[2048,1152]{0,1:T(8,128)} fusion(bf16[2048,1152]{1,0:T(8,128)(2,1)} %bitcast.81, bf16[2048,2176]{1,0:T(8,128)(2,1)} %bitcast.825), kind=kOutput, calls=%fused_computation.34 | convolution fusion | flops 9663676416 | bytes 22544384 | tf_op jit(solution)/shard_map/dot_general | solution.py:22
  643.3 16.6 %fusion.13 = f32[2048,1152]{0,1:T(8,128)} fusion(bf16[2048,1152]{1,0:T(8,128)(2,1)} %bitcast.99, bf16[2048,2176]{1,0:T(8,128)(2,1)} %bitcast.826), kind=kOutput, calls=%fused_computation.32 | convolution fusion | flops 9663676416 | bytes 22544384 | tf_op jit(solution)/shard_map/dot_general | solution.py:22
  659.9 22.9 %multiply_multiply_fusion = (f32[2048,1152]{0,1:T(8,128)}, bf16[2048,1152]{0,1:T(8,128)(2,1)}, bf16[2048,1152]{0,1:T(8,128)(2,1)}, bf16[2048,1152]{0,1:T(8,128)(2,1)}) fusion(f32[1152]{0:T(1024)S(1)} %mul.563, f32[2048,1152]{0,1:T(8,128)} %fusion.13, f32[2048,1152]{0,1:T(8,128)} %fusion.15, f32[2048,3]{0,1:T(4,128)S(1)} %pad_maximum_fusion.25, ...), kind=kOutput, calls=%fused_computation.6 | convolution fusion | flops 9710862336 | bytes 55603712 | tf_op jit(solution)/shard_map/dot_general | solution.py:22
  682.9 17.5 %convolution_convert_fusion.1 = bf16[2048,1152]{1,0:T(8,128)(2,1)} fusion(bf16[2048,1152]{0,1:T(8,128)(2,1)} %get-tuple-element.87, bf16[2048,2176]{1,0:T(8,128)(2,1)} %bitcast.827), kind=kOutput, calls=%fused_computation.16 | convolution fusion | flops 9666035712 | bytes 17825792 | tf_op jit(solution)/shard_map/dot_general | solution.py:22
  700.4 16.1 %fusion.157 = f32[2048,2048]{0,1:T(8,128)} fusion(bf16[2048,1152]{1,0:T(8,128)(2,1)} %bitcast.99, bf16[2048,1152]{0,1:T(8,128)(2,1)S(1)} %copy-done.21), kind=kOutput, calls=%fused_computation.614 | convolution fusion | flops 9663676416 | bytes 26214400 | tf_op jit(solution)/shard_map/dot_general | solution.py:22
  720.8 16.7 %convolution_convert_fusion = bf16[2048,1152]{1,0:T(8,128)(2,1)} fusion(bf16[2048,2048]{1,0:T(8,128)(2,1)} %bitcast.806, bf16[2048,1152]{0,1:T(8,128)(2,1)} %get-tuple-element.86), kind=kOutput, calls=%fused_computation.15 | convolution fusion | flops 9666035712 | bytes 17825792 | tf_op jit(solution)/shard_map/dot_general | solution.py:22
  737.5 16.5 %convolution_convert_fusion.4 = bf16[2048,2048]{1,0:T(8,128)(2,1)} fusion(bf16[2048,1152]{0,1:T(8,128)(2,1)} %get-tuple-element.86, bf16[2048,1152]{1,0:T(8,128)(2,1)} %bitcast.118), kind=kOutput, calls=%fused_computation.19 | convolution fusion | flops 9667870720 | bytes 17825792 | tf_op jit(solution)/shard_map/dot_general | solution.py:22
  771.8 16.7 %add_convert_fusion = bf16[2048,2048]{0,1:T(8,128)(2,1)} fusion(f32[2048,2048]{0,1:T(8,128)} %fusion.157, bf16[2048,1152]{1,0:T(8,128)(2,1)} %bitcast.81, bf16[2048,1152]{0,1:T(8,128)(2,1)S(1)} %bitcast.842), kind=kOutput, calls=%fused_computation.1 | convolution fusion | flops 9672065024 | bytes 34603008 | tf_op jit(solution)/shard_map/dot_general | solution.py:22
  788.6 39.4 %concatenate.251 = bf16[2048,2176]{0,1:T(8,128)(2,1)} concatenate(bf16[2048,2048]{0,1:T(8,128)(2,1)} %add_convert_fusion, bf16[2048,8]{0,1:T(8,128)(2,1)S(1)} %multiply_reduce_fusion.5, bf16[2048,1]{0,1:T(2,128)(2,1)S(1)} %slice.981, bf16[2048,119]{0,1:T(8,128)(2,1)S(1)} %broadcast_in_dim.357), dimensions={1} | concatenate | bytes 17825792 | tf_op jit(solution)/shard_map/concatenate | solution.py:458
  900.6 20.9 %collective-permute-done.73 = bf16[128,2176]{0,1:T(8,128)(2,1)S(1)} collective-permute-done((bf16[128,2176]{0,1:T(8,128)(2,1)S(1)}, bf16[128,2176]{0,1:T(8,128)(2,1)S(1)}, u32[]{:S(2)}, u32[]{:S(2)}) %collective-permute-start.73) | collective-permute-done | bytes 557088 | tf_op jit(solution)/shard_map/ppermute | solution.py:103
  948.7 23.2 %collective-permute-done.77 = bf16[128,2176]{0,1:T(8,128)(2,1)S(1)} collective-permute-done((bf16[128,2176]{0,1:T(8,128)(2,1)S(1)}, bf16[128,2176]{0,1:T(8,128)(2,1)S(1)}, u32[]{:S(2)}, u32[]{:S(2)}) %collective-permute-start.77) | collective-permute-done | bytes 557088 | tf_op jit(solution)/shard_map/ppermute | solution.py:103
  983.0 14.3 %collective-permute-done.109 = f32[4,2,10,64]{3,1,0,2:T(2,128)S(1)} collective-permute-done((f32[4,2,10,64]{3,1,0,2:T(2,128)S(1)}, f32[4,2,10,64]{3,1,0,2:T(2,128)S(1)}, u32[]{:S(2)}, u32[]{:S(2)}) %collective-permute-start.109) | collective-permute-done | bytes 20512 | tf_op jit(solution)/shard_map/ppermute | solution.py:103
  1009.1 24.0 %collective-permute-done.53 = bf16[128,2048]{0,1:T(8,128)(2,1)S(1)} collective-permute-done((bf16[128,2048]{0,1:T(8,128)(2,1)S(1)}, bf16[128,2048]{0,1:T(8,128)(2,1)S(1)}, u32[]{:S(2)}, u32[]{:S(2)}) %collective-permute-start.53) | collective-permute-done | bytes 524320 | tf_op jit(solution)/shard_map/ppermute | solution.py:103
  1062.5 41.2 %collective-permute-done.114 = bf16[4,256,1152]{2,1,0:T(8,128)(2,1)} collective-permute-done((bf16[4,256,1152]{2,1,0:T(8,128)(2,1)}, bf16[4,256,1152]{2,1,0:T(8,128)(2,1)}, u32[]{:S(2)}, u32[]{:S(2)}) %collective-permute-start.114) | collective-permute-done | bytes 2359328 | tf_op jit(solution)/shard_map/ppermute | solution.py:103
  1151.8 20.8 %collective-permute-start.116 = (bf16[256,1152]{1,0:T(8,128)(2,1)S(1)}, bf16[256,1152]{1,0:T(8,128)(2,1)S(1)}, u32[]{:S(2)}, u32[]{:S(2)}) collective-permute-start(bf16[256,1152]{1,0:T(8,128)(2,1)S(1)} %copy-done.100), channel_id=1, source_target_pairs={{0,16},{1,17},{2,18},{3,19},{4,20},{5,21},{6,22},{7,23},{8,24},{9,... | collective-permute-start | bytes 1769480 | tf_op jit(solution)/shard_map/ppermute | solution.py:103
  1173.8 17.6 %collective-permute-start.117 = (bf16[256,1152]{1,0:T(8,128)(2,1)S(1)}, bf16[256,1152]{1,0:T(8,128)(2,1)S(1)}, u32[]{:S(2)}, u32[]{:S(2)}) collective-permute-start(bf16[256,1152]{1,0:T(8,128)(2,1)S(1)} %copy-done.99), channel_id=1, source_target_pairs={{0,24},{1,25},{2,26},{3,27},{4,28},{5,29},{6,30},{7,31},{8,0},{9,1... | collective-permute-start | bytes 1769480 | tf_op jit(solution)/shard_map/ppermute | solution.py:103
  1192.6 13.8 collective-permute-done.120
  1209.1 22.4 %collective-permute-done.116 = bf16[256,1152]{1,0:T(8,128)(2,1)S(1)} collective-permute-done((bf16[256,1152]{1,0:T(8,128)(2,1)S(1)}, bf16[256,1152]{1,0:T(8,128)(2,1)S(1)}, u32[]{:S(2)}, u32[]{:S(2)}) %collective-permute-start.116) | collective-permute-done | bytes 589856 | tf_op jit(solution)/shard_map/ppermute | solution.py:103
  1349.7 25.4 %collective-permute-done.88 = bf16[128,2048]{0,1:T(8,128)(2,1)S(1)} collective-permute-done((bf16[128,2048]{0,1:T(8,128)(2,1)S(1)}, bf16[128,2048]{0,1:T(8,128)(2,1)S(1)}, u32[]{:S(2)}, u32[]{:S(2)}) %collective-permute-start.88) | collective-permute-done | bytes 524320 | tf_op jit(solution)/shard_map/ppermute | solution.py:103
  (1013 shorter events, 883.6 us)
Async XLA Ops:
  2.1 99.8 %collective-permute-start.64 = (bf16[128,2048]{0,1:T(8,128)(2,1)S(1)}, bf16[128,2048]{0,1:T(8,128)(2,1)}, u32[]{:S(2)}, u32[]{:S(2)}) collective-permute-start(bf16[128,2048]{0,1:T(8,128)(2,1)S(1)} %bitcast.833), channel_id=1, source_target_pairs={{0,2},{1,3},{2,0},{3,1},{4,6},{5,7},{6,4},{7,5},{8,10},{9,11},{10,... | collective-permute-start | bytes 1572872 | tf_op jit(solution)/shard_map/ppermute | solution.py:103
  5.1 98.8 %collective-permute-start.65 = (bf16[128,2048]{0,1:T(8,128)(2,1)S(1)}, bf16[128,2048]{0,1:T(8,128)(2,1)}, u32[]{:S(2)}, u32[]{:S(2)}) collective-permute-start(bf16[128,2048]{0,1:T(8,128)(2,1)S(1)} %bitcast.834), channel_id=1, source_target_pairs={{0,8},{1,9},{2,10},{3,11},{4,12},{5,13},{6,14},{7,15},{8,16},{9,17... | collective-permute-start | bytes 1572872 | tf_op jit(solution)/shard_map/ppermute | solution.py:103
  6.7 141.0 %collective-permute-start.67 = (bf16[128,2048]{0,1:T(8,128)(2,1)S(1)}, bf16[128,2048]{0,1:T(8,128)(2,1)}, u32[]{:S(2)}, u32[]{:S(2)}) collective-permute-start(bf16[128,2048]{0,1:T(8,128)(2,1)S(1)} %bitcast.835), channel_id=1, source_target_pairs={{0,16},{1,17},{2,18},{3,19},{4,20},{5,21},{6,22},{7,23},{8,24},{9,... | collective-permute-start | bytes 1572872 | tf_op jit(solution)/shard_map/ppermute | solution.py:103
  13.4 82.4 %collective-permute-start.9 = (bf16[64,2176]{1,0:T(8,128)(2,1)}, bf16[64,2176]{1,0:T(8,128)(2,1)}, u32[]{:S(2)}, u32[]{:S(2)}) collective-permute-start(bf16[64,2176]{1,0:T(8,128)(2,1)} %concatenate.224), channel_id=1, source_target_pairs={{0,4},{1,5},{2,6},{3,7},{4,0},{5,1},{6,2},{7,3},{8,12},{9,13},{10,... | collective-permute-start | bytes 835592 | tf_op jit(solution)/shard_map/ppermute | solution.py:103
  135.5 80.0 %collective-permute-start.6 = (bf16[4,64,1664]{2,1,0:T(8,128)(2,1)S(1)}, bf16[4,64,1664]{2,1,0:T(8,128)(2,1)S(1)}, u32[]{:S(2)}, u32[]{:S(2)}) collective-permute-start(bf16[4,64,1664]{2,1,0:T(8,128)(2,1)S(1)} %bitcast_dynamic-update-slice_fusion.81), channel_id=1, source_target_pairs={{0,4},{1,5},{2,6},{3,7},{4,0},{5,1},{6,2},{7,3},{8,12},{9,13},{10,... | collective-permute-start | bytes 2555912 | tf_op jit(solution)/shard_map/ppermute | solution.py:103
  197.6 79.6 %collective-permute-start.44 = (bf16[256,1152]{1,0:T(8,128)(2,1)S(1)}, bf16[256,1152]{1,0:T(8,128)(2,1)S(1)}, u32[]{:S(2)}, u32[]{:S(2)}) collective-permute-start(bf16[256,1152]{1,0:T(8,128)(2,1)S(1)} %pad_maximum_fusion.17), channel_id=1, source_target_pairs={{0,16},{1,17},{2,18},{3,19},{4,20},{5,21},{6,22},{7,23},{8,24},{9,... | collective-permute-start | bytes 1769480 | tf_op jit(solution)/shard_map/ppermute | solution.py:103
  209.1 92.8 %collective-permute-start.46 = (bf16[256,1152]{1,0:T(8,128)(2,1)S(1)}, bf16[256,1152]{1,0:T(8,128)(2,1)S(1)}, u32[]{:S(2)}, u32[]{:S(2)}) collective-permute-start(bf16[256,1152]{1,0:T(8,128)(2,1)S(1)} %pad_maximum_fusion.18), channel_id=1, source_target_pairs={{0,24},{1,25},{2,26},{3,27},{4,28},{5,29},{6,30},{7,31},{8,0},{9,1... | collective-permute-start | bytes 1769480 | tf_op jit(solution)/shard_map/ppermute | solution.py:103
  261.1 81.4 %collective-permute-start.30 = (bf16[256,1152]{1,0:T(8,128)(2,1)}, bf16[256,1152]{1,0:T(8,128)(2,1)S(1)}, u32[]{:S(2)}, u32[]{:S(2)}) collective-permute-start(bf16[256,1152]{1,0:T(8,128)(2,1)} %pad_maximum_fusion.9), channel_id=1, source_target_pairs={{0,16},{1,17},{2,18},{3,19},{4,20},{5,21},{6,22},{7,23},{8,24},{9,... | collective-permute-start | bytes 1769480 | tf_op jit(solution)/shard_map/ppermute | solution.py:103
  300.0 232.0 %collective-permute-start.32 = (bf16[256,1152]{1,0:T(8,128)(2,1)}, bf16[256,1152]{1,0:T(8,128)(2,1)}, u32[]{:S(2)}, u32[]{:S(2)}) collective-permute-start(bf16[256,1152]{1,0:T(8,128)(2,1)} %pad_maximum_fusion.10), channel_id=1, source_target_pairs={{0,24},{1,25},{2,26},{3,27},{4,28},{5,29},{6,30},{7,31},{8,0},{9,1... | collective-permute-start | bytes 1769480 | tf_op jit(solution)/shard_map/ppermute | solution.py:103
  301.9 232.0 %collective-permute-start.39 = (bf16[256,1152]{1,0:T(8,128)(2,1)}, bf16[256,1152]{1,0:T(8,128)(2,1)}, u32[]{:S(2)}, u32[]{:S(2)}) collective-permute-start(bf16[256,1152]{1,0:T(8,128)(2,1)} %pad_maximum_fusion.14), channel_id=1, source_target_pairs={{0,24},{1,25},{2,26},{3,27},{4,28},{5,29},{6,30},{7,31},{8,0},{9,1... | collective-permute-start | bytes 1769480 | tf_op jit(solution)/shard_map/ppermute | solution.py:103
  380.8 64.0 %collective-permute-start.14 = (bf16[128,2048]{0,1:T(8,128)(2,1)S(1)}, bf16[128,2048]{0,1:T(8,128)(2,1)S(1)}, u32[]{:S(2)}, u32[]{:S(2)}) collective-permute-start(bf16[128,2048]{0,1:T(8,128)(2,1)S(1)} %get-tuple-element.179), channel_id=1, source_target_pairs={{0,16},{1,17},{2,18},{3,19},{4,20},{5,21},{6,22},{7,23},{8,24},{9,... | collective-permute-start | bytes 1572872 | tf_op jit(solution)/shard_map/ppermute | solution.py:103
  393.2 125.5 %collective-permute-start.37 = (bf16[256,1152]{1,0:T(8,128)(2,1)S(1)}, bf16[256,1152]{1,0:T(8,128)(2,1)S(1)}, u32[]{:S(2)}, u32[]{:S(2)}) collective-permute-start(bf16[256,1152]{1,0:T(8,128)(2,1)S(1)} %copy-done.103), channel_id=1, source_target_pairs={{0,16},{1,17},{2,18},{3,19},{4,20},{5,21},{6,22},{7,23},{8,24},{9,... | collective-permute-start | bytes 1769480 | tf_op jit(solution)/shard_map/ppermute | solution.py:103
  496.5 85.7 %collective-permute-start.71 = (bf16[8,128,2048]{1,2,0:T(8,128)(2,1)S(1)}, bf16[8,128,2048]{1,2,0:T(8,128)(2,1)S(1)}, u32[]{:S(2)}, u32[]{:S(2)}) collective-permute-start(bf16[8,128,2048]{1,2,0:T(8,128)(2,1)S(1)} %copy-done.140), channel_id=1, source_target_pairs={{0,1},{1,0},{2,3},{3,2},{4,5},{5,4},{6,7},{7,6},{8,9},{9,8},{10,11... | collective-permute-start | bytes 12582920 | tf_op jit(solution)/shard_map/ppermute | solution.py:103
  518.7 89.2 %collective-permute-start.23 = (bf16[8,128,2176]{1,2,0:T(8,128)(2,1)}, bf16[8,128,2176]{1,2,0:T(8,128)(2,1)}, u32[]{:S(2)}, u32[]{:S(2)}) collective-permute-start(bf16[8,128,2176]{1,2,0:T(8,128)(2,1)} %get-tuple-element.262), channel_id=1, source_target_pairs={{0,1},{1,0},{2,3},{3,2},{4,5},{5,4},{6,7},{7,6},{8,9},{9,8},{10,11... | collective-permute-start | bytes 13369352 | tf_op jit(solution)/shard_map/ppermute | solution.py:103
  757.3 285.9 %collective-permute-start.122 = (bf16[4,256,1152]{2,1,0:T(8,128)(2,1)}, bf16[4,256,1152]{2,1,0:T(8,128)(2,1)}, u32[]{:S(2)}, u32[]{:S(2)}) collective-permute-start(bf16[4,256,1152]{2,1,0:T(8,128)(2,1)} %dynamic-slice_bitcast_fusion), channel_id=1, source_target_pairs={{0,4},{1,5},{2,6},{3,7},{4,0},{5,1},{6,2},{7,3},{8,12},{9,13},{10,... | collective-permute-start | bytes 7077896 | tf_op jit(solution)/shard_map/ppermute | solution.py:103
  1033.1 70.5 %collective-permute-start.114 = (bf16[4,256,1152]{2,1,0:T(8,128)(2,1)}, bf16[4,256,1152]{2,1,0:T(8,128)(2,1)}, u32[]{:S(2)}, u32[]{:S(2)}) collective-permute-start(bf16[4,256,1152]{2,1,0:T(8,128)(2,1)} %dynamic-slice_bitcast_fusion.2), channel_id=1, source_target_pairs={{0,4},{1,5},{2,6},{3,7},{4,0},{5,1},{6,2},{7,3},{8,12},{9,13},{10,... | collective-permute-start | bytes 7077896 | tf_op jit(solution)/shard_map/ppermute | solution.py:103
  1038.5 72.9 %collective-permute-start.83 = (bf16[128,2048]{0,1:T(8,128)(2,1)S(1)}, bf16[128,2048]{0,1:T(8,128)(2,1)S(1)}, u32[]{:S(2)}, u32[]{:S(2)}) collective-permute-start(bf16[128,2048]{0,1:T(8,128)(2,1)S(1)} %get-tuple-element.188), channel_id=1, source_target_pairs={{0,8},{1,9},{2,10},{3,11},{4,12},{5,13},{6,14},{7,15},{8,16},{9,17... | collective-permute-start | bytes 1572872 | tf_op jit(solution)/shard_map/ppermute | solution.py:103
  1039.2 74.7 %collective-permute-start.84 = (bf16[128,2048]{0,1:T(8,128)(2,1)S(1)}, bf16[128,2048]{0,1:T(8,128)(2,1)S(1)}, u32[]{:S(2)}, u32[]{:S(2)}) collective-permute-start(bf16[128,2048]{0,1:T(8,128)(2,1)S(1)} %get-tuple-element.188), channel_id=1, source_target_pairs={{0,16},{1,17},{2,18},{3,19},{4,20},{5,21},{6,22},{7,23},{8,24},{9,... | collective-permute-start | bytes 1572872 | tf_op jit(solution)/shard_map/ppermute | solution.py:103
  1043.2 70.7 %collective-permute-start.85 = (bf16[128,2048]{0,1:T(8,128)(2,1)S(1)}, bf16[128,2048]{0,1:T(8,128)(2,1)S(1)}, u32[]{:S(2)}, u32[]{:S(2)}) collective-permute-start(bf16[128,2048]{0,1:T(8,128)(2,1)S(1)} %get-tuple-element.188), channel_id=1, source_target_pairs={{0,24},{1,25},{2,26},{3,27},{4,28},{5,29},{6,30},{7,31},{8,0},{9,1... | collective-permute-start | bytes 1572872 | tf_op jit(solution)/shard_map/ppermute | solution.py:103
  1057.5 82.0 %collective-permute-start.123 = (bf16[256,1152]{1,0:T(8,128)(2,1)}, bf16[256,1152]{1,0:T(8,128)(2,1)}, u32[]{:S(2)}, u32[]{:S(2)}) collective-permute-start(bf16[256,1152]{1,0:T(8,128)(2,1)} %get-tuple-element.159), channel_id=1, source_target_pairs={{0,8},{1,9},{2,10},{3,11},{4,12},{5,13},{6,14},{7,15},{8,16},{9,17... | collective-permute-start | bytes 1769480 | tf_op jit(solution)/shard_map/ppermute | solution.py:103
  1114.0 92.3 %collective-permute-start.120 = (bf16[256,1152]{1,0:T(8,128)(2,1)}, bf16[256,1152]{1,0:T(8,128)(2,1)}, u32[]{:S(2)}, u32[]{:S(2)}) collective-permute-start(bf16[256,1152]{1,0:T(8,128)(2,1)} %get-tuple-element.154), channel_id=1, source_target_pairs={{0,16},{1,17},{2,18},{3,19},{4,20},{5,21},{6,22},{7,23},{8,24},{9,... | collective-permute-start | bytes 1769480 | tf_op jit(solution)/shard_map/ppermute | solution.py:103
  1139.5 68.8 %collective-permute-start.121 = (bf16[256,1152]{1,0:T(8,128)(2,1)S(1)}, bf16[256,1152]{1,0:T(8,128)(2,1)S(1)}, u32[]{:S(2)}, u32[]{:S(2)}) collective-permute-start(bf16[256,1152]{1,0:T(8,128)(2,1)S(1)} %copy-done.102), channel_id=1, source_target_pairs={{0,24},{1,25},{2,26},{3,27},{4,28},{5,29},{6,30},{7,31},{8,0},{9,1... | collective-permute-start | bytes 1769480 | tf_op jit(solution)/shard_map/ppermute | solution.py:103
  1151.8 79.7 %collective-permute-start.116 = (bf16[256,1152]{1,0:T(8,128)(2,1)S(1)}, bf16[256,1152]{1,0:T(8,128)(2,1)S(1)}, u32[]{:S(2)}, u32[]{:S(2)}) collective-permute-start(bf16[256,1152]{1,0:T(8,128)(2,1)S(1)} %copy-done.100), channel_id=1, source_target_pairs={{0,16},{1,17},{2,18},{3,19},{4,20},{5,21},{6,22},{7,23},{8,24},{9,... | collective-permute-start | bytes 1769480 | tf_op jit(solution)/shard_map/ppermute | solution.py:103
  1208.3 82.6 %collective-permute-start.96 = (bf16[2,2,64,2048]{3,2,0,1:T(8,128)(2,1)}, bf16[2,2,64,2048]{3,2,0,1:T(8,128)(2,1)}, u32[]{:S(2)}, u32[]{:S(2)}) collective-permute-start(bf16[2,2,64,2048]{3,2,0,1:T(8,128)(2,1)} %bitcast.789), channel_id=1, source_target_pairs={{0,1},{1,0},{2,3},{3,2},{4,5},{5,4},{6,7},{7,6},{8,9},{9,8},{10,11... | collective-permute-start | bytes 3145736 | tf_op jit(solution)/shard_map/ppermute | solution.py:103
  (287 other events, 7713.3 us)

commit v2 on v1

v2 whole, which is shorter than its diff:
```python
import jax
import jax.numpy as jnp
from jax import lax
from jax.experimental import pallas as pl
from jax.experimental.pallas import tpu as pltpu
from jax.sharding import Mesh
from jax.sharding import PartitionSpec as P

HEADS = 16
HD = 128
LANES = 128
PLANES = 4
PAIR = 2
TILE = 256
VMEM_BYTES = 56 * 2**20
ALL = ("z", "x", "y", "c")
GROUP = ("z", "y", "c")

f32 = jnp.float32
bf16 = jnp.bfloat16

epsilon = 1e-06
rope_base = 1000000.0
highest = lax.Precision.HIGHEST
neg_large = -1e30


def mm(left, right, contract=((1,), (0,))):
    return lax.dot_general(left, right, (contract, ((), ())), preferred_element_type=f32)


def mm_t(left, right):
    return mm(left, right, ((1,), (1,)))


def t_mm(left, right):
    return mm(left, right, ((0,), (0,)))


def rope_tables(positions, head_width):
    halfway = head_width // 2
    freqs = rope_base ** (-jnp.arange(halfway, dtype=f32) * 2.0 / head_width)
    angles = positions.astype(f32)[:, None] * freqs[None, :]
    angles = jnp.concatenate([angles, angles], axis=1)
    return (jnp.cos(angles), jnp.sin(angles))


def rotate(values, cosine, sine):
    halfway = values.shape[-1] // 2
    turned = jnp.concatenate([-values[..., halfway:], values[..., :halfway]], axis=-1)
    return values * cosine[:, None, :] + turned * sine[:, None, :]


def rotate_back(grads_in, cosine, sine):
    halfway = grads_in.shape[-1] // 2
    scaled = grads_in * sine[:, None, :]
    turned = jnp.concatenate([scaled[..., halfway:], -scaled[..., :halfway]], axis=-1)
    return grads_in * cosine[:, None, :] + turned


def norm_back(grad_normed, rows_in, inverse, gain):
    weighted = grad_normed * gain
    inner = jnp.sum(weighted * rows_in, axis=-1, keepdims=True)
    grad_rows = inverse * weighted - rows_in * inverse**3 * inner / rows_in.shape[-1]
    grad_gain = jnp.sum(grad_normed * rows_in * inverse, axis=0)
    return (grad_rows, grad_gain)


def add_low(*parts):
    total = parts[0].astype(f32)
    for part in parts[1:]:
        total = total + part.astype(f32)
    return total.astype(bf16)


class Links:
    def __init__(self):
        self.sizes = {axis: lax.axis_size(axis) for axis in ALL}
        self.at = {axis: lax.axis_index(axis) for axis in ALL}
        self.across = self.sizes["x"]
        self.rows = self.sizes["y"]

    def turn(self, value, axis, steps):
        size = self.sizes[axis]
        return lax.ppermute(value, axis, [(i, (i + steps) % size) for i in range(size)])

    def line(self, value, *pairs):
        return lax.ppermute(value, "z", pairs)

    def behind(self, axis, steps):
        return (self.at[axis] - steps) % self.sizes[axis]

    def ahead(self, axis, steps):
        return (self.at[axis] + steps) % self.sizes[axis]

    def planes_held(self):
        return self.behind("z", jnp.arange(PLANES))

    def gather_z(self, value):
        return [value] + [self.turn(value, "z", k) for k in range(1, PLANES)]

    def scatter_z(self, *blocks):
        return [blocks[0]] + [self.turn(blocks[k], "z", -k) for k in range(1, PLANES)]

    def gather_x(self, value):
        return [value] + [self.turn(value, "x", t) for t in range(1, self.across)]

    def exchange_z(self, value):
        return lax.all_to_all(value, "z", split_axis=0, concat_axis=0, tiled=True)

    def place_rows(self, blocks, axis, dim):
        shape = blocks[0].shape[:dim] + (self.sizes[axis],) + blocks[0].shape[dim:]
        buffer = jnp.zeros(shape, blocks[0].dtype)
        for s, block in enumerate(blocks):
            buffer = lax.dynamic_update_slice_in_dim(
                buffer, jnp.expand_dims(block, dim), self.behind(axis, s), dim
            )
        return buffer

    def pick(self, value, index, dim):
        return lax.dynamic_index_in_dim(value, index, dim, keepdims=False)

    def scatter_axis(self, value, axis, dim):
        total = self.pick(value, self.at[axis], dim).astype(f32)
        for s in range(1, self.sizes[axis]):
            total = total + self.turn(
                self.pick(value, self.ahead(axis, s), dim), axis, s
            ).astype(f32)
        return total

    def exchange_group(self, value):
        return lax.all_to_all(value, GROUP, split_axis=0, concat_axis=0, tiled=True)


def after(value, *others):
    return lax.optimization_barrier((value,) + others)[0]


def weight_copies(places_ref, pieces, targets, sems):
    made = []
    across = len(pieces[0])
    for per_weight, target in zip(pieces, targets):
        cols = target.shape[1]
        for t, (source, first) in enumerate(per_weight):
            planes, block = source.shape[:2]
            for z in range(planes):
                row = pl.multiple_of((z * across + places_ref[t]) * block, block)
                view = source.at[z] if first is None else source.at[z, :, pl.ds(first, cols)]
                made.append(
                    pltpu.make_async_copy(
                        view, target.at[pl.ds(row, block)], sems.at[len(made)]
                    )
                )
    return made


def load_weights(places_ref, pieces, targets, sems):
    @pl.when(pl.program_id(0) == 0)
    def _():
        for copy in weight_copies(places_ref, pieces, targets, sems):
            copy.start()
        for copy in weight_copies(places_ref, pieces, targets, sems):
            copy.wait()


def expert_kernel(stacked, carried, across, places_ref, rows_ref, cot_ref, widen_ref, fold_ref, *refs):
    if carried:
        carry_ref, refs = refs[0], refs[1:]
    count = across if stacked else 3 * across
    sources = refs[:count]
    back_ref, hidden_ref, grad_gate_ref, grad_up_ref = refs[count : count + 4]
    gate_w, up_w, down_w, sems = refs[count + 4 :]
    width = cot_ref.shape[1]
    wide = gate_w.shape[1]
    if stacked:
        pieces = [[(source, k * wide) for source in sources] for k in range(3)]
    else:
        pieces = [
            [(source, None) for source in sources[k * across : (k + 1) * across]]
            for k in range(3)
        ]
    load_weights(places_ref, pieces, (gate_w, up_w, down_w), sems)

    payload = rows_ref[...]
    rows = payload[:, :width]
    wide_gate = mm(payload[:, width:], widen_ref[...])
    gate = mm(rows, gate_w[...])
    up = mm(rows, up_w[...])
    grad_hidden = mm(cot_ref[...], down_w[...])
    sigma = 1.0 / (1.0 + jnp.exp(-gate))
    act = gate * sigma
    hidden = act * up
    hidden_ref[...] = (hidden * wide_gate).astype(bf16)
    tail = mm((hidden * grad_hidden).astype(bf16), fold_ref[...])
    grad_hidden = grad_hidden * wide_gate
    grad_gate = (grad_hidden * up * (sigma * (1.0 + gate * (1.0 - sigma)))).astype(bf16)
    grad_up = (grad_hidden * act).astype(bf16)
    grad_gate_ref[...] = grad_gate
    grad_up_ref[...] = grad_up
    back = mm_t(grad_gate, gate_w[...]) + mm_t(grad_up, up_w[...])
    if carried:
        back = back + carry_ref[:, :width].astype(f32)
        tail = tail + carry_ref[:, width:].astype(f32)
    back_ref[:, :width] = back.astype(bf16)
    back_ref[:, width:] = tail.astype(bf16)


def run_experts(places, rows, cot, widen, fold, weights, carry=None):
    stacked = len(weights) == 1
    across = len(weights[0])
    flat = [piece for per_weight in weights for piece in per_weight]
    planes = flat[0].shape[0]
    wide = widen.shape[1]
    count, width = cot.shape
    full = rows.shape[1]
    carries = [] if carry is None else [carry]

    def row_block(cols):
        return pl.BlockSpec((TILE, cols), lambda i, p: (i, 0))

    def whole(a):
        return pl.BlockSpec(a.shape, lambda i, p: (0, 0))

    return pl.pallas_call(
        lambda *refs: expert_kernel(stacked, bool(carries), across, *refs),
        grid_spec=pltpu.PrefetchScalarGridSpec(
            num_scalar_prefetch=1,
            grid=(count // TILE,),
            in_specs=[row_block(full), row_block(width), whole(widen), whole(fold)]
            + [row_block(full)] * len(carries)
            + [pl.BlockSpec(memory_space=pl.ANY)] * len(flat),
            out_specs=[row_block(full)] + [row_block(wide)] * 3,
            scratch_shapes=[pltpu.VMEM((width, wide), bf16)] * 3
            + [pltpu.SemaphoreType.DMA((3 * across * planes,))],
        ),
        out_shape=[jax.ShapeDtypeStruct((count, full), bf16)]
        + [jax.ShapeDtypeStruct((count, wide), bf16)] * 3,
        compiler_params=pltpu.CompilerParams(
            vmem_limit_bytes=VMEM_BYTES, dimension_semantics=("arbitrary",)
        ),
        cost_estimate=pl.CostEstimate(
            flops=2 * count * width * wide * 5,
            bytes_accessed=3 * width * wide * 2 + count * (2 * full + width + 3 * wide) * 2,
            transcendentals=count * wide,
        ),
    )(places, rows, cot, widen, fold, *carries, *flat)


def output_kernel(across, places_ref, order_ref, first_ref, second_ref, *refs):
    firsts, seconds = refs[:across], refs[across : 2 * across]
    out_ref, first_w, second_w, sems = refs[2 * across :]
    extra = second_w.shape[1]
    pieces = [[(r, None) for r in firsts], [(r, 2 * extra) for r in seconds]]
    load_weights(places_ref, pieces, (first_w, second_w), sems)
    out_ref[0] = (mm_t(first_ref[...], first_w[...]) + mm_t(second_ref[...], second_w[...])).astype(bf16)


def run_output(places, order, size, first, second, first_w, second_w):
    across = len(first_w)
    planes, block, cols = first_w[0].shape
    width = planes * across * block
    extra = second.shape[1]
    count = first.shape[0]

    def row_block(a):
        return pl.BlockSpec((size, a.shape[1]), lambda i, p, o: (i, 0))

    return pl.pallas_call(
        lambda *refs: output_kernel(across, *refs),
        grid_spec=pltpu.PrefetchScalarGridSpec(
            num_scalar_prefetch=2,
            grid=(count // size,),
            in_specs=[row_block(first), row_block(second)]
            + [pl.BlockSpec(memory_space=pl.ANY)] * (2 * across),
            out_specs=pl.BlockSpec((1, size, width), lambda i, p, o: (o[i], 0, 0)),
            scratch_shapes=[
                pltpu.VMEM((width, cols), bf16),
                pltpu.VMEM((width, extra), bf16),
                pltpu.SemaphoreType.DMA((2 * across * planes,)),
            ],
        ),
        out_shape=jax.ShapeDtypeStruct((count // size, size, width), bf16),
        compiler_params=pltpu.CompilerParams(
            vmem_limit_bytes=VMEM_BYTES, dimension_semantics=("arbitrary",)
        ),
        cost_estimate=pl.CostEstimate(
            flops=2 * count * width * (cols + extra),
            bytes_accessed=2 * (width + count) * (cols + extra) + 2 * count * width,
            transcendentals=0,
        ),
    )(places, order, first, second, *first_w, *second_w)


def copy_kernel(order_ref, source_ref, target_ref):
    target_ref[...] = source_ref[0]


def take_blocks(blocks, order):
    count, size, width = blocks.shape
    return pl.pallas_call(
        copy_kernel,
        grid_spec=pltpu.PrefetchScalarGridSpec(
            num_scalar_prefetch=1,
            grid=(count,),
            in_specs=[pl.BlockSpec((1, size, width), lambda i, o: (o[i], 0, 0))],
            out_specs=pl.BlockSpec((size, width), lambda i, o: (i, 0)),
        ),
        out_shape=jax.ShapeDtypeStruct((count * size, width), blocks.dtype),
        cost_estimate=pl.CostEstimate(
            flops=0, bytes_accessed=4 * blocks.size, transcendentals=0
        ),
    )(order, blocks)


def term_kernel(groups, *refs):
    out_ref = refs[-1]
    side, block, cols = out_ref.shape[0], out_ref.shape[2], 0
    for pairs in groups:
        total = None
        for left, right in pairs:
            part = t_mm(refs[left][...], refs[right][...])
            total = part if total is None else total + part
        wide = total.shape[1]
        out_ref[:, 0, :, cols : cols + wide] = total.astype(bf16).reshape(side, block, wide)
        cols += wide


def run_terms(groups, width, planes, across):
    block = width // (planes * across)
    side = max(1, LANES // block)
    arrays, numbers = [], []

    def number(a):
        for k, b in enumerate(arrays):
            if a is b:
                return k
        arrays.append(a)
        return len(arrays) - 1

    lefts = set()
    for pairs in groups:
        for left, right in pairs:
            lefts.add(number(left))
    numbers = [[(number(left), number(right)) for left, right in pairs] for pairs in groups]
    wide = sum(pairs[0][1].shape[1] for pairs in groups)
    steps = planes * across // side
    per_plane = across // side

    def spec(k, a):
        if k in lefts:
            return pl.BlockSpec((a.shape[0], side * block), lambda i: (0, i))
        return pl.BlockSpec(a.shape, lambda i: (0, 0))

    flops = sum(2 * l.shape[0] * width * r.shape[1] for pairs in groups for l, r in pairs)
    return pl.pallas_call(
        lambda *refs: term_kernel(numbers, *refs),
        grid=(steps,),
        in_specs=[spec(k, a) for k, a in enumerate(arrays)],
        out_specs=pl.BlockSpec(
            (side, 1, block, wide), lambda i: (i % per_plane, i // per_plane, 0, 0)
        ),
        out_shape=jax.ShapeDtypeStruct((across, planes, block, wide), bf16),
        compiler_params=pltpu.CompilerParams(
            vmem_limit_bytes=VMEM_BYTES, dimension_semantics=("arbitrary",)
        ),
        cost_estimate=pl.CostEstimate(
            flops=flops,
            bytes_accessed=sum(a.size * 2 for a in arrays) + width * wide * 2,
            transcendentals=0,
        ),
    )(*arrays)


def cut_kernel(plans, window, *refs):
    out_ref = refs[-1]
    for k, plan in enumerate(plans):

        @pl.when(pl.program_id(0) == k)
        def _(plan=plan):
            for j, (source, lead, start) in enumerate(plan):
                ref = refs[source]
                cols = slice(start, start + window)
                block = ref[:, cols] if lead is None else ref[lead, :, cols]
                out_ref[0, :, j * window : (j + 1) * window] = block


def cut_columns(arrays, plans, window):
    rows = arrays[0].shape[-2]
    wide = len(plans[0]) * window

    def whole(a):
        return pl.BlockSpec(a.shape, lambda i, n=a.ndim: (0,) * n)

    return pl.pallas_call(
        lambda *refs: cut_kernel(plans, window, *refs),
        grid=(len(plans),),
        in_specs=[whole(a) for a in arrays],
        out_specs=pl.BlockSpec((1, rows, wide), lambda i: (i, 0, 0)),
        out_shape=jax.ShapeDtypeStruct((len(plans), rows, wide), bf16),
        compiler_params=pltpu.CompilerParams(dimension_semantics=("arbitrary",)),
        cost_estimate=pl.CostEstimate(
            flops=0,
            bytes_accessed=2 * (sum(a.size for a in arrays) + len(plans) * rows * wide),
            transcendentals=0,
        ),
    )(*arrays)


def per_device(
    tokens,
    cotangent,
    lengths,
    routes,
    query_weight,
    key_weight,
    value_weight,
    output_weight,
    query_bias,
    key_bias,
    value_bias,
    attention_gain,
    router_weight,
    shared_switch,
    mixer_gain,
    shared_gate_weight,
    shared_up_weight,
    shared_down_weight,
    expert_gate,
    expert_up,
    expert_down,
):
    net = Links()
    across, yrows = net.across, net.rows
    dp_size = PLANES * across
    groups = yrows * PAIR
    rows = tokens.shape[1]
    width = tokens.shape[2]
    top_count = routes.shape[2]
    local_experts = expert_gate.shape[0]
    num_experts = local_experts * groups
    units = local_experts + 1
    inner = expert_gate.shape[2]
    weight_rows = expert_gate.shape[1]
    shard = query_weight.shape[0]
    head_cols = width // PLANES
    heads = head_cols // HD
    window = -(-inner // (PLANES * LANES)) * LANES
    scale = HD ** (-0.5)
    all_slots = float(groups * rows * dp_size)
    iz, ix, iy, ic = net.at["z"], net.at["x"], net.at["y"], net.at["c"]
    expert_at = iy * PAIR + ic

    tok = tokens.reshape(rows, width)
    cot = cotangent.reshape(rows, width)
    length = jnp.take(lengths, expert_at)
    own_start = (iz * across + ix) * rows
    positions = own_start + jnp.arange(rows)
    valid = positions < length
    live = valid.astype(f32)[:, None]
    token_rows = tok.astype(f32)
    grad_final = cot.astype(f32) * live

    tok_blocks = net.gather_z(tok)
    extras = jnp.concatenate(
        [
            attention_gain[:, None],
            mixer_gain[:, None],
            shared_switch[:, None],
            router_weight,
            jnp.zeros((shard, LANES - 3 - num_experts), bf16),
        ],
        axis=1,
    )

    def by_plane(w):
        return jnp.transpose(w.reshape(shard, PLANES, head_cols), (1, 0, 2))

    qkv_own = jnp.concatenate(
        [by_plane(w) for w in (query_weight, key_weight, value_weight)]
        + [jnp.broadcast_to(extras[None], (PLANES, shard, LANES))],
        axis=2,
    )
    qkv_own = net.exchange_z(qkv_own)
    starts = [min(k * window, inner - window) for k in range(PLANES)]
    plans = [[(0, j, s) for j in range(local_experts)] for s in starts]
    down_cut, gate_cut, up_cut = [
        cut_columns([w], plans, window) for w in (expert_down, expert_gate, expert_up)
    ]
    shared_cut = cut_columns(
        [shared_gate_weight, shared_up_weight, shared_down_weight],
        [
            [(k, None, e * inner + s) for k in range(3)]
            for s in starts
            for e in range(groups)
        ],
        window,
    )
    cot_all = lax.all_gather(cot, GROUP)
    down_own = net.exchange_z(after(down_cut, qkv_own))
    if across == 2 and yrows == 2:
        half = PLANES // 2
        from_x = net.turn(qkv_own, "x", 1)
        from_y = net.turn(qkv_own, "y", 1)
        across_both = jnp.concatenate(
            [net.turn(from_y[:half], "x", 1), net.turn(from_x[half:], "y", 1)], axis=0
        )
        across_both = after(across_both, down_own)
        qkv_w = net.place_rows(
            [
                net.place_rows([qkv_own, from_x], "x", 1),
                net.place_rows([from_y, across_both], "x", 1),
            ],
            "y",
            2,
        )
    else:
        qkv_w = net.place_rows(net.gather_x(qkv_own), "x", 1)
        qkv_w = net.place_rows([net.turn(qkv_w, "y", t) if t else qkv_w for t in range(yrows)], "y", 2)
    gate_own = net.exchange_z(after(gate_cut, qkv_w))
    qkv_w = net.place_rows([qkv_w, net.turn(qkv_w, "c", 1)], "c", 3)
    qkv_w = qkv_w.reshape(width, 3 * head_cols + LANES)
    small = qkv_w[:, 3 * head_cols :]
    qkv_w = qkv_w[:, : 3 * head_cols]
    small_rows = mm_t(jnp.eye(16, LANES, dtype=bf16), small)
    attn_gain_f = small_rows[0]
    mixer_gain_f = small_rows[1]
    switch_full = small[:, 2]
    switch_row = small_rows[2]
    router_full = small[:, 3 : 3 + num_experts]

    biases = jnp.concatenate(
        [
            query_bias[:, None],
            key_bias[:, None],
            value_bias[:, None],
            jnp.zeros((shard, LANES - 3), bf16),
        ],
        axis=1,
    )
    out_w = jnp.concatenate([output_weight, biases], axis=1)
    out_w = net.place_rows(net.gather_x(out_w), "x", 0)
    out_w = net.place_rows([out_w, net.turn(out_w, "y", 1)], "y", 1)
    out_w = net.place_rows([out_w, net.turn(out_w, "c", 1)], "c", 2)
    out_w = out_w.reshape(head_cols, width + LANES)
    bias_cols = out_w[:, width : width + 3].astype(f32)
    out_w = out_w[:, :width]
    qkv_bias = jnp.concatenate([bias_cols[:, 0], bias_cols[:, 1], bias_cols[:, 2]])

    def gather_rows(blocks):
        pairs = [
            jnp.concatenate(
                [
                    b if t == 0 else net.turn(b, "y", t)
                    for b in blocks[k : k + 2]
                    for t in range(yrows)
                ],
                axis=0,
            )
            for k in (0, 2)
        ]
        return jnp.concatenate(pairs + [net.turn(pair, "c", 1) for pair in pairs], axis=0)

    def row_sum(pair):
        total = pair[:, 0]
        for t in range(1, yrows):
            total = add_low(total, net.turn(pair[:, t], "y", -t))
        return total

    block_c = jnp.arange(PAIR)[:, None, None]
    block_z = jnp.arange(PLANES)[None, :, None]
    block_y = jnp.arange(yrows)[None, None, :]
    block_order = (
        (net.behind("z", block_z) * yrows + net.behind("y", block_y)) * PAIR
        + net.behind("c", block_c)
    ).reshape(-1)
    block_order = block_order.astype(jnp.int32)
    places = net.behind("x", jnp.arange(across)).astype(jnp.int32)

    hidden_rows = jnp.concatenate(tok_blocks, axis=0)
    hidden_f = hidden_rows.astype(f32)
    attn_inv_group = lax.rsqrt(jnp.mean(hidden_f * hidden_f, axis=-1, keepdims=True) + epsilon)
    normed_attn = (hidden_f * attn_inv_group * attn_gain_f).astype(bf16)
    qkv_pre = mm(normed_attn, qkv_w) + qkv_bias
    planes_held = net.planes_held()
    query_pos = jnp.concatenate(
        [
            (planes_held[s] * across + ix) * rows + jnp.arange(rows)
            for s in range(PLANES)
        ]
    )
    group_rows = PLANES * rows
    cosine, sine = rope_tables(query_pos, HD)
    queries = rotate(
        qkv_pre[:, :head_cols].reshape(group_rows, heads, HD), cosine, sine
    ).astype(bf16)
    keys_own = (
        rotate(
            qkv_pre[:, head_cols : 2 * head_cols].reshape(group_rows, heads, HD), cosine, sine
        )
        .astype(bf16)
        .reshape(group_rows, head_cols)
    )
    values_own = qkv_pre[:, 2 * head_cols :].astype(bf16)
    keys_values = net.gather_x(jnp.concatenate([keys_own, values_own], axis=1))
    key_pos = jnp.concatenate(
        [query_pos + (net.behind("x", t) - ix) * rows for t in range(across)]
    )
    all_kv = after(jnp.concatenate(keys_values, axis=0), gate_own)
    up_own = net.exchange_z(after(up_cut, all_kv))
    cot_group = take_blocks(cot_all.reshape(-1, rows, width), block_order)
    keys_all = all_kv[:, :head_cols].reshape(-1, heads, HD)
    values_all = all_kv[:, head_cols:].reshape(-1, heads, HD)
    scores = jnp.einsum("qhd,khd->hqk", queries, keys_all, preferred_element_type=f32) * scale
    allowed = (key_pos[None, :] <= query_pos[:, None]) & (key_pos[None, :] < length)
    scores = jnp.where(allowed[None], scores, neg_large)
    attn_weights = jax.nn.softmax(scores, axis=-1)
    weights_low = attn_weights.astype(bf16)
    mixed = jnp.einsum("hqk,khd->qhd", weights_low, values_all, preferred_element_type=f32)
    mixed = mixed.astype(bf16).reshape(group_rows, head_cols)
    down_pieces = net.gather_x(down_own)
    mixed = after(mixed, *down_pieces)
    branch = mm(mixed, out_w).astype(bf16).reshape(PLANES, rows, width)
    resid = token_rows
    for part in net.scatter_z(*[branch[s] for s in range(PLANES)]):
        resid = resid + part.astype(f32)

    mix_inv = lax.rsqrt(jnp.mean(resid * resid, axis=-1, keepdims=True) + epsilon)
    normed_mix = (resid * mix_inv * mixer_gain_f).astype(bf16)
    logits = mm(normed_mix, router_full)
    probs = jax.nn.softmax(logits, axis=-1)
    route_ids = routes.reshape(rows, top_count)
    chosen = (route_ids[:, :, None] == jnp.arange(num_experts)[None, None, :]) & valid[
        :, None, None
    ]
    chosen_any = jnp.sum(chosen.astype(f32), axis=1)
    gates = probs * chosen_any
    switch = jax.nn.sigmoid(mm(normed_mix, switch_full[:, None]))
    gate_count = num_experts + 1

    def two_parts(value):
        high = lax.reduce_precision(value, 8, 7)
        return [high.astype(bf16), (value - high).astype(bf16)]

    parts = two_parts(jnp.concatenate([gates, switch * live], axis=1))
    parts += [chosen_any.astype(bf16)] + two_parts(probs * live)
    extra_at = 2 * gate_count
    extra_count = 3 * num_experts
    parts.append(jnp.zeros((rows, LANES - extra_at - extra_count), bf16))
    mix_blocks = net.gather_z(jnp.concatenate([normed_mix] + parts, axis=1))
    mix_blocks = [after(b, up_own) for b in mix_blocks]
    shared_own = net.exchange_group(after(shared_cut, *mix_blocks))
    shared_own = shared_own.reshape(PLANES, weight_rows, 3 * window)
    weight_parts = [net.gather_x(gate_own), net.gather_x(up_own), down_pieces]
    shared_parts = [net.gather_x(shared_own)]
    mix_group = gather_rows(mix_blocks)

    block_sums = jnp.sum(
        mix_group[:, width + extra_at : width + extra_at + extra_count]
        .astype(f32)
        .reshape(PAIR * PLANES * yrows, rows, extra_count),
        axis=1,
    )
    block_sums = jnp.zeros_like(block_sums).at[block_order].set(block_sums)
    sums = jnp.sum(block_sums.reshape(-1, extra_count), axis=0, keepdims=True)
    sums = jnp.sum(net.place_rows(net.gather_x(sums), "x", 0)[:, 0], axis=0)
    count_all = sums[:num_experts]
    mass_all = sums[num_experts : 2 * num_experts] + sums[2 * num_experts :]
    fraction = count_all / (top_count * all_slots)
    balance_loss = (num_experts * jnp.sum(fraction * mass_all / all_slots)).reshape(1)

    column = jnp.arange(window)
    fresh = column + jnp.minimum(iz * window, inner - window) >= iz * window
    unit_at = jnp.concatenate(
        [
            expert_at * local_experts + jnp.arange(local_experts),
            jnp.full((1,), num_experts),
        ]
    )
    unit_at = jnp.broadcast_to(unit_at[:, None], (units, window)).reshape(-1)
    fresh = jnp.tile(fresh, units)
    lane = jnp.arange(LANES)
    lane_gate = jnp.where(lane < extra_at, lane % gate_count, -1)
    widen = ((lane_gate[:, None] == unit_at[None]) & fresh[None]).astype(bf16)
    fold = ((lane[None] == unit_at[:, None]) & fresh[:, None]).astype(bf16)
    split = local_experts * window
    routed = run_experts(
        places, mix_group, cot_group, widen[:, :split], fold[:split], weight_parts
    )
    shared = run_experts(
        places, mix_group, cot_group, widen[:, split:], fold[split:], shared_parts, routed[0]
    )
    back = shared[0].reshape(PAIR, PLANES, yrows, rows, -1)
    pair = add_low(back[0], net.turn(back[1], "c", 1))
    kept_far = row_sum(pair[1:3])
    kept_near = row_sum(jnp.stack([pair[0], pair[3]]))

    shared_term = run_terms(
        [
            [(after(mix_group, pair), shared[2])],
            [(after(mix_group, pair), shared[3])],
            [(after(cot_group, pair), shared[1])],
        ],
        width,
        PLANES,
        across,
    )
    mix_late = after(mix_group, shared_term, kept_far)
    pair_term = run_terms(
        [[(mix_late, routed[2])], [(mix_late, routed[3])]], width, PLANES, across
    )
    down_term = run_terms(
        [[(after(cot_group, pair_term, kept_near), routed[1])]], width, PLANES, across
    )
    grad_sum = sum(
        part.astype(f32)
        for part in net.scatter_z(kept_near[0], kept_far[0], kept_far[1], kept_near[1])
    )
    grad_sum = after(grad_sum, down_term)
    scattered = [
        net.scatter_axis(term, "x", 0).astype(bf16)
        for term in (shared_term, pair_term, down_term)
    ]
    grad_gates = grad_sum[:, width : width + num_experts]
    grad_switch = grad_sum[:, width + num_experts : width + gate_count]
    grad_switch_logit = grad_switch * live * switch * (1.0 - switch)
    grad_probs = grad_gates * chosen_any * live + live * (num_experts * fraction / all_slots)[None, :]
    grad_logits = (
        probs * (grad_probs - jnp.sum(probs * grad_probs, axis=1, keepdims=True))
    ).astype(bf16)
    grad_normed_mix = (
        grad_sum[:, :width]
        + grad_switch_logit * switch_row[None, :]
        + mm_t(grad_logits, router_full)
    )
    grad_mix_rows, grad_mixer_gain = norm_back(grad_normed_mix, resid, mix_inv, mixer_gain_f)
    grad_resid = grad_final + grad_mix_rows
    grad_branch = grad_resid.astype(bf16)
    branch_group = jnp.concatenate(net.gather_z(grad_branch), axis=0)
    out_blocks = run_output(
        places,
        block_order,
        rows,
        after(routed[1], grad_branch),
        shared[1],
        down_pieces,
        shared_parts[0],
    )
    branch_group = after(branch_group, out_blocks)
    out_sum = lax.psum_scatter(out_blocks, GROUP, scatter_dimension=0, tiled=True)[0]
    sorted_grads = [net.exchange_group(after(scattered[0], branch_group).reshape(-1, shard, 3 * window))]
    for part in scattered[1:]:
        sorted_grads.append(net.exchange_z(after(part, sorted_grads[-1])))

    grad_mixed = mm_t(branch_group, out_w).astype(bf16).reshape(group_rows, heads, HD)
    grad_attn = jnp.einsum("qhd,khd->hqk", grad_mixed, values_all, preferred_element_type=f32)
    delta = jnp.sum(attn_weights * grad_attn, axis=-1, keepdims=True)
    grad_scores = (attn_weights * (grad_attn - delta)).astype(bf16)
    grad_keys = (
        jnp.einsum("hqk,qhd->khd", grad_scores, queries, preferred_element_type=f32) * scale
    )
    grad_values = jnp.einsum("hqk,qhd->khd", weights_low, grad_mixed, preferred_element_type=f32)
    grad_kv = jnp.concatenate(
        [grad_keys.reshape(-1, head_cols), grad_values.reshape(-1, head_cols)], axis=1
    ).reshape(across, group_rows, 2 * head_cols)
    grad_kv_own = grad_kv[0]
    for t in range(1, across):
        grad_kv_own = grad_kv_own + net.turn(grad_kv[t].astype(bf16), "x", -t).astype(f32)
    grad_queries = (
        jnp.einsum("hqk,khd->qhd", grad_scores, keys_all, preferred_element_type=f32) * scale
    )
    grad_query_pre = (
        rotate_back(grad_queries, cosine, sine).reshape(group_rows, head_cols).astype(bf16)
    )
    grad_key_pre = (
        rotate_back(grad_kv_own[:, :head_cols].reshape(group_rows, heads, HD), cosine, sine)
        .reshape(group_rows, head_cols)
        .astype(bf16)
    )
    grad_value_pre = grad_kv_own[:, head_cols:].astype(bf16)
    grad_qkv = jnp.concatenate([grad_query_pre, grad_key_pre, grad_value_pre], axis=1)
    grad_qkv = after(grad_qkv, sorted_grads[0])
    grad_normed_part = mm_t(grad_qkv, qkv_w)
    gain_part = jnp.sum(grad_normed_part * hidden_f * attn_inv_group, axis=0)
    normed_part_low = grad_normed_part.astype(bf16).reshape(PLANES, rows, width)
    grad_normed_attn = jnp.zeros((rows, width), f32)
    for part in net.scatter_z(*[normed_part_low[s] for s in range(PLANES)]):
        grad_normed_attn = grad_normed_attn + part.astype(f32)
    attn_inv = attn_inv_group[:rows]
    grad_attn_rows, _ = norm_back(grad_normed_attn, token_rows, attn_inv, attn_gain_f)
    grad_tokens = (grad_resid + grad_attn_rows).astype(bf16).reshape(1, rows, width)

    layer_out = ((resid + out_sum.astype(f32)) * live).astype(bf16)

    def unit_columns(by_plane, j):
        cols = [by_plane[k, :, j * window : (j + 1) * window] for k in range(PLANES)]
        used = window * (PLANES - 1)
        cols[-1] = cols[-1][:, window - (inner - used) :]
        return jnp.concatenate(cols, axis=1)

    def routed_grads(by_plane):
        return jnp.stack(
            [unit_columns(by_plane, j) for j in range(local_experts)]
        ).astype(f32)

    grad_expert_gate = routed_grads(sorted_grads[1][:, :, :split])
    grad_expert_up = routed_grads(sorted_grads[1][:, :, split:])
    grad_expert_down = routed_grads(sorted_grads[2])
    shared_back = sorted_grads[0].reshape(PLANES, groups, shard, 3 * window)
    shared_grads = []
    for k in range(3):
        cols = []
        for e in range(groups):
            for z in range(PLANES):
                first = k * window + (window * PLANES - inner if z == PLANES - 1 else 0)
                cols.append(shared_back[z, e, :, first : (k + 1) * window])
        shared_grads.append(jnp.concatenate(cols, axis=1).astype(f32))

    def to_rows(part, dims):
        part = net.scatter_axis(part, "c", dims - 1).astype(bf16)
        cut = part.shape[-1] // (2 * LANES) * LANES
        if across > 2:
            cut = part.shape[-1]
        first = net.scatter_axis(part[..., :cut], "y", dims - 2).astype(bf16)
        first = net.scatter_axis(first, "x", dims - 3).astype(bf16)
        if cut == part.shape[-1]:
            return first
        second = net.scatter_axis(part[..., cut:], "x", dims - 3).astype(bf16)
        second = net.scatter_axis(second, "y", dims - 3).astype(bf16)
        return jnp.concatenate([first, second], axis=-1)

    grad_out_w = t_mm(mixed, branch_group).astype(bf16)
    grad_output_weight = to_rows(
        grad_out_w.reshape(across, yrows, PAIR, shard, width), 3
    ).astype(f32)
    row_terms = jnp.concatenate(
        [
            t_mm(grad_logits, normed_mix),
            jnp.sum(grad_switch_logit * normed_mix.astype(f32), axis=0)[None],
            grad_mixer_gain[None],
            gain_part[None],
            jnp.zeros((16 - num_experts - 3, width), f32),
        ],
        axis=0,
    ).astype(bf16)
    qkv_term = run_terms(
        [[(normed_attn, grad_qkv)], [(row_terms, jnp.eye(16, LANES, dtype=bf16))]],
        width,
        PLANES,
        across,
    )
    qkv_rows = to_rows(
        jnp.swapaxes(qkv_term.reshape(across, PLANES, yrows, PAIR, shard, -1), 0, 1), 4
    )
    qkv_planes = net.exchange_z(qkv_rows)
    grad_qkv_weights = [
        jnp.concatenate(
            [qkv_planes[k, :, j * head_cols : (j + 1) * head_cols] for k in range(PLANES)], axis=1
        ).astype(f32)
        for j in range(3)
    ]

    row_grads = jnp.sum(
        qkv_planes[:, :, 3 * head_cols : 3 * head_cols + num_experts + 3].astype(f32), axis=0
    )

    bias_part = jnp.sum(grad_qkv.astype(f32), axis=0).reshape(3, across, yrows, PAIR, shard)
    bias_part = jnp.transpose(bias_part, (1, 2, 3, 0, 4))
    bias_part = net.scatter_axis(bias_part, "c", 2)
    bias_part = net.scatter_axis(bias_part, "y", 1)
    bias_part = net.scatter_axis(bias_part, "x", 0)
    return (
        layer_out.reshape(1, rows, width),
        balance_loss,
        grad_tokens,
        grad_qkv_weights[0],
        grad_qkv_weights[1],
        grad_qkv_weights[2],
        grad_output_weight,
        bias_part[0],
        bias_part[1],
        bias_part[2],
        row_grads[:, num_experts + 2],
        row_grads[:, :num_experts],
        row_grads[:, num_experts],
        row_grads[:, num_experts + 1],
        shared_grads[0],
        shared_grads[1],
        shared_grads[2],
        grad_expert_gate,
        grad_expert_up,
        grad_expert_down,
    )


def solution(mesh):
    dp_size, expert_size = mesh.devices.shape
    shape = (PLANES, dp_size // PLANES, expert_size // PAIR, PAIR)
    fine = Mesh(mesh.devices.reshape(shape), ALL)
    rows = P(("y", "c"), ("z", "x"), None)
    shard2 = P(ALL, None)
    shard1 = P(ALL)
    placed = (
        (rows, rows, P(), rows)
        + (shard2,) * 4
        + (shard1,) * 4
        + (shard2, shard1, shard1)
        + (shard2,) * 3
        + (rows,) * 3
    )
    outs = (
        (rows, P(), rows)
        + (shard2,) * 4
        + (shard1,) * 4
        + (shard2, shard1, shard1)
        + (shard2,) * 3
        + (rows,) * 3
    )
    return jax.shard_map(
        per_device, mesh=fine, in_specs=placed, out_specs=outs, check_vma=False
    )
```

time: 1410 us -> 1100 us (0.78)
  Pallas kernels: 0 us -> 206 us
  local copies, waits for them, and re-layouts: 312 us -> 145 us
  matrix products: 200 us -> 48.6 us
  starting transfers between devices: 277 us -> 127 us
  waiting for transfers between devices: 518 us -> 441 us
  between operations: 6.72 us -> 21.5 us
    pallas_call x0 -> x12, Pallas kernels: none -> 206 us  [the longest x2 83.1 us: run_experts(): pl.pallas_call(lambda *refs: expert_kernel(stacked, bool(carries), across...]
    ppermute x129 -> x58, starting transfers between devices: 277 us -> 77.2 us  [turn(): lax.ppermute(value, axis, [(i, (i + steps) % size) for i in range(size)])]
    ppermute x129 -> x58, waiting for transfers between devices: 518 us -> 329 us  [turn(): lax.ppermute(value, axis, [(i, (i + steps) % size) for i in range(size)])]
    dot_general x19 -> x10, matrix products: 179 us -> 19.3 us  [mm(): lax.dot_general(left, right, (contract, ((), ())), preferred_element_type...]
    all_to_all x0 -> x9, waiting for transfers between devices: none -> 112 us  [the longest x7 112 us: exchange_z(): return lax.all_to_all(value, 'z', split_axis=0, concat_axis=0, tiled=True)]
    concatenate x15 -> x6, local copies, waits for them, and re-layouts: 88.7 us -> 5.01 us  [the longest x1 1.52 us: gather_rows(): jnp.concatenate(pairs + [net.turn(pair, 'c', 1) for pair in pairs], axis=0)]
    all_to_all x0 -> x9, starting transfers between devices: none -> 49.8 us  [the longest x7 31.1 us: exchange_z(): return lax.all_to_all(value, 'z', split_axis=0, concat_axis=0, tiled=True)]
    unnamed x411 -> x182, local copies, waits for them, and re-layouts: 71.8 us -> 40.2 us
  transfers between devices with their start and end apart: 129 -> 69, of which waited for: 48 -> 30; matrix products, arithmetic and copies ran while one was open for 31% -> 24% of each run, Pallas kernels for 0% -> 16%
where the time goes in v2:
time: 1100 us; the launch traced here: 1090 us
  waiting for transfers between devices  441 us (40%)
  Pallas kernels  206 us (19%)
  local copies, waits for them, and re-layouts  145 us (13%)
  starting transfers between devices  127 us (12%)
  other arithmetic  97.1 us (9%)
  matrix products  48.6 us (4%)
  between operations  21.5 us (2%)
    ppermute x58, waiting for transfers between devices, turn(): lax.ppermute(value, axis, [(i, (i + steps) % size) for i in range(size)])  329 us
    all_to_all x7, waiting for transfers between devices, exchange_z(): return lax.all_to_all(value, 'z', split_axis=0, concat_axis=0, tiled=True)  112 us
    pallas_call x2, Pallas kernels, run_experts(): pl.pallas_call(lambda *refs: expert_kernel(stacked, bool(carries), across...  83.1 us
    ppermute x58, starting transfers between devices, turn(): lax.ppermute(value, axis, [(i, (i + steps) % size) for i in range(size)])  77.2 us
    pallas_call x4, Pallas kernels, run_terms(): pl.pallas_call(lambda *refs: term_kernel(numbers, *refs), grid=(steps,),...  61.1 us
    unnamed x182, local copies, waits for them, and re-layouts  40.2 us
    pallas_call x1, Pallas kernels, run_output(): pl.pallas_call(lambda *refs: output_kernel(across, *refs), grid_spec=pltp...  31.5 us
    all_to_all x7, starting transfers between devices, exchange_z(): return lax.all_to_all(value, 'z', split_axis=0, concat_axis=0, tiled=True)  31.1 us
  transfers between devices with their start and end apart: 69, of which 30 were waited for; matrix products, arithmetic and copies ran while one was open for 24% of the time, Pallas kernels for 16%

profile of v2, /device:TPU:0, one launch (start us, length us, event | category | flops | bytes accessed | tf_op | source)
XLA Modules:
  0.0 1086.3 jit_solution(2711761289478855009)
XLA Ops:
  50.8 53.7 %all-to-all-done = bf16[4,64,1664]{2,1,0:T(8,128)(2,1)S(1)} async-done(((bf16[4,64,1664]{2,1,0:T(8,128)(2,1)}), bf16[4,64,1664]{2,1,0:T(8,128)(2,1)S(1)}, u32[]{:S(2)}, u32[]{:S(2)}) %all-to-all-start) | async-done | bytes 852000 | tf_op jit(solution)/shard_map/all_to_all | solution.py:109
  117.5 12.1 %collective-permute-done.4 = bf16[4,64,1664]{2,1,0:T(8,128)(2,1)S(1)} collective-permute-done((bf16[4,64,1664]{2,1,0:T(8,128)(2,1)S(1)}, bf16[4,64,1664]{2,1,0:T(8,128)(2,1)S(1)}, u32[]{:S(2)}, u32[]{:S(2)}) %collective-permute-start.4) | collective-permute-done | bytes 852000 | tf_op jit(solution)/shard_map/ppermute | solution.py:85
  142.4 18.7 %all-to-all-done.1.refs_9_.refs_4_ = bf16[4,256,768]{2,1,0:T(8,128)(2,1)} async-done(((bf16[4,256,768]{2,1,0:T(8,128)(2,1)}), bf16[4,256,768]{2,1,0:T(8,128)(2,1)}, u32[]{:S(2)}, u32[]{:S(2)}) %all-to-all-start.1) | async-done | bytes 1572896 | tf_op jit(solution)/shard_map/all_to_all | solution.py:109
  211.1 16.5 %collective-permute-done.11 = bf16[512,1024]{1,0:T(8,128)(2,1)} collective-permute-done((bf16[512,1024]{1,0:T(8,128)(2,1)}, bf16[512,1024]{1,0:T(8,128)(2,1)}, u32[]{:S(2)}, u32[]{:S(2)}) %collective-permute-start.11) | collective-permute-done | bytes 1048608 | tf_op jit(solution)/shard_map/ppermute | solution.py:85
  246.1 14.4 %collective-permute-done.12.refs_10_.refs_5_ = bf16[4,256,768]{2,1,0:T(8,128)(2,1)} collective-permute-done((bf16[4,256,768]{2,1,0:T(8,128)(2,1)}, bf16[4,256,768]{2,1,0:T(8,128)(2,1)}, u32[]{:S(2)}, u32[]{:S(2)}) %collective-permute-start.12) | collective-permute-done | bytes 1572896 | tf_op jit(solution)/shard_map/ppermute | solution.py:85
  280.3 50.5 %collective-permute-done.14 = bf16[128,2048]{1,0:T(8,128)(2,1)S(1)} collective-permute-done((bf16[128,2048]{1,0:T(8,128)(2,1)S(1)}, bf16[128,2048]{1,0:T(8,128)(2,1)S(1)}, u32[]{:S(2)}, u32[]{:S(2)}) %collective-permute-start.14) | collective-permute-done | bytes 524320 | tf_op jit(solution)/shard_map/ppermute | solution.py:85
  357.5 35.9 %collective-permute-done.19 = bf16[128,2176]{1,0:T(8,128)(2,1)S(1)} collective-permute-done((bf16[128,2176]{1,0:T(8,128)(2,1)S(1)}, bf16[128,2176]{1,0:T(8,128)(2,1)S(1)}, u32[]{:S(2)}, u32[]{:S(2)}) %collective-permute-start.19) | collective-permute-done | bytes 557088 | tf_op jit(solution)/shard_map/ppermute | solution.py:85
  422.5 22.0 %collective-permute-done.18 = bf16[128,2176]{1,0:T(8,128)(2,1)} collective-permute-done((bf16[128,2176]{1,0:T(8,128)(2,1)}, bf16[128,2176]{1,0:T(8,128)(2,1)}, u32[]{:S(2)}, u32[]{:S(2)}) %collective-permute-start.18) | collective-permute-done | bytes 557088 | tf_op jit(solution)/shard_map/ppermute | solution.py:85
  444.4 15.2 %collective-permute-done.16 = bf16[128,2176]{1,0:T(8,128)(2,1)} collective-permute-done((bf16[128,2176]{1,0:T(8,128)(2,1)S(1)}, bf16[128,2176]{1,0:T(8,128)(2,1)}, u32[]{:S(2)}, u32[]{:S(2)}) %collective-permute-start.16) | collective-permute-done | bytes 557088 | tf_op jit(solution)/shard_map/ppermute | solution.py:85
  481.1 13.0 %shard_map.359.refs_2_.refs_0_ = bf16[2048,2048]{1,0:T(8,128)(2,1)} custom-call(s32[16]{0:T(128)} %add.601.order_ref.refs_1_, bf16[16,128,2048]{2,1,0:T(8,128)(2,1)} %all-gather.2.cloned.1.call-done.source_ref), custom_call_target="tpu_custom_call" | custom-call | bytes 16777216 | tf_op jit(solution)/shard_map/pallas_call | solution.py:300
  494.1 51.2 %shard_map.360 = (bf16[2048,2176]{1,0:T(8,128)(2,1)}, bf16[2048,768]{1,0:T(8,128)(2,1)}, bf16[2048,768]{1,0:T(8,128)(2,1)}, bf16[2048,768]{1,0:T(8,128)(2,1)}) custom-call(s32[2]{0:T(128)} %and_select_fusion.3.refs_0_, bf16[2048,2176]{1,0:T(8,128)(2,1)} %constant_dynamic-update-slice_fusion.refs_1_.refs_0_, bf16[2048,2048]{1,0:T(8,128)(2,1)} %shard_map.359.refs_2_.refs_0_, ...), custom_call_target="tpu_custom_call" | custom-call | flops 32212254720 | bytes 45088768 | tf_op jit(solution)/shard_map/pallas_call | solution.py:224
  545.3 31.9 %shard_map.362 = (bf16[2048,2176]{1,0:T(8,128)(2,1)}, bf16[2048,384]{1,0:T(8,128)(2,1)}, bf16[2048,384]{1,0:T(8,128)(2,1)}, bf16[2048,384]{1,0:T(8,128)(2,1)}) custom-call(s32[2]{0:T(128)} %and_select_fusion.3.refs_0_, bf16[2048,2176]{1,0:T(8,128)(2,1)} %constant_dynamic-update-slice_fusion.refs_1_.refs_0_, bf16[2048,2048]{1,0:T(8,128)(2,1)} %shard_map.359.refs_2_.refs_0_, ...), custom_call_target="tpu_custom_call" | custom-call | flops 16106127360 | bytes 35651584 | tf_op jit(solution)/shard_map/pallas_call | solution.py:224
  604.3 20.2 %shard_map.363 = bf16[2,4,256,1152]{3,2,1,0:T(8,128)(2,1)} custom-call(bf16[2048,2176]{1,0:T(8,128)(2,1)} %constant_dynamic-update-slice_fusion.refs_1_.refs_0_, bf16[2048,2176]{1,0:T(8,128)(2,1)} %constant_dynamic-update-slice_fusion.refs_1_.refs_0_, bf16[2048,2048]{1,0:T(8,128)(2,1)} %shard_map.359.refs_2_.refs_0_, ...), custom_call_target="tpu_custom_call" | custom-call | flops 9663676416 | bytes 35651584 | tf_op jit(solution)/shard_map/pallas_call | solution.py:355
  630.6 20.4 %collective-permute-done.29 = bf16[2,128,2176]{2,1,0:T(8,128)(2,1)} collective-permute-done((bf16[2,128,2176]{2,1,0:T(8,128)(2,1)}, bf16[2,128,2176]{2,1,0:T(8,128)(2,1)}, u32[]{:S(2)}, u32[]{:S(2)}) %collective-permute-start.29) | collective-permute-done | bytes 1114144 | tf_op jit(solution)/shard_map/ppermute | solution.py:85
  652.5 19.0 %shard_map.364 = bf16[2,4,256,1536]{3,2,1,0:T(8,128)(2,1)} custom-call(bf16[2048,2176]{1,0:T(8,128)(2,1)} %constant_dynamic-update-slice_fusion.refs_1_.refs_0_, bf16[2048,768]{1,0:T(8,128)(2,1)} %get-tuple-element.70.refs_1_, bf16[2048,768]{1,0:T(8,128)(2,1)} %get-tuple-element.71.refs_2_), custom_call_target="tpu_custom_call" | custom-call | flops 12884901888 | bytes 21495808 | tf_op jit(solution)/shard_map/pallas_call | solution.py:355
  673.6 12.5 %shard_map.365 = bf16[2,4,256,768]{3,2,1,0:T(8,128)(2,1)} custom-call(bf16[2048,2048]{1,0:T(8,128)(2,1)} %shard_map.359.refs_2_.refs_0_, bf16[2048,768]{1,0:T(8,128)(2,1)} %get-tuple-element.74.refs_1_.refs_2_), custom_call_target="tpu_custom_call" | custom-call | flops 6442450944 | bytes 14680064 | tf_op jit(solution)/shard_map/pallas_call | solution.py:355
  692.7 19.9 %collective-permute-done.32 = bf16[128,2176]{1,0:T(8,128)(2,1)S(1)} collective-permute-done((bf16[128,2176]{1,0:T(8,128)(2,1)S(1)}, bf16[128,2176]{1,0:T(8,128)(2,1)S(1)}, u32[]{:S(2)}, u32[]{:S(2)}) %collective-permute-start.32) | collective-permute-done | bytes 557088 | tf_op jit(solution)/shard_map/ppermute | solution.py:85
  729.9 31.5 %shard_map.366 = bf16[16,128,2048]{2,1,0:T(8,128)(2,1)} custom-call(s32[2]{0:T(128)} %and_select_fusion.3.refs_0_, s32[16]{0:T(128)} %add.601.order_ref.refs_1_, bf16[2048,768]{1,0:T(8,128)(2,1)} %get-tuple-element.74.refs_1_.refs_2_, bf16[2048,384]{1,0:T(8,128)(2,1)} %get-tuple-element.68.refs_5_.refs_3_, ...), custom_call_target="tpu_custom_call" | custom-call | flops 9663676416 | bytes 17825792 | tf_op jit(solution)/shard_map/pallas_call | solution.py:268
  806.8 14.3 %all-to-all-start.5 = ((bf16[16,64,1152]{2,1,0:T(8,128)(2,1)}), bf16[16,64,1152]{2,1,0:T(8,128)(2,1)}, u32[]{:S(2)}, u32[]{:S(2)}) async-start(bf16[16,64,1152]{2,1,0:T(8,128)(2,1)} %bitcast.567), calls=%async_computation.6 | async-start | bytes 4718592 | tf_op jit(solution)/shard_map/all_to_all | solution.py:132
  824.6 29.5 %collective-permute-done.38 = bf16[512,1024]{1,0:T(8,128)(2,1)} collective-permute-done((bf16[512,1024]{1,0:T(8,128)(2,1)}, bf16[512,1024]{1,0:T(8,128)(2,1)}, u32[]{:S(2)}, u32[]{:S(2)}) %collective-permute-start.38) | collective-permute-done | bytes 1048608 | tf_op jit(solution)/shard_map/ppermute | solution.py:85
  948.9 11.5 %collective-permute-done.55 = f32[3,64]{1,0:T(4,128)S(1)} collective-permute-done((f32[3,64]{1,0:T(4,128)S(1)}, f32[3,64]{1,0:T(4,128)S(1)}, u32[]{:S(2)}, u32[]{:S(2)}) %collective-permute-start.55) | collective-permute-done | bytes 800 | tf_op jit(solution)/shard_map/ppermute | solution.py:85
  977.2 14.2 %all-to-all-done.7 = bf16[4,256,1536]{2,1,0:T(8,128)(2,1)} async-done(((bf16[4,256,1536]{2,1,0:T(8,128)(2,1)}), bf16[4,256,1536]{2,1,0:T(8,128)(2,1)}, u32[]{:S(2)}, u32[]{:S(2)}) %all-to-all-start.7) | async-done | bytes 3145760 | tf_op jit(solution)/shard_map/all_to_all | solution.py:109
  994.9 28.1 %collective-permute-done.41 = bf16[128,2048]{1,0:T(8,128)(2,1)} collective-permute-done((bf16[128,2048]{1,0:T(8,128)(2,1)}, bf16[128,2048]{1,0:T(8,128)(2,1)}, u32[]{:S(2)}, u32[]{:S(2)}) %collective-permute-start.41) | collective-permute-done | bytes 524320 | tf_op jit(solution)/shard_map/ppermute | solution.py:85
  1048.4 25.3 %all-to-all-done.8 = bf16[4,256,768]{2,1,0:T(8,128)(2,1)S(1)} async-done(((bf16[4,256,768]{2,1,0:T(8,128)(2,1)}), bf16[4,256,768]{2,1,0:T(8,128)(2,1)S(1)}, u32[]{:S(2)}, u32[]{:S(2)}) %all-to-all-start.8) | async-done | bytes 1572896 | tf_op jit(solution)/shard_map/all_to_all | solution.py:109
  (579 shorter events, 483.6 us)
Async XLA Ops:
  7.2 158.9 %collective-permute-start = (bf16[128,2048]{1,0:T(8,128)(2,1)}, bf16[128,2048]{1,0:T(8,128)(2,1)}, u32[]{:S(2)}, u32[]{:S(2)}) collective-permute-start(bf16[128,2048]{1,0:T(8,128)(2,1)} %bitcast.555), channel_id=1, source_target_pairs={{0,8},{8,16},{16,24},{24,0},{1,9},{9,17},{17,25},{25,1},{2,10},{10... | collective-permute-start | bytes 1572872 | tf_op jit(solution)/shard_map/ppermute | solution.py:85
  10.3 155.8 %collective-permute-start.1 = (bf16[128,2048]{1,0:T(8,128)(2,1)}, bf16[128,2048]{1,0:T(8,128)(2,1)}, u32[]{:S(2)}, u32[]{:S(2)}) collective-permute-start(bf16[128,2048]{1,0:T(8,128)(2,1)} %bitcast.556), channel_id=1, source_target_pairs={{0,16},{8,24},{16,0},{24,8},{1,17},{9,25},{17,1},{25,9},{2,18},{10... | collective-permute-start | bytes 1572872 | tf_op jit(solution)/shard_map/ppermute | solution.py:85
  12.9 153.2 %collective-permute-start.2 = (bf16[128,2048]{1,0:T(8,128)(2,1)}, bf16[128,2048]{1,0:T(8,128)(2,1)}, u32[]{:S(2)}, u32[]{:S(2)}) collective-permute-start(bf16[128,2048]{1,0:T(8,128)(2,1)} %bitcast.557), channel_id=1, source_target_pairs={{0,24},{8,0},{16,8},{24,16},{1,25},{9,1},{17,9},{25,17},{2,26},{10... | collective-permute-start | bytes 1572872 | tf_op jit(solution)/shard_map/ppermute | solution.py:85
  25.2 79.3 %all-to-all-start = ((bf16[4,64,1664]{2,1,0:T(8,128)(2,1)}), bf16[4,64,1664]{2,1,0:T(8,128)(2,1)S(1)}, u32[]{:S(2)}, u32[]{:S(2)}) async-start(bf16[4,64,1664]{2,1,0:T(8,128)(2,1)} %copy.357), calls=%async_computation | async-start | bytes 1703936 | tf_op jit(solution)/shard_map/all_to_all | solution.py:109
  28.7 452.4 %all-gather.2.cloned.1.call-start = ((), (), s32[]{:S(2)}) async-start(), calls=%async_computation.10 | async-start | bytes 8912896 | tf_op jit(solution)/shard_map/all_gather | solution.py:498
  267.5 63.3 %collective-permute-start.14 = (bf16[128,2048]{1,0:T(8,128)(2,1)S(1)}, bf16[128,2048]{1,0:T(8,128)(2,1)S(1)}, u32[]{:S(2)}, u32[]{:S(2)}) collective-permute-start(bf16[128,2048]{1,0:T(8,128)(2,1)S(1)} %get-tuple-element.284), channel_id=1, source_target_pairs={{0,16},{8,24},{16,0},{24,8},{1,17},{9,25},{17,1},{25,9},{2,18},{10... | collective-permute-start | bytes 1572872 | tf_op jit(solution)/shard_map/ppermute | solution.py:85
  267.5 63.3 %collective-permute-start.15 = (bf16[128,2048]{1,0:T(8,128)(2,1)S(1)}, bf16[128,2048]{1,0:T(8,128)(2,1)S(1)}, u32[]{:S(2)}, u32[]{:S(2)}) collective-permute-start(bf16[128,2048]{1,0:T(8,128)(2,1)S(1)} %get-tuple-element.283), channel_id=1, source_target_pairs={{0,8},{8,16},{16,24},{24,0},{1,9},{9,17},{17,25},{25,1},{2,10},{10... | collective-permute-start | bytes 1572872 | tf_op jit(solution)/shard_map/ppermute | solution.py:85
  271.0 86.6 %all-to-all-start.3 = ((bf16[4,256,768]{2,1,0:T(8,128)(2,1)}), bf16[4,256,768]{2,1,0:T(8,128)(2,1)}, u32[]{:S(2)}, u32[]{:S(2)}) async-start(bf16[4,256,768]{2,1,0:T(8,128)(2,1)} %shard_map.358), calls=%async_computation.3 | async-start | bytes 3145728 | tf_op jit(solution)/shard_map/all_to_all | solution.py:109
  336.1 57.3 %collective-permute-start.19 = (bf16[128,2176]{1,0:T(8,128)(2,1)S(1)}, bf16[128,2176]{1,0:T(8,128)(2,1)S(1)}, u32[]{:S(2)}, u32[]{:S(2)}) collective-permute-start(bf16[128,2176]{1,0:T(8,128)(2,1)S(1)} %concatenate.155), channel_id=1, source_target_pairs={{0,16},{8,24},{16,0},{24,8},{1,17},{9,25},{17,1},{25,9},{2,18},{10... | collective-permute-start | bytes 1671176 | tf_op jit(solution)/shard_map/ppermute | solution.py:85
  345.1 66.7 %collective-permute-start.17 = (bf16[128,2176]{1,0:T(8,128)(2,1)S(1)}, bf16[128,2176]{1,0:T(8,128)(2,1)}, u32[]{:S(2)}, u32[]{:S(2)}) collective-permute-start(bf16[128,2176]{1,0:T(8,128)(2,1)S(1)} %concatenate.155), channel_id=1, source_target_pairs={{0,8},{8,16},{16,24},{24,0},{1,9},{9,17},{17,25},{25,1},{2,10},{10... | collective-permute-start | bytes 1671176 | tf_op jit(solution)/shard_map/ppermute | solution.py:85
  410.2 83.8 %collective-permute-start.25 = (bf16[4,256,768]{2,1,0:T(8,128)(2,1)}, bf16[4,256,768]{2,1,0:T(8,128)(2,1)}, u32[]{:S(2)}, u32[]{:S(2)}) collective-permute-start(bf16[4,256,768]{2,1,0:T(8,128)(2,1)} %all-to-all-done.2.refs_5_), channel_id=1, source_target_pairs={{0,4},{4,0},{1,5},{5,1},{2,6},{6,2},{3,7},{7,3},{8,12},{12,8},{9,1... | collective-permute-start | bytes 4718600 | tf_op jit(solution)/shard_map/ppermute | solution.py:85
  413.7 61.8 %all-to-all-start.4 = ((bf16[16,64,1152]{2,1,0:T(8,128)(2,1)}), bf16[16,64,1152]{2,1,0:T(8,128)(2,1)}, u32[]{:S(2)}, u32[]{:S(2)}) async-start(bf16[16,64,1152]{2,1,0:T(8,128)(2,1)} %shard_map.361), calls=%async_computation.4 | async-start | bytes 4718592 | tf_op jit(solution)/shard_map/all_to_all | solution.py:132
  418.2 657.6 %reduce-scatter.2.cloned.1.call-start = ((), (), s32[]{:S(2)}) async-start(), calls=%async_computation.11 | async-start | bytes 8912896 | tf_op jit(solution)/shard_map/reduce_scatter | solution.py:749
  419.1 75.0 %collective-permute-start.26 = (bf16[4,256,768]{2,1,0:T(8,128)(2,1)}, bf16[4,256,768]{2,1,0:T(8,128)(2,1)}, u32[]{:S(2)}, u32[]{:S(2)}) collective-permute-start(bf16[4,256,768]{2,1,0:T(8,128)(2,1)} %all-to-all-done.3.refs_7_), channel_id=1, source_target_pairs={{0,4},{4,0},{1,5},{5,1},{2,6},{6,2},{3,7},{7,3},{8,12},{12,8},{9,1... | collective-permute-start | bytes 4718600 | tf_op jit(solution)/shard_map/ppermute | solution.py:85
  475.5 69.8 %collective-permute-start.27 = (bf16[4,256,1152]{2,1,0:T(8,128)(2,1)}, bf16[4,256,1152]{2,1,0:T(8,128)(2,1)}, u32[]{:S(2)}, u32[]{:S(2)}) collective-permute-start(bf16[4,256,1152]{2,1,0:T(8,128)(2,1)} %bitcast.45.refs_6_), channel_id=1, source_target_pairs={{0,4},{4,0},{1,5},{5,1},{2,6},{6,2},{3,7},{7,3},{8,12},{12,8},{9,1... | collective-permute-start | bytes 7077896 | tf_op jit(solution)/shard_map/ppermute | solution.py:85
  627.7 174.6 %collective-permute-start.39 = (bf16[4,256,1152]{2,1,0:T(8,128)(2,1)}, bf16[4,256,1152]{2,1,0:T(8,128)(2,1)}, u32[]{:S(2)}, u32[]{:S(2)}) collective-permute-start(bf16[4,256,1152]{2,1,0:T(8,128)(2,1)} %dynamic-slice_bitcast_fusion.1), channel_id=1, source_target_pairs={{0,4},{4,0},{1,5},{5,1},{2,6},{6,2},{3,7},{7,3},{8,12},{12,8},{9,1... | collective-permute-start | bytes 7077896 | tf_op jit(solution)/shard_map/ppermute | solution.py:85
  688.7 132.4 %collective-permute-start.57 = (bf16[4,256,768]{2,1,0:T(8,128)(2,1)}, bf16[4,256,768]{2,1,0:T(8,128)(2,1)}, u32[]{:S(2)}, u32[]{:S(2)}) collective-permute-start(bf16[4,256,768]{2,1,0:T(8,128)(2,1)} %dynamic-slice_bitcast_fusion.2), channel_id=1, source_target_pairs={{0,4},{4,0},{1,5},{5,1},{2,6},{6,2},{3,7},{7,3},{8,12},{12,8},{9,1... | collective-permute-start | bytes 4718600 | tf_op jit(solution)/shard_map/ppermute | solution.py:85
  762.0 125.7 %collective-permute-start.56 = (bf16[4,256,1536]{2,1,0:T(8,128)(2,1)}, bf16[4,256,1536]{2,1,0:T(8,128)(2,1)}, u32[]{:S(2)}, u32[]{:S(2)}) collective-permute-start(bf16[4,256,1536]{2,1,0:T(8,128)(2,1)} %dynamic-slice_bitcast_fusion), channel_id=1, source_target_pairs={{0,4},{4,0},{1,5},{5,1},{2,6},{6,2},{3,7},{7,3},{8,12},{12,8},{9,1... | collective-permute-start | bytes 9437192 | tf_op jit(solution)/shard_map/ppermute | solution.py:85
  794.2 60.0 %collective-permute-start.38 = (bf16[512,1024]{1,0:T(8,128)(2,1)}, bf16[512,1024]{1,0:T(8,128)(2,1)}, u32[]{:S(2)}, u32[]{:S(2)}) collective-permute-start(bf16[512,1024]{1,0:T(8,128)(2,1)} %fusion.26), channel_id=1, source_target_pairs={{0,4},{4,0},{1,5},{5,1},{2,6},{6,2},{3,7},{7,3},{8,12},{12,8},{9,1... | collective-permute-start | bytes 3145736 | tf_op jit(solution)/shard_map/ppermute | solution.py:85
  802.4 62.4 %collective-permute-start.48 = (bf16[2,2,64,2048]{3,2,1,0:T(8,128)(2,1)}, bf16[2,2,64,2048]{3,2,1,0:T(8,128)(2,1)}, u32[]{:S(2)}, u32[]{:S(2)}) collective-permute-start(bf16[2,2,64,2048]{3,2,1,0:T(8,128)(2,1)} %dynamic-slice_bitcast_fusion.3), channel_id=1, source_target_pairs={{0,1},{1,0},{2,3},{3,2},{4,5},{5,4},{6,7},{7,6},{8,9},{9,8},{10,11... | collective-permute-start | bytes 3145736 | tf_op jit(solution)/shard_map/ppermute | solution.py:85
  806.8 85.4 %all-to-all-start.5 = ((bf16[16,64,1152]{2,1,0:T(8,128)(2,1)}), bf16[16,64,1152]{2,1,0:T(8,128)(2,1)}, u32[]{:S(2)}, u32[]{:S(2)}) async-start(bf16[16,64,1152]{2,1,0:T(8,128)(2,1)} %bitcast.567), calls=%async_computation.6 | async-start | bytes 4718592 | tf_op jit(solution)/shard_map/all_to_all | solution.py:132
  892.1 99.2 %all-to-all-start.7 = ((bf16[4,256,1536]{2,1,0:T(8,128)(2,1)}), bf16[4,256,1536]{2,1,0:T(8,128)(2,1)}, u32[]{:S(2)}, u32[]{:S(2)}) async-start(bf16[4,256,1536]{2,1,0:T(8,128)(2,1)} %fusion.4), calls=%async_computation.8 | async-start | bytes 6291456 | tf_op jit(solution)/shard_map/all_to_all | solution.py:109
  948.9 74.1 %collective-permute-start.41 = (bf16[128,2048]{1,0:T(8,128)(2,1)}, bf16[128,2048]{1,0:T(8,128)(2,1)}, u32[]{:S(2)}, u32[]{:S(2)}) collective-permute-start(bf16[128,2048]{1,0:T(8,128)(2,1)} %get-tuple-element.281), channel_id=1, source_target_pairs={{0,16},{8,24},{16,0},{24,8},{1,17},{9,25},{17,1},{25,9},{2,18},{10... | collective-permute-start | bytes 1572872 | tf_op jit(solution)/shard_map/ppermute | solution.py:85
  960.4 62.6 %collective-permute-start.42 = (bf16[128,2048]{1,0:T(8,128)(2,1)}, bf16[128,2048]{1,0:T(8,128)(2,1)}, u32[]{:S(2)}, u32[]{:S(2)}) collective-permute-start(bf16[128,2048]{1,0:T(8,128)(2,1)} %get-tuple-element.280), channel_id=1, source_target_pairs={{0,8},{8,16},{16,24},{24,0},{1,9},{9,17},{17,25},{25,1},{2,10},{10... | collective-permute-start | bytes 1572872 | tf_op jit(solution)/shard_map/ppermute | solution.py:85
  (123 other events, 2544.1 us)
Sparse Core Ops, SparseCore 0:
  31.7 123.3 all-gather.1
  761.9 129.1 reduce-scatter.1

commit v3 on v2

--- a/solution.py
+++ b/solution.py
@@ -11,10 +11,10 @@
 LANES = 128
 PLANES = 4
 PAIR = 2
-TILE = 256
 VMEM_BYTES = 56 * 2**20
 ALL = ("z", "x", "y", "c")
 GROUP = ("z", "y", "c")
+TILES = ("c", "z", "y")
 
 f32 = jnp.float32
 bf16 = jnp.bfloat16
@@ -145,7 +145,7 @@
             planes, block = source.shape[:2]
             for z in range(planes):
                 row = pl.multiple_of((z * across + places_ref[t]) * block, block)
-                view = source.at[z] if first is None else source.at[z, :, pl.ds(first, cols)]
+                view = source.at[z, :, pl.ds(first, cols)]
                 made.append(
                     pltpu.make_async_copy(
                         view, target.at[pl.ds(row, block)], sems.at[len(made)]
@@ -163,34 +163,41 @@
             copy.wait()
 
 
-def expert_kernel(stacked, carried, across, places_ref, rows_ref, cot_ref, widen_ref, fold_ref, *refs):
-    if carried:
-        carry_ref, refs = refs[0], refs[1:]
-    count = across if stacked else 3 * across
-    sources = refs[:count]
-    back_ref, hidden_ref, grad_gate_ref, grad_up_ref = refs[count : count + 4]
-    gate_w, up_w, down_w, sems = refs[count + 4 :]
-    width = cot_ref.shape[1]
-    wide = gate_w.shape[1]
-    if stacked:
-        pieces = [[(source, k * wide) for source in sources] for k in range(3)]
+def expert_kernel(second, across, places_ref, order_ref, rows_ref, cot_ref, widen_ref, fold_ref, *refs):
+    tile = rows_ref.shape[0]
+    half = tile // 2
+    own_at = pl.multiple_of(places_ref[across] * half, half)
+    other_at = pl.multiple_of(half - own_at, half)
+    if second:
+        carry_ref, first_ref, refs = refs[0], refs[1], refs[2:]
+    count = 2 * across if second else across
+    outs, scratch = refs[count : count + 5], refs[count + 5 :]
+    wide = scratch[0].shape[1]
+    pieces = [[(source, k * wide) for source in refs[:across]] for k in range(3)]
+    if second:
+        pieces.append([(source, 2 * first_ref.shape[1]) for source in refs[across:count]])
+    back_ref, hidden_ref, grad_gate_ref, grad_up_ref, last_ref = outs
+    gate_w, up_w, down_w = scratch[:3]
+    load_weights(places_ref, pieces, scratch[:-1], scratch[-1])
+    if second:
+        cot = cot_ref[...]
     else:
-        pieces = [
-            [(source, None) for source in sources[k * across : (k + 1) * across]]
-            for k in range(3)
-        ]
-    load_weights(places_ref, pieces, (gate_w, up_w, down_w), sems)
-
+        cot = jnp.concatenate(
+            [cot_ref[0, pl.ds(own_at, half)], cot_ref[0, pl.ds(other_at, half)]], axis=0
+        )
+        last_ref[...] = cot
+    width = cot.shape[1]
     payload = rows_ref[...]
     rows = payload[:, :width]
     wide_gate = mm(payload[:, width:], widen_ref[...])
     gate = mm(rows, gate_w[...])
     up = mm(rows, up_w[...])
-    grad_hidden = mm(cot_ref[...], down_w[...])
+    grad_hidden = mm(cot, down_w[...])
     sigma = 1.0 / (1.0 + jnp.exp(-gate))
     act = gate * sigma
     hidden = act * up
-    hidden_ref[...] = (hidden * wide_gate).astype(bf16)
+    hidden_gated = (hidden * wide_gate).astype(bf16)
+    hidden_ref[...] = hidden_gated
     tail = mm((hidden * grad_hidden).astype(bf16), fold_ref[...])
     grad_hidden = grad_hidden * wide_gate
     grad_gate = (grad_hidden * up * (sigma * (1.0 + gate * (1.0 - sigma)))).astype(bf16)
@@ -198,137 +205,88 @@
     grad_gate_ref[...] = grad_gate
     grad_up_ref[...] = grad_up
     back = mm_t(grad_gate, gate_w[...]) + mm_t(grad_up, up_w[...])
-    if carried:
+    if second:
         back = back + carry_ref[:, :width].astype(f32)
         tail = tail + carry_ref[:, width:].astype(f32)
+        out = mm_t(first_ref[...], scratch[3][...]) + mm_t(hidden_gated, down_w[...])
+        last_ref[0, pl.ds(own_at, half)] = out[:half].astype(bf16)
+        last_ref[0, pl.ds(other_at, half)] = out[half:].astype(bf16)
     back_ref[:, :width] = back.astype(bf16)
     back_ref[:, width:] = tail.astype(bf16)
 
 
-def run_experts(places, rows, cot, widen, fold, weights, carry=None):
-    stacked = len(weights) == 1
+def run_experts(places, order, tile, rows, cot, widen, fold, weights, carry=None, first=None):
+    second = carry is not None
     across = len(weights[0])
     flat = [piece for per_weight in weights for piece in per_weight]
     planes = flat[0].shape[0]
     wide = widen.shape[1]
-    count, width = cot.shape
-    full = rows.shape[1]
-    carries = [] if carry is None else [carry]
+    count, full = rows.shape
+    width = cot.shape[-1]
 
     def row_block(cols):
-        return pl.BlockSpec((TILE, cols), lambda i, p: (i, 0))
+        return pl.BlockSpec((tile, cols), lambda i, p, o: (i, 0))
 
     def whole(a):
-        return pl.BlockSpec(a.shape, lambda i, p: (0, 0))
-
+        return pl.BlockSpec(a.shape, lambda i, p, o: (0, 0))
+
+    placed = pl.BlockSpec((1, tile, width), lambda i, p, o: (o[i], 0, 0))
+    extra = [carry, first] if second else []
+    scratch = [pltpu.VMEM((width, wide), bf16)] * 3
+    if second:
+        scratch.append(pltpu.VMEM((width, first.shape[1]), bf16))
     return pl.pallas_call(
-        lambda *refs: expert_kernel(stacked, bool(carries), across, *refs),
+        lambda *refs: expert_kernel(second, across, *refs),
         grid_spec=pltpu.PrefetchScalarGridSpec(
-            num_scalar_prefetch=1,
-            grid=(count // TILE,),
-            in_specs=[row_block(full), row_block(width), whole(widen), whole(fold)]
-            + [row_block(full)] * len(carries)
+            num_scalar_prefetch=2,
+            grid=(count // tile,),
+            in_specs=[
+                row_block(full),
+                row_block(width) if second else placed,
+                whole(widen),
+                whole(fold),
+            ]
+            + [row_block(a.shape[1]) for a in extra]
             + [pl.BlockSpec(memory_space=pl.ANY)] * len(flat),
-            out_specs=[row_block(full)] + [row_block(wide)] * 3,
-            scratch_shapes=[pltpu.VMEM((width, wide), bf16)] * 3
-            + [pltpu.SemaphoreType.DMA((3 * across * planes,))],
+            out_specs=[row_block(full)]
+            + [row_block(wide)] * 3
+            + [placed if second else row_block(width)],
+            scratch_shapes=scratch
+            + [pltpu.SemaphoreType.DMA((len(scratch) * across * planes,))],
         ),
         out_shape=[jax.ShapeDtypeStruct((count, full), bf16)]
-        + [jax.ShapeDtypeStruct((count, wide), bf16)] * 3,
+        + [jax.ShapeDtypeStruct((count, wide), bf16)] * 3
+        + [
+            jax.ShapeDtypeStruct(
+                (count // tile, tile, width) if second else (count, width), bf16
+            )
+        ],
         compiler_params=pltpu.CompilerParams(
             vmem_limit_bytes=VMEM_BYTES, dimension_semantics=("arbitrary",)
         ),
         cost_estimate=pl.CostEstimate(
             flops=2 * count * width * wide * 5,
-            bytes_accessed=3 * width * wide * 2 + count * (2 * full + width + 3 * wide) * 2,
+            bytes_accessed=3 * width * wide * 2 + count * (3 * full + 2 * width + 3 * wide) * 2,
             transcendentals=count * wide,
         ),
-    )(places, rows, cot, widen, fold, *carries, *flat)
-
-
-def output_kernel(across, places_ref, order_ref, first_ref, second_ref, *refs):
-    firsts, seconds = refs[:across], refs[across : 2 * across]
-    out_ref, first_w, second_w, sems = refs[2 * across :]
-    extra = second_w.shape[1]
-    pieces = [[(r, None) for r in firsts], [(r, 2 * extra) for r in seconds]]
-    load_weights(places_ref, pieces, (first_w, second_w), sems)
-    out_ref[0] = (mm_t(first_ref[...], first_w[...]) + mm_t(second_ref[...], second_w[...])).astype(bf16)
-
-
-def run_output(places, order, size, first, second, first_w, second_w):
-    across = len(first_w)
-    planes, block, cols = first_w[0].shape
-    width = planes * across * block
-    extra = second.shape[1]
-    count = first.shape[0]
-
-    def row_block(a):
-        return pl.BlockSpec((size, a.shape[1]), lambda i, p, o: (i, 0))
-
-    return pl.pallas_call(
-        lambda *refs: output_kernel(across, *refs),
-        grid_spec=pltpu.PrefetchScalarGridSpec(
-            num_scalar_prefetch=2,
-            grid=(count // size,),
-            in_specs=[row_block(first), row_block(second)]
-            + [pl.BlockSpec(memory_space=pl.ANY)] * (2 * across),
-            out_specs=pl.BlockSpec((1, size, width), lambda i, p, o: (o[i], 0, 0)),
-            scratch_shapes=[
-                pltpu.VMEM((width, cols), bf16),
-                pltpu.VMEM((width, extra), bf16),
-                pltpu.SemaphoreType.DMA((2 * across * planes,)),
-            ],
-        ),
-        out_shape=jax.ShapeDtypeStruct((count // size, size, width), bf16),
-        compiler_params=pltpu.CompilerParams(
-            vmem_limit_bytes=VMEM_BYTES, dimension_semantics=("arbitrary",)
-        ),
-        cost_estimate=pl.CostEstimate(
-            flops=2 * count * width * (cols + extra),
-            bytes_accessed=2 * (width + count) * (cols + extra) + 2 * count * width,
-            transcendentals=0,
-        ),
-    )(places, order, first, second, *first_w, *second_w)
-
-
-def copy_kernel(order_ref, source_ref, target_ref):
-    target_ref[...] = source_ref[0]
-
-
-def take_blocks(blocks, order):
-    count, size, width = blocks.shape
-    return pl.pallas_call(
-        copy_kernel,
-        grid_spec=pltpu.PrefetchScalarGridSpec(
-            num_scalar_prefetch=1,
-            grid=(count,),
-            in_specs=[pl.BlockSpec((1, size, width), lambda i, o: (o[i], 0, 0))],
-            out_specs=pl.BlockSpec((size, width), lambda i, o: (i, 0)),
-        ),
-        out_shape=jax.ShapeDtypeStruct((count * size, width), blocks.dtype),
-        cost_estimate=pl.CostEstimate(
-            flops=0, bytes_accessed=4 * blocks.size, transcendentals=0
-        ),
-    )(order, blocks)
-
-
-def term_kernel(groups, *refs):
-    out_ref = refs[-1]
-    side, block, cols = out_ref.shape[0], out_ref.shape[2], 0
-    for pairs in groups:
-        total = None
-        for left, right in pairs:
+    )(places, order, rows, cot, widen, fold, *extra, *flat)
+
+
+def term_kernel(sets, *refs):
+    out_refs = refs[len(refs) - len(sets) :]
+    for groups, out_ref in zip(sets, out_refs):
+        side, block, cols = out_ref.shape[0], out_ref.shape[2], 0
+        for left, right in groups:
             part = t_mm(refs[left][...], refs[right][...])
-            total = part if total is None else total + part
-        wide = total.shape[1]
-        out_ref[:, 0, :, cols : cols + wide] = total.astype(bf16).reshape(side, block, wide)
-        cols += wide
-
-
-def run_terms(groups, width, planes, across):
+            wide = part.shape[1]
+            out_ref[:, 0, :, cols : cols + wide] = part.astype(bf16).reshape(side, block, wide)
+            cols += wide
+
+
+def run_terms(sets, width, planes, across):
     block = width // (planes * across)
     side = max(1, LANES // block)
-    arrays, numbers = [], []
+    arrays, lefts = [], set()
 
     def number(a):
         for k, b in enumerate(arrays):
@@ -337,13 +295,10 @@
         arrays.append(a)
         return len(arrays) - 1
 
-    lefts = set()
-    for pairs in groups:
-        for left, right in pairs:
-            lefts.add(number(left))
-    numbers = [[(number(left), number(right)) for left, right in pairs] for pairs in groups]
-    wide = sum(pairs[0][1].shape[1] for pairs in groups)
-    steps = planes * across // side
+    numbers = [[(number(left), number(right)) for left, right in pairs] for pairs in sets]
+    for pairs in numbers:
+        lefts.update(left for left, _ in pairs)
+    wides = [sum(right.shape[1] for _, right in pairs) for pairs in sets]
     per_plane = across // side
 
     def spec(k, a):
@@ -351,21 +306,22 @@
             return pl.BlockSpec((a.shape[0], side * block), lambda i: (0, i))
         return pl.BlockSpec(a.shape, lambda i: (0, 0))
 
-    flops = sum(2 * l.shape[0] * width * r.shape[1] for pairs in groups for l, r in pairs)
+    flops = sum(2 * l.shape[0] * width * r.shape[1] for pairs in sets for l, r in pairs)
     return pl.pallas_call(
         lambda *refs: term_kernel(numbers, *refs),
-        grid=(steps,),
+        grid=(planes * across // side,),
         in_specs=[spec(k, a) for k, a in enumerate(arrays)],
-        out_specs=pl.BlockSpec(
-            (side, 1, block, wide), lambda i: (i % per_plane, i // per_plane, 0, 0)
-        ),
-        out_shape=jax.ShapeDtypeStruct((across, planes, block, wide), bf16),
+        out_specs=[
+            pl.BlockSpec((side, 1, block, wide), lambda i: (i % per_plane, i // per_plane, 0, 0))
+            for wide in wides
+        ],
+        out_shape=[jax.ShapeDtypeStruct((across, planes, block, wide), bf16) for wide in wides],
         compiler_params=pltpu.CompilerParams(
             vmem_limit_bytes=VMEM_BYTES, dimension_semantics=("arbitrary",)
         ),
         cost_estimate=pl.CostEstimate(
             flops=flops,
-            bytes_accessed=sum(a.size * 2 for a in arrays) + width * wide * 2,
+            bytes_accessed=sum(a.size * 2 for a in arrays) + width * sum(wides) * 2,
             transcendentals=0,
         ),
     )(*arrays)
@@ -482,10 +438,11 @@
     )
     qkv_own = net.exchange_z(qkv_own)
     starts = [min(k * window, inner - window) for k in range(PLANES)]
-    plans = [[(0, j, s) for j in range(local_experts)] for s in starts]
-    down_cut, gate_cut, up_cut = [
-        cut_columns([w], plans, window) for w in (expert_down, expert_gate, expert_up)
-    ]
+    routed_cut = cut_columns(
+        [expert_gate, expert_up, expert_down],
+        [[(k, j, s) for k in range(3) for j in range(local_experts)] for s in starts],
+        window,
+    )
     shared_cut = cut_columns(
         [shared_gate_weight, shared_up_weight, shared_down_weight],
         [
@@ -495,8 +452,8 @@
         ],
         window,
     )
-    cot_all = lax.all_gather(cot, GROUP)
-    down_own = net.exchange_z(after(down_cut, qkv_own))
+    cot_all = lax.all_gather(after(cot, qkv_own), TILES)
+    routed_own = net.exchange_z(after(routed_cut, qkv_own))
     if across == 2 and yrows == 2:
         half = PLANES // 2
         from_x = net.turn(qkv_own, "x", 1)
@@ -504,7 +461,6 @@
         across_both = jnp.concatenate(
             [net.turn(from_y[:half], "x", 1), net.turn(from_x[half:], "y", 1)], axis=0
         )
-        across_both = after(across_both, down_own)
         qkv_w = net.place_rows(
             [
                 net.place_rows([qkv_own, from_x], "x", 1),
@@ -516,7 +472,6 @@
     else:
         qkv_w = net.place_rows(net.gather_x(qkv_own), "x", 1)
         qkv_w = net.place_rows([net.turn(qkv_w, "y", t) if t else qkv_w for t in range(yrows)], "y", 2)
-    gate_own = net.exchange_z(after(gate_cut, qkv_w))
     qkv_w = net.place_rows([qkv_w, net.turn(qkv_w, "c", 1)], "c", 3)
     qkv_w = qkv_w.reshape(width, 3 * head_cols + LANES)
     small = qkv_w[:, 3 * head_cols :]
@@ -537,7 +492,7 @@
         ],
         axis=1,
     )
-    out_w = jnp.concatenate([output_weight, biases], axis=1)
+    out_w = after(jnp.concatenate([output_weight, biases], axis=1), qkv_own)
     out_w = net.place_rows(net.gather_x(out_w), "x", 0)
     out_w = net.place_rows([out_w, net.turn(out_w, "y", 1)], "y", 1)
     out_w = net.place_rows([out_w, net.turn(out_w, "c", 1)], "c", 2)
@@ -574,7 +529,20 @@
         + net.behind("c", block_c)
     ).reshape(-1)
     block_order = block_order.astype(jnp.int32)
-    places = net.behind("x", jnp.arange(across)).astype(jnp.int32)
+    tile_order = (
+        net.behind("c", jnp.arange(PAIR))[:, None] * PLANES
+        + net.behind("z", jnp.arange(PLANES))[None, :]
+    )
+    tile_order = tile_order.reshape(-1).astype(jnp.int32)
+    tile = yrows * rows
+    places = jnp.concatenate([net.behind("x", jnp.arange(across)), iy[None]]).astype(jnp.int32)
+
+    route_ids = routes.reshape(rows, top_count)
+    chosen = (route_ids[:, :, None] == jnp.arange(num_experts)[None, None, :]) & valid[
+        :, None, None
+    ]
+    chosen_any = jnp.sum(chosen.astype(f32), axis=1)
+    counts = jnp.sum(chosen_any, axis=0)
 
     hidden_rows = jnp.concatenate(tok_blocks, axis=0)
     hidden_f = hidden_rows.astype(f32)
@@ -601,13 +569,22 @@
         .reshape(group_rows, head_cols)
     )
     values_own = qkv_pre[:, 2 * head_cols :].astype(bf16)
-    keys_values = net.gather_x(jnp.concatenate([keys_own, values_own], axis=1))
+    count_rows = jnp.zeros((16, 2 * head_cols), f32).at[0, :num_experts].set(counts)
+    keys_values = net.gather_x(
+        jnp.concatenate(
+            [
+                jnp.concatenate([keys_own, values_own], axis=1),
+                count_rows.astype(bf16),
+            ],
+            axis=0,
+        )
+    )
+    counts_x = sum(kv[group_rows, :num_experts].astype(f32) for kv in keys_values)
+    keys_values = [kv[:group_rows] for kv in keys_values]
     key_pos = jnp.concatenate(
         [query_pos + (net.behind("x", t) - ix) * rows for t in range(across)]
     )
-    all_kv = after(jnp.concatenate(keys_values, axis=0), gate_own)
-    up_own = net.exchange_z(after(up_cut, all_kv))
-    cot_group = take_blocks(cot_all.reshape(-1, rows, width), block_order)
+    all_kv = jnp.concatenate(keys_values, axis=0)
     keys_all = all_kv[:, :head_cols].reshape(-1, heads, HD)
     values_all = all_kv[:, head_cols:].reshape(-1, heads, HD)
     scores = jnp.einsum("qhd,khd->hqk", queries, keys_all, preferred_element_type=f32) * scale
@@ -617,9 +594,8 @@
     weights_low = attn_weights.astype(bf16)
     mixed = jnp.einsum("hqk,khd->qhd", weights_low, values_all, preferred_element_type=f32)
     mixed = mixed.astype(bf16).reshape(group_rows, head_cols)
-    down_pieces = net.gather_x(down_own)
-    mixed = after(mixed, *down_pieces)
     branch = mm(mixed, out_w).astype(bf16).reshape(PLANES, rows, width)
+    routed_parts = net.gather_x(after(routed_own, branch))
     resid = token_rows
     for part in net.scatter_z(*[branch[s] for s in range(PLANES)]):
         resid = resid + part.astype(f32)
@@ -628,11 +604,6 @@
     normed_mix = (resid * mix_inv * mixer_gain_f).astype(bf16)
     logits = mm(normed_mix, router_full)
     probs = jax.nn.softmax(logits, axis=-1)
-    route_ids = routes.reshape(rows, top_count)
-    chosen = (route_ids[:, :, None] == jnp.arange(num_experts)[None, None, :]) & valid[
-        :, None, None
-    ]
-    chosen_any = jnp.sum(chosen.astype(f32), axis=1)
     gates = probs * chosen_any
     switch = jax.nn.sigmoid(mm(normed_mix, switch_full[:, None]))
     gate_count = num_experts + 1
@@ -642,16 +613,16 @@
         return [high.astype(bf16), (value - high).astype(bf16)]
 
     parts = two_parts(jnp.concatenate([gates, switch * live], axis=1))
-    parts += [chosen_any.astype(bf16)] + two_parts(probs * live)
+    first_row = (jnp.arange(rows) == 0).astype(f32)[:, None]
+    parts += two_parts(first_row * counts_x[None]) + two_parts(probs * live)
     extra_at = 2 * gate_count
-    extra_count = 3 * num_experts
+    extra_count = 4 * num_experts
     parts.append(jnp.zeros((rows, LANES - extra_at - extra_count), bf16))
     mix_blocks = net.gather_z(jnp.concatenate([normed_mix] + parts, axis=1))
-    mix_blocks = [after(b, up_own) for b in mix_blocks]
+    mix_blocks = mix_blocks[:1] + [after(b, *routed_parts) for b in mix_blocks[1:]]
     shared_own = net.exchange_group(after(shared_cut, *mix_blocks))
     shared_own = shared_own.reshape(PLANES, weight_rows, 3 * window)
-    weight_parts = [net.gather_x(gate_own), net.gather_x(up_own), down_pieces]
-    shared_parts = [net.gather_x(shared_own)]
+    shared_parts = net.gather_x(shared_own)
     mix_group = gather_rows(mix_blocks)
 
     block_sums = jnp.sum(
@@ -662,12 +633,6 @@
     )
     block_sums = jnp.zeros_like(block_sums).at[block_order].set(block_sums)
     sums = jnp.sum(block_sums.reshape(-1, extra_count), axis=0, keepdims=True)
-    sums = jnp.sum(net.place_rows(net.gather_x(sums), "x", 0)[:, 0], axis=0)
-    count_all = sums[:num_experts]
-    mass_all = sums[num_experts : 2 * num_experts] + sums[2 * num_experts :]
-    fraction = count_all / (top_count * all_slots)
-    balance_loss = (num_experts * jnp.sum(fraction * mass_all / all_slots)).reshape(1)
-
     column = jnp.arange(window)
     fresh = column + jnp.minimum(iz * window, inner - window) >= iz * window
     unit_at = jnp.concatenate(
@@ -684,42 +649,68 @@
     fold = ((lane[None] == unit_at[:, None]) & fresh[:, None]).astype(bf16)
     split = local_experts * window
     routed = run_experts(
-        places, mix_group, cot_group, widen[:, :split], fold[:split], weight_parts
-    )
+        places,
+        tile_order,
+        tile,
+        mix_group,
+        cot_all.reshape(-1, tile, width),
+        widen[:, :split],
+        fold[:split],
+        [routed_parts],
+    )
+    cot_group = routed[4]
+    count_all = sums[0, :num_experts] + sums[0, num_experts : 2 * num_experts]
+    mass_x = sums[0, 2 * num_experts : 3 * num_experts] + sums[0, 3 * num_experts :]
+    fraction = count_all / (top_count * all_slots)
     shared = run_experts(
-        places, mix_group, cot_group, widen[:, split:], fold[split:], shared_parts, routed[0]
-    )
+        places,
+        tile_order,
+        tile,
+        mix_group,
+        cot_group,
+        widen[:, split:],
+        fold[split:],
+        [shared_parts, routed_parts],
+        routed[0],
+        routed[1],
+    )
+    out_sum = lax.psum_scatter(
+        shared[4].reshape(-1, rows, width), TILES, scatter_dimension=0, tiled=True
+    )[0]
     back = shared[0].reshape(PAIR, PLANES, yrows, rows, -1)
     pair = add_low(back[0], net.turn(back[1], "c", 1))
     kept_far = row_sum(pair[1:3])
     kept_near = row_sum(jnp.stack([pair[0], pair[3]]))
 
-    shared_term = run_terms(
-        [
-            [(after(mix_group, pair), shared[2])],
-            [(after(mix_group, pair), shared[3])],
-            [(after(cot_group, pair), shared[1])],
-        ],
+    mix_late = after(mix_group, pair)
+    (shared_term,) = run_terms(
+        [[(mix_late, shared[2]), (mix_late, shared[3]), (after(cot_group, pair), shared[1])]],
         width,
         PLANES,
         across,
     )
-    mix_late = after(mix_group, shared_term, kept_far)
-    pair_term = run_terms(
-        [[(mix_late, routed[2])], [(mix_late, routed[3])]], width, PLANES, across
-    )
-    down_term = run_terms(
-        [[(after(cot_group, pair_term, kept_near), routed[1])]], width, PLANES, across
+
+    def over_x(term, *until):
+        total = net.pick(term, ix, 0).astype(f32)
+        for t in range(1, across):
+            got = net.turn(net.pick(term, net.ahead("x", t), 0), "x", t)
+            total = total + (after(got, *until) if until else got).astype(f32)
+        return total.astype(bf16)
+
+    shared_sent = over_x(shared_term)
+    shared_sorted = net.exchange_group(shared_sent.reshape(-1, shard, 3 * window))
+    mix_late = after(mix_group, shared_sent, kept_far)
+    (routed_term,) = run_terms(
+        [[(mix_late, routed[2]), (mix_late, routed[3]), (cot_group, routed[1])]],
+        width,
+        PLANES,
+        across,
     )
     grad_sum = sum(
-        part.astype(f32)
+        after(part, routed_term).astype(f32)
         for part in net.scatter_z(kept_near[0], kept_far[0], kept_far[1], kept_near[1])
     )
-    grad_sum = after(grad_sum, down_term)
-    scattered = [
-        net.scatter_axis(term, "x", 0).astype(bf16)
-        for term in (shared_term, pair_term, down_term)
-    ]
+
     grad_gates = grad_sum[:, width : width + num_experts]
     grad_switch = grad_sum[:, width + num_experts : width + gate_count]
     grad_switch_logit = grad_switch * live * switch * (1.0 - switch)
@@ -736,23 +727,12 @@
     grad_resid = grad_final + grad_mix_rows
     grad_branch = grad_resid.astype(bf16)
     branch_group = jnp.concatenate(net.gather_z(grad_branch), axis=0)
-    out_blocks = run_output(
-        places,
-        block_order,
-        rows,
-        after(routed[1], grad_branch),
-        shared[1],
-        down_pieces,
-        shared_parts[0],
-    )
-    branch_group = after(branch_group, out_blocks)
-    out_sum = lax.psum_scatter(out_blocks, GROUP, scatter_dimension=0, tiled=True)[0]
-    sorted_grads = [net.exchange_group(after(scattered[0], branch_group).reshape(-1, shard, 3 * window))]
-    for part in scattered[1:]:
-        sorted_grads.append(net.exchange_z(after(part, sorted_grads[-1])))
+    branch_group = after(branch_group, out_sum, shared_sorted)
 
     grad_mixed = mm_t(branch_group, out_w).astype(bf16).reshape(group_rows, heads, HD)
     grad_attn = jnp.einsum("qhd,khd->hqk", grad_mixed, values_all, preferred_element_type=f32)
+    routed_sent = over_x(routed_term, grad_attn)
+    routed_sorted = net.exchange_z(routed_sent)
     delta = jnp.sum(attn_weights * grad_attn, axis=-1, keepdims=True)
     grad_scores = (attn_weights * (grad_attn - delta)).astype(bf16)
     grad_keys = (
@@ -762,6 +742,7 @@
     grad_kv = jnp.concatenate(
         [grad_keys.reshape(-1, head_cols), grad_values.reshape(-1, head_cols)], axis=1
     ).reshape(across, group_rows, 2 * head_cols)
+    grad_kv = after(grad_kv, routed_sent)
     grad_kv_own = grad_kv[0]
     for t in range(1, across):
         grad_kv_own = grad_kv_own + net.turn(grad_kv[t].astype(bf16), "x", -t).astype(f32)
@@ -778,43 +759,6 @@
     )
     grad_value_pre = grad_kv_own[:, head_cols:].astype(bf16)
     grad_qkv = jnp.concatenate([grad_query_pre, grad_key_pre, grad_value_pre], axis=1)
-    grad_qkv = after(grad_qkv, sorted_grads[0])
-    grad_normed_part = mm_t(grad_qkv, qkv_w)
-    gain_part = jnp.sum(grad_normed_part * hidden_f * attn_inv_group, axis=0)
-    normed_part_low = grad_normed_part.astype(bf16).reshape(PLANES, rows, width)
-    grad_normed_attn = jnp.zeros((rows, width), f32)
-    for part in net.scatter_z(*[normed_part_low[s] for s in range(PLANES)]):
-        grad_normed_attn = grad_normed_attn + part.astype(f32)
-    attn_inv = attn_inv_group[:rows]
-    grad_attn_rows, _ = norm_back(grad_normed_attn, token_rows, attn_inv, attn_gain_f)
-    grad_tokens = (grad_resid + grad_attn_rows).astype(bf16).reshape(1, rows, width)
-
-    layer_out = ((resid + out_sum.astype(f32)) * live).astype(bf16)
-
-    def unit_columns(by_plane, j):
-        cols = [by_plane[k, :, j * window : (j + 1) * window] for k in range(PLANES)]
-        used = window * (PLANES - 1)
-        cols[-1] = cols[-1][:, window - (inner - used) :]
-        return jnp.concatenate(cols, axis=1)
-
-    def routed_grads(by_plane):
-        return jnp.stack(
-            [unit_columns(by_plane, j) for j in range(local_experts)]
-        ).astype(f32)
-
-    grad_expert_gate = routed_grads(sorted_grads[1][:, :, :split])
-    grad_expert_up = routed_grads(sorted_grads[1][:, :, split:])
-    grad_expert_down = routed_grads(sorted_grads[2])
-    shared_back = sorted_grads[0].reshape(PLANES, groups, shard, 3 * window)
-    shared_grads = []
-    for k in range(3):
-        cols = []
-        for e in range(groups):
-            for z in range(PLANES):
-                first = k * window + (window * PLANES - inner if z == PLANES - 1 else 0)
-                cols.append(shared_back[z, e, :, first : (k + 1) * window])
-        shared_grads.append(jnp.concatenate(cols, axis=1).astype(f32))
-
     def to_rows(part, dims):
         part = net.scatter_axis(part, "c", dims - 1).astype(bf16)
         cut = part.shape[-1] // (2 * LANES) * LANES
@@ -828,30 +772,65 @@
         second = net.scatter_axis(second, "y", dims - 3).astype(bf16)
         return jnp.concatenate([first, second], axis=-1)
 
-    grad_out_w = t_mm(mixed, branch_group).astype(bf16)
-    grad_output_weight = to_rows(
-        grad_out_w.reshape(across, yrows, PAIR, shard, width), 3
-    ).astype(f32)
     row_terms = jnp.concatenate(
         [
             t_mm(grad_logits, normed_mix),
             jnp.sum(grad_switch_logit * normed_mix.astype(f32), axis=0)[None],
             grad_mixer_gain[None],
-            gain_part[None],
-            jnp.zeros((16 - num_experts - 3, width), f32),
+            jnp.zeros((16 - num_experts - 2, width), f32),
         ],
         axis=0,
     ).astype(bf16)
-    qkv_term = run_terms(
-        [[(normed_attn, grad_qkv)], [(row_terms, jnp.eye(16, LANES, dtype=bf16))]],
+    (qkv_term,) = run_terms(
+        [[(normed_attn, grad_qkv), (row_terms, jnp.eye(16, LANES, dtype=bf16))]],
         width,
         PLANES,
         across,
     )
     qkv_rows = to_rows(
-        jnp.swapaxes(qkv_term.reshape(across, PLANES, yrows, PAIR, shard, -1), 0, 1), 4
-    )
-    qkv_planes = net.exchange_z(qkv_rows)
+        jnp.swapaxes(qkv_term.reshape(across, PLANES, yrows, PAIR, shard, -1), 0, 1),
+        4,
+    )
+    grad_normed_part = mm_t(after(grad_qkv, qkv_term), qkv_w)
+    normed_part_low = grad_normed_part.astype(bf16).reshape(PLANES, rows, width)
+    grad_normed_attn = jnp.zeros((rows, width), f32)
+    for part in net.scatter_z(*[normed_part_low[s] for s in range(PLANES)]):
+        grad_normed_attn = grad_normed_attn + after(part, qkv_rows, routed_sorted).astype(f32)
+    attn_inv = attn_inv_group[:rows]
+    grad_attn_rows, _ = norm_back(grad_normed_attn, token_rows, attn_inv, attn_gain_f)
+    grad_tokens = (grad_resid + grad_attn_rows).astype(bf16).reshape(1, rows, width)
+
+    layer_out = ((resid + out_sum.astype(f32)) * live).astype(bf16)
+
+    def unit_columns(by_plane, j):
+        cols = [by_plane[k, :, j * window : (j + 1) * window] for k in range(PLANES)]
+        used = window * (PLANES - 1)
+        cols[-1] = cols[-1][:, window - (inner - used) :]
+        return jnp.concatenate(cols, axis=1)
+
+    def routed_grads(by_plane):
+        return jnp.stack(
+            [unit_columns(by_plane, j) for j in range(local_experts)]
+        ).astype(f32)
+
+    grad_expert_gate, grad_expert_up, grad_expert_down = [
+        routed_grads(routed_sorted[:, :, k * split : (k + 1) * split]) for k in range(3)
+    ]
+    shared_back = shared_sorted.reshape(PLANES, groups, shard, 3 * window)
+    shared_grads = []
+    for k in range(3):
+        cols = []
+        for e in range(groups):
+            for z in range(PLANES):
+                first = k * window + (window * PLANES - inner if z == PLANES - 1 else 0)
+                cols.append(shared_back[z, e, :, first : (k + 1) * window])
+        shared_grads.append(jnp.concatenate(cols, axis=1).astype(f32))
+
+    grad_out_w = t_mm(mixed, branch_group).astype(bf16)
+    grad_output_weight = to_rows(
+        grad_out_w.reshape(across, yrows, PAIR, shard, width), 3
+    ).astype(f32)
+    qkv_planes = net.exchange_z(after(qkv_rows, routed_sorted))
     grad_qkv_weights = [
         jnp.concatenate(
             [qkv_planes[k, :, j * head_cols : (j + 1) * head_cols] for k in range(PLANES)], axis=1
@@ -860,14 +839,26 @@
     ]
 
     row_grads = jnp.sum(
-        qkv_planes[:, :, 3 * head_cols : 3 * head_cols + num_experts + 3].astype(f32), axis=0
-    )
+        qkv_planes[:, :, 3 * head_cols : 3 * head_cols + num_experts + 2].astype(f32), axis=0
+    )
+
+    gain_grad = sum(
+        jnp.sum(w.astype(f32) * g, axis=1)
+        for w, g in zip((query_weight, key_weight, value_weight), grad_qkv_weights)
+    ) / attention_gain.astype(f32)
 
     bias_part = jnp.sum(grad_qkv.astype(f32), axis=0).reshape(3, across, yrows, PAIR, shard)
+    bias_part = after(bias_part, grad_normed_attn)
     bias_part = jnp.transpose(bias_part, (1, 2, 3, 0, 4))
     bias_part = net.scatter_axis(bias_part, "c", 2)
     bias_part = net.scatter_axis(bias_part, "y", 1)
+    mass_row = jnp.broadcast_to(
+        jnp.pad(mass_x, (0, shard - num_experts))[None, None], (across, 1, shard)
+    )
+    bias_part = jnp.concatenate([bias_part, mass_row], axis=1)
     bias_part = net.scatter_axis(bias_part, "x", 0)
+    mass_all = bias_part[3, :num_experts]
+    balance_loss = (num_experts * jnp.sum(fraction * mass_all / all_slots)).reshape(1)
     return (
         layer_out.reshape(1, rows, width),
         balance_loss,
@@ -879,7 +870,7 @@
         bias_part[0],
         bias_part[1],
         bias_part[2],
-        row_grads[:, num_experts + 2],
+        gain_grad,
         row_grads[:, :num_experts],
         row_grads[:, num_experts],
         row_grads[:, num_experts + 1],

time: 1100 us -> 1000 us (0.909)
  Pallas kernels: 206 us -> 165 us
  waiting for transfers between devices: 441 us -> 412 us
    all_to_all x7 -> x4, waiting for transfers between devices: 112 us -> 66.8 us  [exchange_z(): return lax.all_to_all(value, 'z', split_axis=0, concat_axis=0, tiled=True)]
    pallas_call x8 -> x5, Pallas kernels: 189 us -> 152 us  [the longest x2 95.9 us: run_experts(): pl.pallas_call(lambda *refs: expert_kernel(second, across, *refs), grid_s...]
    dynamic_update_slice x16 -> x13, local copies, waits for them, and re-layouts: 18.2 us -> 4.59 us  [place_rows(): lax.dynamic_update_slice_in_dim(buffer, jnp.expand_dims(block, dim), self...]
    all_to_all x7 -> x4, starting transfers between devices: 31.1 us -> 18.7 us  [exchange_z(): return lax.all_to_all(value, 'z', split_axis=0, concat_axis=0, tiled=True)]
    all_to_all x2, waiting for transfers between devices: 0.01 us -> 11.3 us  [exchange_group(): return lax.all_to_all(value, GROUP, split_axis=0, concat_axis=0, tiled=True)]
    concatenate x1 -> x5, local copies, waits for them, and re-layouts: 1.75 us -> 12.8 us  [the longest x4 12.7 us: per_device(): jnp.concatenate([grad_keys.reshape(-1, head_cols), grad_values.reshape(-1...]
    ppermute x58 -> x54, waiting for transfers between devices: 329 us -> 334 us  [turn(): lax.ppermute(value, axis, [(i, (i + steps) % size) for i in range(size)])]
    ppermute x58 -> x54, starting transfers between devices: 77.2 us -> 80.9 us  [turn(): lax.ppermute(value, axis, [(i, (i + steps) % size) for i in range(size)])]
  transfers between devices with their start and end apart: 69 -> 62, of which waited for: 30 -> 32; matrix products, arithmetic and copies ran while one was open for 24% -> 25% of each run, Pallas kernels for 16% -> 12%
where the time goes in v3:
time: 1000 us; the launch traced here: 989 us
  waiting for transfers between devices  412 us (41%)
  Pallas kernels  165 us (16%)
  local copies, waits for them, and re-layouts  137 us (14%)
  starting transfers between devices  124 us (12%)
  other arithmetic  91.2 us (9%)
  matrix products  38.1 us (4%)
  between operations  21.5 us (2%)
    ppermute x54, waiting for transfers between devices, turn(): lax.ppermute(value, axis, [(i, (i + steps) % size) for i in range(size)])  334 us
    pallas_call x2, Pallas kernels, run_experts(): pl.pallas_call(lambda *refs: expert_kernel(second, across, *refs), grid_s...  95.9 us
    ppermute x54, starting transfers between devices, turn(): lax.ppermute(value, axis, [(i, (i + steps) % size) for i in range(size)])  80.9 us
    all_to_all x4, waiting for transfers between devices, exchange_z(): return lax.all_to_all(value, 'z', split_axis=0, concat_axis=0, tiled=True)  66.8 us
    pallas_call x3, Pallas kernels, run_terms(): pl.pallas_call(lambda *refs: term_kernel(numbers, *refs), grid=(planes *...  56.4 us
    unnamed x197, local copies, waits for them, and re-layouts  41.3 us
  transfers between devices with their start and end apart: 62, of which 32 were waited for; matrix products, arithmetic and copies ran while one was open for 25% of the time, Pallas kernels for 12%

profile of v3, /device:TPU:0, one launch (start us, length us, event | category | flops | bytes accessed | tf_op | source)
XLA Modules:
  0.0 988.7 jit_solution(7953637817784973797)
XLA Ops:
  49.7 26.8 %all-to-all-done = bf16[4,64,1664]{2,1,0:T(8,128)(2,1)} async-done(((bf16[4,64,1664]{2,1,0:T(8,128)(2,1)}), bf16[4,64,1664]{2,1,0:T(8,128)(2,1)}, u32[]{:S(2)}, u32[]{:S(2)}) %all-to-all-start) | async-done | bytes 852000 | tf_op jit(solution)/shard_map/all_to_all | solution.py:109
  88.9 23.2 %collective-permute-done.4 = bf16[4,64,1664]{2,1,0:T(8,128)(2,1)S(1)} collective-permute-done((bf16[4,64,1664]{2,1,0:T(8,128)(2,1)}, bf16[4,64,1664]{2,1,0:T(8,128)(2,1)S(1)}, u32[]{:S(2)}, u32[]{:S(2)}) %collective-permute-start.4) | collective-permute-done | bytes 852000 | tf_op jit(solution)/shard_map/ppermute | solution.py:85
  121.0 10.6 %collective-permute-done.6 = bf16[2,64,1664]{2,1,0:T(8,128)(2,1)S(1)} collective-permute-done((bf16[2,64,1664]{2,1,0:T(8,128)(2,1)S(1)}, bf16[2,64,1664]{2,1,0:T(8,128)(2,1)S(1)}, u32[]{:S(2)}, u32[]{:S(2)}) %collective-permute-start.6) | collective-permute-done | bytes 426016 | tf_op jit(solution)/shard_map/ppermute | solution.py:85
  169.2 20.5 %collective-permute-done.11 = bf16[528,1024]{1,0:T(8,128)(2,1)} collective-permute-done((bf16[528,1024]{1,0:T(8,128)(2,1)}, bf16[528,1024]{1,0:T(8,128)(2,1)}, u32[]{:S(2)}, u32[]{:S(2)}) %collective-permute-start.11) | collective-permute-done | bytes 1081376 | tf_op jit(solution)/shard_map/ppermute | solution.py:85
  199.9 38.2 %all-to-all-done.1.refs_6_.refs_10_ = bf16[4,256,2304]{2,1,0:T(8,128)(2,1)} async-done(((bf16[4,256,2304]{2,1,0:T(8,128)(2,1)}), bf16[4,256,2304]{2,1,0:T(8,128)(2,1)}, u32[]{:S(2)}, u32[]{:S(2)}) %all-to-all-start.1) | async-done | bytes 4718624 | tf_op jit(solution)/shard_map/all_to_all | solution.py:109
  249.7 10.4 %collective-permute-done.12 = bf16[128,2048]{1,0:T(8,128)(2,1)S(1)} collective-permute-done((bf16[128,2048]{1,0:T(8,128)(2,1)S(1)}, bf16[128,2048]{1,0:T(8,128)(2,1)S(1)}, u32[]{:S(2)}, u32[]{:S(2)}) %collective-permute-start.12) | collective-permute-done | bytes 524320 | tf_op jit(solution)/shard_map/ppermute | solution.py:85
  260.2 29.4 %collective-permute-done.13 = bf16[128,2048]{1,0:T(8,128)(2,1)S(1)} collective-permute-done((bf16[128,2048]{1,0:T(8,128)(2,1)S(1)}, bf16[128,2048]{1,0:T(8,128)(2,1)S(1)}, u32[]{:S(2)}, u32[]{:S(2)}) %collective-permute-start.13) | collective-permute-done | bytes 524320 | tf_op jit(solution)/shard_map/ppermute | solution.py:85
  310.9 30.4 %collective-permute-done.17.refs_7_.refs_11_ = bf16[4,256,2304]{2,1,0:T(8,128)(2,1)} collective-permute-done((bf16[4,256,2304]{2,1,0:T(8,128)(2,1)}, bf16[4,256,2304]{2,1,0:T(8,128)(2,1)}, u32[]{:S(2)}, u32[]{:S(2)}) %collective-permute-start.17) | collective-permute-done | bytes 4718624 | tf_op jit(solution)/shard_map/ppermute | solution.py:85
  365.4 22.6 %collective-permute-done.20 = bf16[128,2176]{1,0:T(8,128)(2,1)S(1)} collective-permute-done((bf16[128,2176]{1,0:T(8,128)(2,1)S(1)}, bf16[128,2176]{1,0:T(8,128)(2,1)S(1)}, u32[]{:S(2)}, u32[]{:S(2)}) %collective-permute-start.20) | collective-permute-done | bytes 557088 | tf_op jit(solution)/shard_map/ppermute | solution.py:85
  388.0 15.4 %collective-permute-done.22 = bf16[128,2176]{1,0:T(8,128)(2,1)S(1)} collective-permute-done((bf16[128,2176]{1,0:T(8,128)(2,1)S(1)}, bf16[128,2176]{1,0:T(8,128)(2,1)S(1)}, u32[]{:S(2)}, u32[]{:S(2)}) %collective-permute-start.22) | collective-permute-done | bytes 557088 | tf_op jit(solution)/shard_map/ppermute | solution.py:85
  414.8 51.4 %shard_map.357 = (bf16[2048,2176]{1,0:T(8,128)(2,1)}, bf16[2048,768]{1,0:T(8,128)(2,1)}, bf16[2048,768]{1,0:T(8,128)(2,1)}, bf16[2048,768]{1,0:T(8,128)(2,1)}, bf16[2048,2048]{1,0:T(8,128)(2,1)}) custom-call(s32[3]{0:T(128)} %pad_add_fusion.2.refs_0_, s32[8]{0:T(128)} %add.638.refs_1_, bf16[2048,2176]{1,0:T(8,128)(2,1)} %constant_dynamic-update-slice_fusion.refs_2_.refs_0_, ...), custom_call_target="tpu_custom_call" | custom-call | flops 32212254720 | bytes 62390272 | tf_op jit(solution)/shard_map/pallas_call | solution.py:238
  467.8 44.4 %shard_map.359 = (bf16[2048,2176]{1,0:T(8,128)(2,1)}, bf16[2048,384]{1,0:T(8,128)(2,1)}, bf16[2048,384]{1,0:T(8,128)(2,1)}, bf16[2048,384]{1,0:T(8,128)(2,1)}, bf16[8,256,2048]{2,1,0:T(8,128)(2,1)}) custom-call(s32[3]{0:T(128)} %pad_add_fusion.2.refs_0_, s32[8]{0:T(128)} %add.638.refs_1_, ...), custom_call_target="tpu_custom_call" | custom-call | flops 16106127360 | bytes 52953088 | tf_op jit(solution)/shard_map/pallas_call | solution.py:238
  536.3 19.9 %shard_map.360 = bf16[2,4,256,1152]{3,2,1,0:T(8,128)(2,1)} custom-call(bf16[2048,2176]{1,0:T(8,128)(2,1)} %constant_dynamic-update-slice_fusion.refs_2_.refs_0_, bf16[2048,384]{1,0:T(8,128)(2,1)} %get-tuple-element.79.refs_1_, bf16[2048,384]{1,0:T(8,128)(2,1)} %get-tuple-element.80.refs_2_, bf16[2048,2048]{1,0:T(8,128)(2,1)} %get-tuple-element.81.refs_3_, ...), custom_call_target="tpu_custom_call" | custom-call | flops 9663676416 | bytes 26738688 | tf_op jit(solution)/shard_map/pallas_call | solution.py:310
  564.7 8.8 collective-permute-start.30
  573.5 23.2 %collective-permute-done.27 = bf16[2,128,2176]{2,1,0:T(8,128)(2,1)S(1)} collective-permute-done((bf16[2,128,2176]{2,1,0:T(8,128)(2,1)S(1)}, bf16[2,128,2176]{2,1,0:T(8,128)(2,1)S(1)}, u32[]{:S(2)}, u32[]{:S(2)}) %collective-permute-start.27) | collective-permute-done | bytes 1114144 | tf_op jit(solution)/shard_map/ppermute | solution.py:85
  601.4 9.6 collective-permute-done.28
  621.2 27.0 %shard_map.361 = bf16[2,4,256,2304]{3,2,1,0:T(8,128)(2,1)} custom-call(bf16[2048,2176]{1,0:T(8,128)(2,1)} %constant_dynamic-update-slice_fusion.refs_2_.refs_0_, bf16[2048,768]{1,0:T(8,128)(2,1)} %get-tuple-element.84.refs_1_, bf16[2048,768]{1,0:T(8,128)(2,1)} %get-tuple-element.85.refs_2_, bf16[2048,2048]{1,0:T(8,128)(2,1)} %get-tuple-element.81.refs_3_, ...), custom_call_target="tpu_custom_call" | custom-call | flops 19327352832 | bytes 36175872 | tf_op jit(solution)/shard_map/pallas_call | solution.py:310
  648.3 32.4 %collective-permute-done.31 = bf16[128,2176]{1,0:T(8,128)(2,1)} collective-permute-done((bf16[128,2176]{1,0:T(8,128)(2,1)}, bf16[128,2176]{1,0:T(8,128)(2,1)}, u32[]{:S(2)}, u32[]{:S(2)}) %collective-permute-start.31) | collective-permute-done | bytes 557088 | tf_op jit(solution)/shard_map/ppermute | solution.py:85
  693.2 11.3 %all-to-all-done.3 = bf16[16,64,1152]{2,1,0:T(8,128)(2,1)} async-done(((bf16[16,64,1152]{2,1,0:T(8,128)(2,1)}), bf16[16,64,1152]{2,1,0:T(8,128)(2,1)}, u32[]{:S(2)}, u32[]{:S(2)}) %all-to-all-start.3) | async-done | bytes 2359328 | tf_op jit(solution)/shard_map/all_to_all | solution.py:132
  742.8 22.2 %collective-permute-done.34 = bf16[128,2048]{1,0:T(8,128)(2,1)S(1)} collective-permute-done((bf16[128,2048]{1,0:T(8,128)(2,1)S(1)}, bf16[128,2048]{1,0:T(8,128)(2,1)S(1)}, u32[]{:S(2)}, u32[]{:S(2)}) %collective-permute-start.34) | collective-permute-done | bytes 524320 | tf_op jit(solution)/shard_map/ppermute | solution.py:85
  773.2 14.2 %collective-permute-done.36 = bf16[4,256,2304]{2,1,0:T(8,128)(2,1)} collective-permute-done((bf16[4,256,2304]{2,1,0:T(8,128)(2,1)}, bf16[4,256,2304]{2,1,0:T(8,128)(2,1)}, u32[]{:S(2)}, u32[]{:S(2)}) %collective-permute-start.36) | collective-permute-done | bytes 4718624 | tf_op jit(solution)/shard_map/ppermute | solution.py:85
  831.0 16.7 %collective-permute-done.37 = bf16[512,1024]{1,0:T(8,128)(2,1)} collective-permute-done((bf16[512,1024]{1,0:T(8,128)(2,1)}, bf16[512,1024]{1,0:T(8,128)(2,1)}, u32[]{:S(2)}, u32[]{:S(2)}) %collective-permute-start.37) | collective-permute-done | bytes 1048608 | tf_op jit(solution)/shard_map/ppermute | solution.py:85
  859.6 9.4 shard_map.362
  913.2 16.1 %collective-permute-done.53 = bf16[64,1024]{1,0:T(8,128)(2,1)S(1)} collective-permute-done((bf16[64,1024]{1,0:T(8,128)(2,1)S(1)}, bf16[64,1024]{1,0:T(8,128)(2,1)S(1)}, u32[]{:S(2)}, u32[]{:S(2)}) %collective-permute-start.53) | collective-permute-done | bytes 131104 | tf_op jit(solution)/shard_map/ppermute | solution.py:85
  (581 shorter events, 432.8 us)
Async XLA Ops:
  22.2 54.4 %all-to-all-start = ((bf16[4,64,1664]{2,1,0:T(8,128)(2,1)}), bf16[4,64,1664]{2,1,0:T(8,128)(2,1)}, u32[]{:S(2)}, u32[]{:S(2)}) async-start(bf16[4,64,1664]{2,1,0:T(8,128)(2,1)} %copy.355), calls=%async_computation | async-start | bytes 1703936 | tf_op jit(solution)/shard_map/all_to_all | solution.py:109
  78.1 160.1 %all-to-all-start.1 = ((bf16[4,256,2304]{2,1,0:T(8,128)(2,1)}), bf16[4,256,2304]{2,1,0:T(8,128)(2,1)}, u32[]{:S(2)}, u32[]{:S(2)}) async-start(bf16[4,256,2304]{2,1,0:T(8,128)(2,1)} %shard_map.356), calls=%async_computation.1 | async-start | bytes 9437184 | tf_op jit(solution)/shard_map/all_to_all | solution.py:109
  83.0 331.8 %all-gather.3.cloned.1.call-start = ((), (), s32[]{:S(2)}) async-start(), calls=%async_computation.8 | async-start | bytes 8912896 | tf_op jit(solution)/shard_map/all_gather | solution.py:455
  88.3 43.9 %collective-permute-start.9 = (bf16[2,64,2176]{2,1,0:T(8,128)(2,1)S(1)}, bf16[2,64,2176]{2,1,0:T(8,128)(2,1)S(1)}, u32[]{:S(2)}, u32[]{:S(2)}) collective-permute-start(bf16[2,64,2176]{2,1,0:T(8,128)(2,1)S(1)} %bitcast_dynamic-update-slice_fusion.9), channel_id=1, source_target_pairs={{0,2},{2,0},{1,3},{3,1},{4,6},{6,4},{5,7},{7,5},{8,10},{10,8},{9,1... | collective-permute-start | bytes 1671176 | tf_op jit(solution)/shard_map/ppermute | solution.py:85
  238.2 103.1 %collective-permute-start.17 = (bf16[4,256,2304]{2,1,0:T(8,128)(2,1)}, bf16[4,256,2304]{2,1,0:T(8,128)(2,1)}, u32[]{:S(2)}, u32[]{:S(2)}) collective-permute-start(bf16[4,256,2304]{2,1,0:T(8,128)(2,1)} %all-to-all-done.1.refs_6_.refs_10_), channel_id=1, source_target_pairs={{0,4},{4,0},{1,5},{5,1},{2,6},{6,2},{3,7},{7,3},{8,12},{12,8},{9,1... | collective-permute-start | bytes 14155784 | tf_op jit(solution)/shard_map/ppermute | solution.py:85
  246.9 42.7 %collective-permute-start.13 = (bf16[128,2048]{1,0:T(8,128)(2,1)S(1)}, bf16[128,2048]{1,0:T(8,128)(2,1)S(1)}, u32[]{:S(2)}, u32[]{:S(2)}) collective-permute-start(bf16[128,2048]{1,0:T(8,128)(2,1)S(1)} %get-tuple-element.322), channel_id=1, source_target_pairs={{0,16},{8,24},{16,0},{24,8},{1,17},{9,25},{17,1},{25,9},{2,18},{10... | collective-permute-start | bytes 1572872 | tf_op jit(solution)/shard_map/ppermute | solution.py:85
  246.9 42.7 %collective-permute-start.14 = (bf16[128,2048]{1,0:T(8,128)(2,1)S(1)}, bf16[128,2048]{1,0:T(8,128)(2,1)S(1)}, u32[]{:S(2)}, u32[]{:S(2)}) collective-permute-start(bf16[128,2048]{1,0:T(8,128)(2,1)S(1)} %get-tuple-element.321), channel_id=1, source_target_pairs={{0,8},{8,16},{16,24},{24,0},{1,9},{9,17},{17,25},{25,1},{2,10},{10... | collective-permute-start | bytes 1572872 | tf_op jit(solution)/shard_map/ppermute | solution.py:85
  295.0 46.2 %collective-permute-start.19 = (bf16[128,2176]{1,0:T(8,128)(2,1)S(1)}, bf16[128,2176]{1,0:T(8,128)(2,1)S(1)}, u32[]{:S(2)}, u32[]{:S(2)}) collective-permute-start(bf16[128,2176]{1,0:T(8,128)(2,1)S(1)} %concatenate.173), channel_id=1, source_target_pairs={{0,16},{8,24},{16,0},{24,8},{1,17},{9,25},{17,1},{25,9},{2,18},{10... | collective-permute-start | bytes 1671176 | tf_op jit(solution)/shard_map/ppermute | solution.py:85
  297.0 44.2 %collective-permute-start.21 = (bf16[128,2176]{1,0:T(8,128)(2,1)S(1)}, bf16[128,2176]{1,0:T(8,128)(2,1)S(1)}, u32[]{:S(2)}, u32[]{:S(2)}) collective-permute-start(bf16[128,2176]{1,0:T(8,128)(2,1)S(1)} %concatenate.173), channel_id=1, source_target_pairs={{0,24},{8,0},{16,8},{24,16},{1,25},{9,1},{17,9},{25,17},{2,26},{10... | collective-permute-start | bytes 1671176 | tf_op jit(solution)/shard_map/ppermute | solution.py:85
  307.9 54.0 %collective-permute-start.15 = (bf16[128,2176]{1,0:T(8,128)(2,1)S(1)}, bf16[128,2176]{1,0:T(8,128)(2,1)}, u32[]{:S(2)}, u32[]{:S(2)}) collective-permute-start(bf16[128,2176]{1,0:T(8,128)(2,1)S(1)} %concatenate.173), channel_id=1, source_target_pairs={{0,2},{2,0},{1,3},{3,1},{4,6},{6,4},{5,7},{7,5},{8,10},{10,8},{9,1... | collective-permute-start | bytes 1671176 | tf_op jit(solution)/shard_map/ppermute | solution.py:85
  342.8 71.1 %all-to-all-start.2 = ((bf16[16,64,1152]{2,1,0:T(8,128)(2,1)}), bf16[16,64,1152]{2,1,0:T(8,128)(2,1)}, u32[]{:S(2)}, u32[]{:S(2)}) async-start(bf16[16,64,1152]{2,1,0:T(8,128)(2,1)} %shard_map.358), calls=%async_computation.2 | async-start | bytes 4718592 | tf_op jit(solution)/shard_map/all_to_all | solution.py:132
  350.5 369.2 %reduce-scatter.2.cloned.1.call-start = ((), (), s32[]{:S(2)}) async-start(), calls=%async_computation.7 | async-start | bytes 8912896 | tf_op jit(solution)/shard_map/reduce_scatter | solution.py:677
  365.3 45.5 %collective-permute-start.23 = (bf16[512,2176]{1,0:T(8,128)(2,1)S(1)}, bf16[512,2176]{1,0:T(8,128)(2,1)S(1)}, u32[]{:S(2)}, u32[]{:S(2)}) collective-permute-start(bf16[512,2176]{1,0:T(8,128)(2,1)S(1)} %pad_maximum_fusion.1), channel_id=1, source_target_pairs={{0,1},{1,0},{2,3},{3,2},{4,5},{5,4},{6,7},{7,6},{8,9},{9,8},{10,11... | collective-permute-start | bytes 6684680 | tf_op jit(solution)/shard_map/ppermute | solution.py:85
  413.9 54.0 %collective-permute-start.25 = (bf16[4,256,1152]{2,1,0:T(8,128)(2,1)}, bf16[4,256,1152]{2,1,0:T(8,128)(2,1)}, u32[]{:S(2)}, u32[]{:S(2)}) collective-permute-start(bf16[4,256,1152]{2,1,0:T(8,128)(2,1)} %bitcast.49.refs_8_), channel_id=1, source_target_pairs={{0,4},{4,0},{1,5},{5,1},{2,6},{6,2},{3,7},{7,3},{8,12},{12,8},{9,1... | collective-permute-start | bytes 7077896 | tf_op jit(solution)/shard_map/ppermute | solution.py:85
  558.1 52.9 %collective-permute-start.28 = (bf16[4,256,1152]{2,1,0:T(8,128)(2,1)S(1)}, bf16[4,256,1152]{2,1,0:T(8,128)(2,1)S(1)}, u32[]{:S(2)}, u32[]{:S(2)}) collective-permute-start(bf16[4,256,1152]{2,1,0:T(8,128)(2,1)S(1)} %dynamic-slice_bitcast_fusion.1), channel_id=1, source_target_pairs={{0,4},{4,0},{1,5},{5,1},{2,6},{6,2},{3,7},{7,3},{8,12},{12,8},{9,1... | collective-permute-start | bytes 7077896 | tf_op jit(solution)/shard_map/ppermute | solution.py:85
  564.7 83.6 %collective-permute-start.30 = (bf16[128,2176]{1,0:T(8,128)(2,1)}, bf16[128,2176]{1,0:T(8,128)(2,1)}, u32[]{:S(2)}, u32[]{:S(2)}) collective-permute-start(bf16[128,2176]{1,0:T(8,128)(2,1)} %get-tuple-element.327), channel_id=1, source_target_pairs={{0,24},{8,0},{16,8},{24,16},{1,25},{9,1},{17,9},{25,17},{2,26},{10... | collective-permute-start | bytes 1671176 | tf_op jit(solution)/shard_map/ppermute | solution.py:85
  573.5 107.1 %collective-permute-start.31 = (bf16[128,2176]{1,0:T(8,128)(2,1)}, bf16[128,2176]{1,0:T(8,128)(2,1)}, u32[]{:S(2)}, u32[]{:S(2)}) collective-permute-start(bf16[128,2176]{1,0:T(8,128)(2,1)} %get-tuple-element.328), channel_id=1, source_target_pairs={{0,16},{8,24},{16,0},{24,8},{1,17},{9,25},{17,1},{25,9},{2,18},{10... | collective-permute-start | bytes 1671176 | tf_op jit(solution)/shard_map/ppermute | solution.py:85
  597.1 83.5 %collective-permute-start.32 = (bf16[128,2176]{1,0:T(8,128)(2,1)S(1)}, bf16[128,2176]{1,0:T(8,128)(2,1)}, u32[]{:S(2)}, u32[]{:S(2)}) collective-permute-start(bf16[128,2176]{1,0:T(8,128)(2,1)S(1)} %get-tuple-element.326), channel_id=1, source_target_pairs={{0,8},{8,16},{16,24},{24,0},{1,9},{9,17},{17,25},{25,1},{2,10},{10... | collective-permute-start | bytes 1671176 | tf_op jit(solution)/shard_map/ppermute | solution.py:85
  613.0 91.5 %all-to-all-start.3 = ((bf16[16,64,1152]{2,1,0:T(8,128)(2,1)}), bf16[16,64,1152]{2,1,0:T(8,128)(2,1)}, u32[]{:S(2)}, u32[]{:S(2)}) async-start(bf16[16,64,1152]{2,1,0:T(8,128)(2,1)} %bitcast.577), calls=%async_computation.4 | async-start | bytes 4718592 | tf_op jit(solution)/shard_map/all_to_all | solution.py:132
  687.6 99.8 %collective-permute-start.36 = (bf16[4,256,2304]{2,1,0:T(8,128)(2,1)}, bf16[4,256,2304]{2,1,0:T(8,128)(2,1)}, u32[]{:S(2)}, u32[]{:S(2)}) collective-permute-start(bf16[4,256,2304]{2,1,0:T(8,128)(2,1)} %dynamic-slice_bitcast_fusion), channel_id=1, source_target_pairs={{0,4},{4,0},{1,5},{5,1},{2,6},{6,2},{3,7},{7,3},{8,12},{12,8},{9,1... | collective-permute-start | bytes 14155784 | tf_op jit(solution)/shard_map/ppermute | solution.py:85
  793.2 150.6 %all-to-all-start.4 = ((bf16[4,256,2304]{2,1,0:T(8,128)(2,1)}), bf16[4,256,2304]{2,1,0:T(8,128)(2,1)}, u32[]{:S(2)}, u32[]{:S(2)}) async-start(bf16[4,256,2304]{2,1,0:T(8,128)(2,1)} %fusion.1), calls=%async_computation.5 | async-start | bytes 9437184 | tf_op jit(solution)/shard_map/all_to_all | solution.py:109
  831.0 55.6 %collective-permute-start.49 = (bf16[2,2,64,2048]{3,2,1,0:T(8,128)(2,1)}, bf16[2,2,64,2048]{3,2,1,0:T(8,128)(2,1)}, u32[]{:S(2)}, u32[]{:S(2)}) collective-permute-start(bf16[2,2,64,2048]{3,2,1,0:T(8,128)(2,1)} %dynamic-slice_bitcast_fusion.2), channel_id=1, source_target_pairs={{0,1},{1,0},{2,3},{3,2},{4,5},{5,4},{6,7},{7,6},{8,9},{9,8},{10,11... | collective-permute-start | bytes 3145736 | tf_op jit(solution)/shard_map/ppermute | solution.py:85
  898.6 58.4 %collective-permute-start.43 = (bf16[128,2048]{1,0:T(8,128)(2,1)}, bf16[128,2048]{1,0:T(8,128)(2,1)}, u32[]{:S(2)}, u32[]{:S(2)}) collective-permute-start(bf16[128,2048]{1,0:T(8,128)(2,1)} %get-tuple-element.319), channel_id=1, source_target_pairs={{0,24},{8,0},{16,8},{24,16},{1,25},{9,1},{17,9},{25,17},{2,26},{10... | collective-permute-start | bytes 1572872 | tf_op jit(solution)/shard_map/ppermute | solution.py:85
  902.6 54.5 %collective-permute-start.44 = (bf16[128,2048]{1,0:T(8,128)(2,1)}, bf16[128,2048]{1,0:T(8,128)(2,1)}, u32[]{:S(2)}, u32[]{:S(2)}) collective-permute-start(bf16[128,2048]{1,0:T(8,128)(2,1)} %get-tuple-element.318), channel_id=1, source_target_pairs={{0,16},{8,24},{16,0},{24,8},{1,17},{9,25},{17,1},{25,9},{2,18},{10... | collective-permute-start | bytes 1572872 | tf_op jit(solution)/shard_map/ppermute | solution.py:85
  (124 other events, 2245.4 us)
Sparse Core Ops, SparseCore 0:
  86.0 137.6 all-gather.2
  525.9 169.4 reduce-scatter.1

commit v4 on v3

--- a/solution.py
+++ b/solution.py
@@ -765,11 +765,11 @@
         if across > 2:
             cut = part.shape[-1]
         first = net.scatter_axis(part[..., :cut], "y", dims - 2).astype(bf16)
-        first = net.scatter_axis(first, "x", dims - 3).astype(bf16)
+        first = net.scatter_axis(first, "x", dims - 3)
         if cut == part.shape[-1]:
             return first
         second = net.scatter_axis(part[..., cut:], "x", dims - 3).astype(bf16)
-        second = net.scatter_axis(second, "y", dims - 3).astype(bf16)
+        second = net.scatter_axis(second, "y", dims - 3)
         return jnp.concatenate([first, second], axis=-1)
 
     row_terms = jnp.concatenate(
@@ -790,7 +790,7 @@
     qkv_rows = to_rows(
         jnp.swapaxes(qkv_term.reshape(across, PLANES, yrows, PAIR, shard, -1), 0, 1),
         4,
-    )
+    ).astype(bf16)
     grad_normed_part = mm_t(after(grad_qkv, qkv_term), qkv_w)
     normed_part_low = grad_normed_part.astype(bf16).reshape(PLANES, rows, width)
     grad_normed_attn = jnp.zeros((rows, width), f32)
@@ -826,10 +826,26 @@
                 cols.append(shared_back[z, e, :, first : (k + 1) * window])
         shared_grads.append(jnp.concatenate(cols, axis=1).astype(f32))
 
-    grad_out_w = t_mm(mixed, branch_group).astype(bf16)
+    spare = jnp.arange(LANES)[None, :]
+    beside = sum(
+        t_mm(grads, jnp.broadcast_to(spare == j, (group_rows, LANES)).astype(bf16))
+        for j, grads in enumerate((grad_query_pre, grad_key_pre, grad_value_pre))
+    ).astype(bf16)
+    mass_parts = jnp.concatenate(
+        [jnp.zeros((3,), bf16)]
+        + two_parts(mass_x)
+        + [jnp.zeros((LANES - 3 - 2 * num_experts,), bf16)]
+    )
+    beside = jnp.where(spare < 3, beside, mass_parts[None])
+    grad_out_w = jnp.concatenate([t_mm(mixed, branch_group).astype(bf16), beside], axis=1)
     grad_output_weight = to_rows(
-        grad_out_w.reshape(across, yrows, PAIR, shard, width), 3
-    ).astype(f32)
+        grad_out_w.reshape(across, yrows, PAIR, shard, width + LANES), 3
+    )
+    bias_part = grad_output_weight[:, width : width + 3].T
+    mass_all = grad_output_weight[0, width + 3 : width + 3 + 2 * num_experts]
+    mass_all = (mass_all[:num_experts] + mass_all[num_experts:]) / (yrows * PAIR)
+    grad_output_weight = grad_output_weight[:, :width]
+    balance_loss = (num_experts * jnp.sum(fraction * mass_all / all_slots)).reshape(1)
     qkv_planes = net.exchange_z(after(qkv_rows, routed_sorted))
     grad_qkv_weights = [
         jnp.concatenate(
@@ -847,18 +863,6 @@
         for w, g in zip((query_weight, key_weight, value_weight), grad_qkv_weights)
     ) / attention_gain.astype(f32)
 
-    bias_part = jnp.sum(grad_qkv.astype(f32), axis=0).reshape(3, across, yrows, PAIR, shard)
-    bias_part = after(bias_part, grad_normed_attn)
-    bias_part = jnp.transpose(bias_part, (1, 2, 3, 0, 4))
-    bias_part = net.scatter_axis(bias_part, "c", 2)
-    bias_part = net.scatter_axis(bias_part, "y", 1)
-    mass_row = jnp.broadcast_to(
-        jnp.pad(mass_x, (0, shard - num_experts))[None, None], (across, 1, shard)
-    )
-    bias_part = jnp.concatenate([bias_part, mass_row], axis=1)
-    bias_part = net.scatter_axis(bias_part, "x", 0)
-    mass_all = bias_part[3, :num_experts]
-    balance_loss = (num_experts * jnp.sum(fraction * mass_all / all_slots)).reshape(1)
     return (
         layer_out.reshape(1, rows, width),
         balance_loss,

time: 1000 us -> 998 us (level)
    unnamed x197 -> x177, local copies, waits for them, and re-layouts: 41.3 us -> 44.9 us
    ppermute x54 -> x51, waiting for transfers between devices: 334 us -> 331 us  [turn(): lax.ppermute(value, axis, [(i, (i + steps) % size) for i in range(size)])]
    ppermute x54 -> x51, starting transfers between devices: 80.9 us -> 81.1 us  [turn(): lax.ppermute(value, axis, [(i, (i + steps) % size) for i in range(size)])]
  transfers between devices with their start and end apart: 62 -> 59, of which waited for: 32 -> 32; matrix products, arithmetic and copies ran while one was open for 25% -> 25% of each run, Pallas kernels for 12% -> 12%
where the time goes in v4:
time: 998 us; the launch traced here: 987 us
  waiting for transfers between devices  409 us (41%)
  Pallas kernels  165 us (17%)
  local copies, waits for them, and re-layouts  141 us (14%)
  starting transfers between devices  119 us (12%)
  other arithmetic  91.3 us (9%)
  matrix products  40.2 us (4%)
  between operations  21.3 us (2%)
    ppermute x51, waiting for transfers between devices, turn(): lax.ppermute(value, axis, [(i, (i + steps) % size) for i in range(size)])  331 us
    pallas_call x2, Pallas kernels, run_experts(): pl.pallas_call(lambda *refs: expert_kernel(second, across, *refs), grid_s...  95.9 us
    ppermute x51, starting transfers between devices, turn(): lax.ppermute(value, axis, [(i, (i + steps) % size) for i in range(size)])  81.1 us
    all_to_all x4, waiting for transfers between devices, exchange_z(): return lax.all_to_all(value, 'z', split_axis=0, concat_axis=0, tiled=True)  66.5 us
    pallas_call x3, Pallas kernels, run_terms(): pl.pallas_call(lambda *refs: term_kernel(numbers, *refs), grid=(planes *...  56.5 us
    unnamed x177, local copies, waits for them, and re-layouts  44.9 us
    all_to_all x4, starting transfers between devices, exchange_z(): return lax.all_to_all(value, 'z', split_axis=0, concat_axis=0, tiled=True)  21.9 us
  transfers between devices with their start and end apart: 59, of which 32 were waited for; matrix products, arithmetic and copies ran while one was open for 25% of the time, Pallas kernels for 12%

profile of v4, /device:TPU:0, one launch (start us, length us, event | category | flops | bytes accessed | tf_op | source)
XLA Modules:
  0.0 986.7 jit_solution(13944176918389634610)
XLA Ops:
  49.7 26.8 %all-to-all-done = bf16[4,64,1664]{2,1,0:T(8,128)(2,1)} async-done(((bf16[4,64,1664]{2,1,0:T(8,128)(2,1)}), bf16[4,64,1664]{2,1,0:T(8,128)(2,1)}, u32[]{:S(2)}, u32[]{:S(2)}) %all-to-all-start) | async-done | bytes 852000 | tf_op jit(solution)/shard_map/all_to_all | solution.py:109
  89.0 23.2 %collective-permute-done.4 = bf16[4,64,1664]{2,1,0:T(8,128)(2,1)S(1)} collective-permute-done((bf16[4,64,1664]{2,1,0:T(8,128)(2,1)}, bf16[4,64,1664]{2,1,0:T(8,128)(2,1)S(1)}, u32[]{:S(2)}, u32[]{:S(2)}) %collective-permute-start.4) | collective-permute-done | bytes 852000 | tf_op jit(solution)/shard_map/ppermute | solution.py:85
  121.1 10.6 %collective-permute-done.6 = bf16[2,64,1664]{2,1,0:T(8,128)(2,1)S(1)} collective-permute-done((bf16[2,64,1664]{2,1,0:T(8,128)(2,1)S(1)}, bf16[2,64,1664]{2,1,0:T(8,128)(2,1)S(1)}, u32[]{:S(2)}, u32[]{:S(2)}) %collective-permute-start.6) | collective-permute-done | bytes 426016 | tf_op jit(solution)/shard_map/ppermute | solution.py:85
  169.4 20.5 %collective-permute-done.11 = bf16[528,1024]{1,0:T(8,128)(2,1)} collective-permute-done((bf16[528,1024]{1,0:T(8,128)(2,1)}, bf16[528,1024]{1,0:T(8,128)(2,1)}, u32[]{:S(2)}, u32[]{:S(2)}) %collective-permute-start.11) | collective-permute-done | bytes 1081376 | tf_op jit(solution)/shard_map/ppermute | solution.py:85
  200.2 38.0 %all-to-all-done.1.refs_6_.refs_10_ = bf16[4,256,2304]{2,1,0:T(8,128)(2,1)} async-done(((bf16[4,256,2304]{2,1,0:T(8,128)(2,1)}), bf16[4,256,2304]{2,1,0:T(8,128)(2,1)}, u32[]{:S(2)}, u32[]{:S(2)}) %all-to-all-start.1) | async-done | bytes 4718624 | tf_op jit(solution)/shard_map/all_to_all | solution.py:109
  249.8 10.4 %collective-permute-done.12 = bf16[128,2048]{1,0:T(8,128)(2,1)S(1)} collective-permute-done((bf16[128,2048]{1,0:T(8,128)(2,1)S(1)}, bf16[128,2048]{1,0:T(8,128)(2,1)S(1)}, u32[]{:S(2)}, u32[]{:S(2)}) %collective-permute-start.12) | collective-permute-done | bytes 524320 | tf_op jit(solution)/shard_map/ppermute | solution.py:85
  260.2 29.4 %collective-permute-done.13 = bf16[128,2048]{1,0:T(8,128)(2,1)S(1)} collective-permute-done((bf16[128,2048]{1,0:T(8,128)(2,1)S(1)}, bf16[128,2048]{1,0:T(8,128)(2,1)S(1)}, u32[]{:S(2)}, u32[]{:S(2)}) %collective-permute-start.13) | collective-permute-done | bytes 524320 | tf_op jit(solution)/shard_map/ppermute | solution.py:85
  311.0 30.4 %collective-permute-done.17.refs_7_.refs_11_ = bf16[4,256,2304]{2,1,0:T(8,128)(2,1)} collective-permute-done((bf16[4,256,2304]{2,1,0:T(8,128)(2,1)}, bf16[4,256,2304]{2,1,0:T(8,128)(2,1)}, u32[]{:S(2)}, u32[]{:S(2)}) %collective-permute-start.17) | collective-permute-done | bytes 4718624 | tf_op jit(solution)/shard_map/ppermute | solution.py:85
  358.4 30.5 %collective-permute-done.20 = bf16[128,2176]{1,0:T(8,128)(2,1)S(1)} collective-permute-done((bf16[128,2176]{1,0:T(8,128)(2,1)S(1)}, bf16[128,2176]{1,0:T(8,128)(2,1)S(1)}, u32[]{:S(2)}, u32[]{:S(2)}) %collective-permute-start.20) | collective-permute-done | bytes 557088 | tf_op jit(solution)/shard_map/ppermute | solution.py:85
  389.0 14.4 %collective-permute-done.22 = bf16[128,2176]{1,0:T(8,128)(2,1)S(1)} collective-permute-done((bf16[128,2176]{1,0:T(8,128)(2,1)S(1)}, bf16[128,2176]{1,0:T(8,128)(2,1)S(1)}, u32[]{:S(2)}, u32[]{:S(2)}) %collective-permute-start.22) | collective-permute-done | bytes 557088 | tf_op jit(solution)/shard_map/ppermute | solution.py:85
  414.9 51.4 %shard_map.357 = (bf16[2048,2176]{1,0:T(8,128)(2,1)}, bf16[2048,768]{1,0:T(8,128)(2,1)}, bf16[2048,768]{1,0:T(8,128)(2,1)}, bf16[2048,768]{1,0:T(8,128)(2,1)}, bf16[2048,2048]{1,0:T(8,128)(2,1)}) custom-call(s32[3]{0:T(128)} %pad_add_fusion.2.refs_0_, s32[8]{0:T(128)} %add.623.refs_1_, bf16[2048,2176]{1,0:T(8,128)(2,1)} %constant_dynamic-update-slice_fusion.refs_2_.refs_0_, ...), custom_call_target="tpu_custom_call" | custom-call | flops 32212254720 | bytes 62390272 | tf_op jit(solution)/shard_map/pallas_call | solution.py:238
  467.9 44.4 %shard_map.359 = (bf16[2048,2176]{1,0:T(8,128)(2,1)}, bf16[2048,384]{1,0:T(8,128)(2,1)}, bf16[2048,384]{1,0:T(8,128)(2,1)}, bf16[2048,384]{1,0:T(8,128)(2,1)}, bf16[8,256,2048]{2,1,0:T(8,128)(2,1)}) custom-call(s32[3]{0:T(128)} %pad_add_fusion.2.refs_0_, s32[8]{0:T(128)} %add.623.refs_1_, ...), custom_call_target="tpu_custom_call" | custom-call | flops 16106127360 | bytes 52953088 | tf_op jit(solution)/shard_map/pallas_call | solution.py:238
  536.5 19.9 %shard_map.360 = bf16[2,4,256,1152]{3,2,1,0:T(8,128)(2,1)} custom-call(bf16[2048,2176]{1,0:T(8,128)(2,1)} %constant_dynamic-update-slice_fusion.refs_2_.refs_0_, bf16[2048,384]{1,0:T(8,128)(2,1)} %get-tuple-element.78.refs_1_, bf16[2048,384]{1,0:T(8,128)(2,1)} %get-tuple-element.79.refs_2_, bf16[2048,2048]{1,0:T(8,128)(2,1)} %get-tuple-element.80.refs_3_, ...), custom_call_target="tpu_custom_call" | custom-call | flops 9663676416 | bytes 26738688 | tf_op jit(solution)/shard_map/pallas_call | solution.py:310
  563.7 9.4 collective-permute-start.30
  573.1 23.8 %collective-permute-done.27 = bf16[2,128,2176]{2,1,0:T(8,128)(2,1)S(1)} collective-permute-done((bf16[2,128,2176]{2,1,0:T(8,128)(2,1)S(1)}, bf16[2,128,2176]{2,1,0:T(8,128)(2,1)S(1)}, u32[]{:S(2)}, u32[]{:S(2)}) %collective-permute-start.27) | collective-permute-done | bytes 1114144 | tf_op jit(solution)/shard_map/ppermute | solution.py:85
  602.4 9.1 collective-permute-done.28
  621.7 27.0 %shard_map.361 = bf16[2,4,256,2304]{3,2,1,0:T(8,128)(2,1)} custom-call(bf16[2048,2176]{1,0:T(8,128)(2,1)} %constant_dynamic-update-slice_fusion.refs_2_.refs_0_, bf16[2048,768]{1,0:T(8,128)(2,1)} %get-tuple-element.83.refs_1_, bf16[2048,768]{1,0:T(8,128)(2,1)} %get-tuple-element.84.refs_2_, bf16[2048,2048]{1,0:T(8,128)(2,1)} %get-tuple-element.80.refs_3_, ...), custom_call_target="tpu_custom_call" | custom-call | flops 19327352832 | bytes 36175872 | tf_op jit(solution)/shard_map/pallas_call | solution.py:310
  648.7 31.6 %collective-permute-done.31 = bf16[128,2176]{1,0:T(8,128)(2,1)S(1)} collective-permute-done((bf16[128,2176]{1,0:T(8,128)(2,1)}, bf16[128,2176]{1,0:T(8,128)(2,1)S(1)}, u32[]{:S(2)}, u32[]{:S(2)}) %collective-permute-start.31) | collective-permute-done | bytes 557088 | tf_op jit(solution)/shard_map/ppermute | solution.py:85
  693.7 10.8 %all-to-all-done.3 = bf16[16,64,1152]{2,1,0:T(8,128)(2,1)} async-done(((bf16[16,64,1152]{2,1,0:T(8,128)(2,1)}), bf16[16,64,1152]{2,1,0:T(8,128)(2,1)}, u32[]{:S(2)}, u32[]{:S(2)}) %all-to-all-start.3) | async-done | bytes 2359328 | tf_op jit(solution)/shard_map/all_to_all | solution.py:132
  751.9 16.9 %collective-permute-done.34 = bf16[128,2048]{1,0:T(8,128)(2,1)S(1)} collective-permute-done((bf16[128,2048]{1,0:T(8,128)(2,1)S(1)}, bf16[128,2048]{1,0:T(8,128)(2,1)S(1)}, u32[]{:S(2)}, u32[]{:S(2)}) %collective-permute-start.34) | collective-permute-done | bytes 524320 | tf_op jit(solution)/shard_map/ppermute | solution.py:85
  777.0 11.1 %collective-permute-done.36 = bf16[4,256,2304]{2,1,0:T(8,128)(2,1)} collective-permute-done((bf16[4,256,2304]{2,1,0:T(8,128)(2,1)}, bf16[4,256,2304]{2,1,0:T(8,128)(2,1)}, u32[]{:S(2)}, u32[]{:S(2)}) %collective-permute-start.36) | collective-permute-done | bytes 4718624 | tf_op jit(solution)/shard_map/ppermute | solution.py:85
  835.7 14.9 %collective-permute-done.37 = bf16[512,1024]{1,0:T(8,128)(2,1)} collective-permute-done((bf16[512,1024]{1,0:T(8,128)(2,1)}, bf16[512,1024]{1,0:T(8,128)(2,1)}, u32[]{:S(2)}, u32[]{:S(2)}) %collective-permute-start.37) | collective-permute-done | bytes 1048608 | tf_op jit(solution)/shard_map/ppermute | solution.py:85
  864.7 9.6 shard_map.362
  916.2 10.9 %collective-permute-done.42 = bf16[4,2,64,768]{3,2,0,1:T(8,128)(2,1)} collective-permute-done((bf16[4,2,64,768]{3,2,0,1:T(8,128)(2,1)}, bf16[4,2,64,768]{3,2,0,1:T(8,128)(2,1)}, u32[]{:S(2)}, u32[]{:S(2)}) %collective-permute-start.42) | collective-permute-done | bytes 786464 | tf_op jit(solution)/shard_map/ppermute | solution.py:85
  (559 shorter events, 440.3 us)
Async XLA Ops:
  22.2 54.4 %all-to-all-start = ((bf16[4,64,1664]{2,1,0:T(8,128)(2,1)}), bf16[4,64,1664]{2,1,0:T(8,128)(2,1)}, u32[]{:S(2)}, u32[]{:S(2)}) async-start(bf16[4,64,1664]{2,1,0:T(8,128)(2,1)} %copy.377), calls=%async_computation | async-start | bytes 1703936 | tf_op jit(solution)/shard_map/all_to_all | solution.py:109
  78.1 160.1 %all-to-all-start.1 = ((bf16[4,256,2304]{2,1,0:T(8,128)(2,1)}), bf16[4,256,2304]{2,1,0:T(8,128)(2,1)}, u32[]{:S(2)}, u32[]{:S(2)}) async-start(bf16[4,256,2304]{2,1,0:T(8,128)(2,1)} %shard_map.356), calls=%async_computation.1 | async-start | bytes 9437184 | tf_op jit(solution)/shard_map/all_to_all | solution.py:109
  83.0 331.9 %all-gather.3.cloned.1.call-start = ((), (), s32[]{:S(2)}) async-start(), calls=%async_computation.8 | async-start | bytes 8912896 | tf_op jit(solution)/shard_map/all_gather | solution.py:455
  88.4 43.9 %collective-permute-start.9 = (bf16[2,64,2176]{2,1,0:T(8,128)(2,1)S(1)}, bf16[2,64,2176]{2,1,0:T(8,128)(2,1)S(1)}, u32[]{:S(2)}, u32[]{:S(2)}) collective-permute-start(bf16[2,64,2176]{2,1,0:T(8,128)(2,1)S(1)} %bitcast_dynamic-update-slice_fusion.9), channel_id=1, source_target_pairs={{0,2},{2,0},{1,3},{3,1},{4,6},{6,4},{5,7},{7,5},{8,10},{10,8},{9,1... | collective-permute-start | bytes 1671176 | tf_op jit(solution)/shard_map/ppermute | solution.py:85
  238.2 103.1 %collective-permute-start.17 = (bf16[4,256,2304]{2,1,0:T(8,128)(2,1)}, bf16[4,256,2304]{2,1,0:T(8,128)(2,1)}, u32[]{:S(2)}, u32[]{:S(2)}) collective-permute-start(bf16[4,256,2304]{2,1,0:T(8,128)(2,1)} %all-to-all-done.1.refs_6_.refs_10_), channel_id=1, source_target_pairs={{0,4},{4,0},{1,5},{5,1},{2,6},{6,2},{3,7},{7,3},{8,12},{12,8},{9,1... | collective-permute-start | bytes 14155784 | tf_op jit(solution)/shard_map/ppermute | solution.py:85
  246.9 42.7 %collective-permute-start.13 = (bf16[128,2048]{1,0:T(8,128)(2,1)S(1)}, bf16[128,2048]{1,0:T(8,128)(2,1)S(1)}, u32[]{:S(2)}, u32[]{:S(2)}) collective-permute-start(bf16[128,2048]{1,0:T(8,128)(2,1)S(1)} %get-tuple-element.321), channel_id=1, source_target_pairs={{0,16},{8,24},{16,0},{24,8},{1,17},{9,25},{17,1},{25,9},{2,18},{10... | collective-permute-start | bytes 1572872 | tf_op jit(solution)/shard_map/ppermute | solution.py:85
  295.1 46.2 %collective-permute-start.19 = (bf16[128,2176]{1,0:T(8,128)(2,1)S(1)}, bf16[128,2176]{1,0:T(8,128)(2,1)S(1)}, u32[]{:S(2)}, u32[]{:S(2)}) collective-permute-start(bf16[128,2176]{1,0:T(8,128)(2,1)S(1)} %concatenate.177), channel_id=1, source_target_pairs={{0,16},{8,24},{16,0},{24,8},{1,17},{9,25},{17,1},{25,9},{2,18},{10... | collective-permute-start | bytes 1671176 | tf_op jit(solution)/shard_map/ppermute | solution.py:85
  297.1 44.3 %collective-permute-start.21 = (bf16[128,2176]{1,0:T(8,128)(2,1)S(1)}, bf16[128,2176]{1,0:T(8,128)(2,1)S(1)}, u32[]{:S(2)}, u32[]{:S(2)}) collective-permute-start(bf16[128,2176]{1,0:T(8,128)(2,1)S(1)} %concatenate.177), channel_id=1, source_target_pairs={{0,24},{8,0},{16,8},{24,16},{1,25},{9,1},{17,9},{25,17},{2,26},{10... | collective-permute-start | bytes 1671176 | tf_op jit(solution)/shard_map/ppermute | solution.py:85
  307.9 45.8 %collective-permute-start.15 = (bf16[128,2176]{1,0:T(8,128)(2,1)S(1)}, bf16[128,2176]{1,0:T(8,128)(2,1)}, u32[]{:S(2)}, u32[]{:S(2)}) collective-permute-start(bf16[128,2176]{1,0:T(8,128)(2,1)S(1)} %concatenate.177), channel_id=1, source_target_pairs={{0,2},{2,0},{1,3},{3,1},{4,6},{6,4},{5,7},{7,5},{8,10},{10,8},{9,1... | collective-permute-start | bytes 1671176 | tf_op jit(solution)/shard_map/ppermute | solution.py:85
  342.9 71.1 %all-to-all-start.2 = ((bf16[16,64,1152]{2,1,0:T(8,128)(2,1)}), bf16[16,64,1152]{2,1,0:T(8,128)(2,1)}, u32[]{:S(2)}, u32[]{:S(2)}) async-start(bf16[16,64,1152]{2,1,0:T(8,128)(2,1)} %shard_map.358), calls=%async_computation.2 | async-start | bytes 4718592 | tf_op jit(solution)/shard_map/all_to_all | solution.py:132
  350.6 373.2 %reduce-scatter.2.cloned.1.call-start = ((), (), s32[]{:S(2)}) async-start(), calls=%async_computation.7 | async-start | bytes 8912896 | tf_op jit(solution)/shard_map/reduce_scatter | solution.py:677
  353.6 49.8 %collective-permute-start.22 = (bf16[128,2176]{1,0:T(8,128)(2,1)S(1)}, bf16[128,2176]{1,0:T(8,128)(2,1)S(1)}, u32[]{:S(2)}, u32[]{:S(2)}) collective-permute-start(bf16[128,2176]{1,0:T(8,128)(2,1)S(1)} %collective-permute-done.21), channel_id=1, source_target_pairs={{0,2},{2,0},{1,3},{3,1},{4,6},{6,4},{5,7},{7,5},{8,10},{10,8},{9,1... | collective-permute-start | bytes 1671176 | tf_op jit(solution)/shard_map/ppermute | solution.py:85
  358.4 52.5 %collective-permute-start.23 = (bf16[512,2176]{1,0:T(8,128)(2,1)S(1)}, bf16[512,2176]{1,0:T(8,128)(2,1)S(1)}, u32[]{:S(2)}, u32[]{:S(2)}) collective-permute-start(bf16[512,2176]{1,0:T(8,128)(2,1)S(1)} %pad_maximum_fusion.1), channel_id=1, source_target_pairs={{0,1},{1,0},{2,3},{3,2},{4,5},{5,4},{6,7},{7,6},{8,9},{9,8},{10,11... | collective-permute-start | bytes 6684680 | tf_op jit(solution)/shard_map/ppermute | solution.py:85
  414.0 54.0 %collective-permute-start.25 = (bf16[4,256,1152]{2,1,0:T(8,128)(2,1)}, bf16[4,256,1152]{2,1,0:T(8,128)(2,1)}, u32[]{:S(2)}, u32[]{:S(2)}) collective-permute-start(bf16[4,256,1152]{2,1,0:T(8,128)(2,1)} %bitcast.49.refs_8_), channel_id=1, source_target_pairs={{0,4},{4,0},{1,5},{5,1},{2,6},{6,2},{3,7},{7,3},{8,12},{12,8},{9,1... | collective-permute-start | bytes 7077896 | tf_op jit(solution)/shard_map/ppermute | solution.py:85
  558.5 53.0 %collective-permute-start.28 = (bf16[4,256,1152]{2,1,0:T(8,128)(2,1)S(1)}, bf16[4,256,1152]{2,1,0:T(8,128)(2,1)S(1)}, u32[]{:S(2)}, u32[]{:S(2)}) collective-permute-start(bf16[4,256,1152]{2,1,0:T(8,128)(2,1)S(1)} %dynamic-slice_bitcast_fusion.1), channel_id=1, source_target_pairs={{0,4},{4,0},{1,5},{5,1},{2,6},{6,2},{3,7},{7,3},{8,12},{12,8},{9,1... | collective-permute-start | bytes 7077896 | tf_op jit(solution)/shard_map/ppermute | solution.py:85
  563.7 85.0 %collective-permute-start.30 = (bf16[128,2176]{1,0:T(8,128)(2,1)}, bf16[128,2176]{1,0:T(8,128)(2,1)S(1)}, u32[]{:S(2)}, u32[]{:S(2)}) collective-permute-start(bf16[128,2176]{1,0:T(8,128)(2,1)} %get-tuple-element.326), channel_id=1, source_target_pairs={{0,24},{8,0},{16,8},{24,16},{1,25},{9,1},{17,9},{25,17},{2,26},{10... | collective-permute-start | bytes 1671176 | tf_op jit(solution)/shard_map/ppermute | solution.py:85
  573.1 107.2 %collective-permute-start.31 = (bf16[128,2176]{1,0:T(8,128)(2,1)}, bf16[128,2176]{1,0:T(8,128)(2,1)S(1)}, u32[]{:S(2)}, u32[]{:S(2)}) collective-permute-start(bf16[128,2176]{1,0:T(8,128)(2,1)} %get-tuple-element.327), channel_id=1, source_target_pairs={{0,16},{8,24},{16,0},{24,8},{1,17},{9,25},{17,1},{25,9},{2,18},{10... | collective-permute-start | bytes 1671176 | tf_op jit(solution)/shard_map/ppermute | solution.py:85
  598.1 83.0 %collective-permute-start.32 = (bf16[128,2176]{1,0:T(8,128)(2,1)}, bf16[128,2176]{1,0:T(8,128)(2,1)}, u32[]{:S(2)}, u32[]{:S(2)}) collective-permute-start(bf16[128,2176]{1,0:T(8,128)(2,1)} %get-tuple-element.325), channel_id=1, source_target_pairs={{0,8},{8,16},{16,24},{24,0},{1,9},{9,17},{17,25},{25,1},{2,10},{10... | collective-permute-start | bytes 1671176 | tf_op jit(solution)/shard_map/ppermute | solution.py:85
  613.4 91.0 %all-to-all-start.3 = ((bf16[16,64,1152]{2,1,0:T(8,128)(2,1)}), bf16[16,64,1152]{2,1,0:T(8,128)(2,1)}, u32[]{:S(2)}, u32[]{:S(2)}) async-start(bf16[16,64,1152]{2,1,0:T(8,128)(2,1)} %bitcast.564), calls=%async_computation.4 | async-start | bytes 4718592 | tf_op jit(solution)/shard_map/all_to_all | solution.py:132
  688.1 100.0 %collective-permute-start.36 = (bf16[4,256,2304]{2,1,0:T(8,128)(2,1)}, bf16[4,256,2304]{2,1,0:T(8,128)(2,1)}, u32[]{:S(2)}, u32[]{:S(2)}) collective-permute-start(bf16[4,256,2304]{2,1,0:T(8,128)(2,1)} %dynamic-slice_bitcast_fusion), channel_id=1, source_target_pairs={{0,4},{4,0},{1,5},{5,1},{2,6},{6,2},{3,7},{7,3},{8,12},{12,8},{9,1... | collective-permute-start | bytes 14155784 | tf_op jit(solution)/shard_map/ppermute | solution.py:85
  793.8 149.9 %all-to-all-start.4 = ((bf16[4,256,2304]{2,1,0:T(8,128)(2,1)}), bf16[4,256,2304]{2,1,0:T(8,128)(2,1)}, u32[]{:S(2)}, u32[]{:S(2)}) async-start(bf16[4,256,2304]{2,1,0:T(8,128)(2,1)} %fusion.1), calls=%async_computation.5 | async-start | bytes 9437184 | tf_op jit(solution)/shard_map/all_to_all | solution.py:109
  887.5 70.7 %collective-permute-start.46 = (bf16[128,2048]{1,0:T(8,128)(2,1)}, bf16[128,2048]{1,0:T(8,128)(2,1)}, u32[]{:S(2)}, u32[]{:S(2)}) collective-permute-start(bf16[128,2048]{1,0:T(8,128)(2,1)} %get-tuple-element.318), channel_id=1, source_target_pairs={{0,24},{8,0},{16,8},{24,16},{1,25},{9,1},{17,9},{25,17},{2,26},{10... | collective-permute-start | bytes 1572872 | tf_op jit(solution)/shard_map/ppermute | solution.py:85
  891.4 66.8 %collective-permute-start.47 = (bf16[128,2048]{1,0:T(8,128)(2,1)}, bf16[128,2048]{1,0:T(8,128)(2,1)}, u32[]{:S(2)}, u32[]{:S(2)}) collective-permute-start(bf16[128,2048]{1,0:T(8,128)(2,1)} %get-tuple-element.317), channel_id=1, source_target_pairs={{0,16},{8,24},{16,0},{24,8},{1,17},{9,25},{17,1},{25,9},{2,18},{10... | collective-permute-start | bytes 1572872 | tf_op jit(solution)/shard_map/ppermute | solution.py:85
  891.6 66.6 %collective-permute-start.48 = (bf16[128,2048]{1,0:T(8,128)(2,1)}, bf16[128,2048]{1,0:T(8,128)(2,1)}, u32[]{:S(2)}, u32[]{:S(2)}) collective-permute-start(bf16[128,2048]{1,0:T(8,128)(2,1)} %get-tuple-element.316), channel_id=1, source_target_pairs={{0,8},{8,16},{16,24},{24,0},{1,9},{9,17},{17,25},{25,1},{2,10},{10... | collective-permute-start | bytes 1572872 | tf_op jit(solution)/shard_map/ppermute | solution.py:85
  (111 other events, 2118.7 us)
Sparse Core Ops, SparseCore 0:
  86.1 137.6 all-gather.2
  525.7 169.0 reduce-scatter.1
